TPU v7x, 256 devices: a whole 4x4x8 slice. The times are simulated.
256 devices in a mesh: ctx: 64 (over z, y, core), pipe: 4 (over x).
Axes of the slice: x: 4, y: 4, z: 8, core: 2. Of those that a mesh axis runs over, the one named last changes fastest.
Arguments:
- queries: bfloat16 [4, 32768, 2048], P('pipe', 'ctx'), may hold values from -400 to 400
- keys: bfloat16 [4, 32768, 2048], P('pipe', 'ctx'), may hold values from -12 to 12
- values: bfloat16 [4, 32768, 2048], P('pipe', 'ctx'), may hold values from -15 to 15
- picks: int32 [4, 64, 16, 2], P('pipe'), may hold values from -1 to 62, as said below
Outputs:
- passed: bfloat16 [4, 32768, 2048], P('pipe', 'ctx')
Inputs may be any that keep to these rules, and one draw needn't show every extreme that they name: Each entry is -1 (no block) or a block earlier than its query block; a head's 2 entries differ unless -1; within one section and query block no block is named more than 1 times over all heads and picks, and this bound is reached; query block 0 names nothing and every later query block names its preceding block at least once.
All inputs are finite; a program needn't handle non-finite values.
Results may differ from a plain program's by a relative error of at most 0.0048.
Values may be sent and summed in bfloat16 or wider, within the bound.
A program may use at most 128 MiB of HBM per device.

v0:
```python
import jax
import jax.numpy as jnp
from jax import lax
from jax.sharding import PartitionSpec as P

HEADS = 16
HD = 128
PICKS = 2


def passed_along(value, axis, steps):
    count = lax.axis_size(axis)
    pairs = [(source, (source + steps) % count) for source in range(count)]
    return lax.ppermute(value, axis, pairs)


def request_table(chosen, owners, slot_count):
    pick_count = chosen.shape[1]
    pick_ids = lax.iota(jnp.int32, pick_count)
    is_live = chosen >= 0
    earlier = pick_ids[None, :] < pick_ids[:, None]
    same_owner = (chosen[:, :, None] == chosen[:, None, :]) & earlier[None]
    pick_order = jnp.sum(same_owner.astype(jnp.int32), axis=2)
    head_ids = pick_ids // PICKS
    slot_ranks = lax.iota(jnp.int32, slot_count)
    matches = (
        is_live[:, None, None, :]
        & (chosen[:, None, None, :] == owners[None, :, None, None])
        & (pick_order[:, None, None, :] == slot_ranks[None, None, :, None])
    )
    was_found = jnp.any(matches, axis=3)
    head_table = jnp.sum(jnp.where(matches, head_ids[None, None, None, :], 0), axis=3)
    return (jnp.where(was_found, head_table, -1), pick_order)


def per_device(queries, keys, values, picks):
    ctx_width = lax.axis_size("ctx")
    rank_here = lax.axis_index("ctx")
    slot_count = max(1, PICKS * HEADS // ctx_width)
    block_rows = queries.shape[1]
    score_scale = HD ** (-0.5)
    every_pick = picks[0].reshape(ctx_width, HEADS * PICKS)
    chosen = lax.dynamic_slice_in_dim(every_pick, rank_here, 1, 0)
    pick_order = request_table(chosen, lax.iota(jnp.int32, ctx_width), slot_count)[1]
    asked_table = request_table(every_pick, rank_here.reshape(1), slot_count)[0]
    asked_heads = asked_table[:, 0, :]
    safe_asked = jnp.maximum(asked_heads, 0)
    query_heads = queries[0].reshape(block_rows, HEADS, HD).transpose(1, 0, 2)
    key_heads = keys[0].reshape(block_rows, HEADS, HD).transpose(1, 0, 2)
    value_heads = values[0].reshape(block_rows, HEADS, HD).transpose(1, 0, 2)
    is_live = chosen[0] >= 0
    flat_slot = jnp.where(is_live, chosen[0] * slot_count + pick_order[0], 0)
    remote_mask = jnp.repeat(is_live.reshape(HEADS, PICKS), block_rows, axis=1)
    row_index = lax.iota(jnp.int32, block_rows)
    causal = row_index[:, None] >= row_index[None, :]

    def arrived(received, last_width):
        flat_slots = received.reshape(ctx_width * slot_count, block_rows, last_width)
        return flat_slots[flat_slot].reshape(HEADS, PICKS * block_rows, last_width)

    def masked_scores(query_head, key_rows, mask_row):
        raw_scores = lax.dot_general(
            query_head, key_rows, (((1,), (1,)), ((), ())), preferred_element_type=jnp.float32
        )
        allowed = jnp.concatenate(
            [causal, jnp.broadcast_to(mask_row[None, :], (block_rows, PICKS * block_rows))], axis=1
        )
        return jnp.where(allowed, raw_scores * score_scale, -jnp.inf)

    def row_stats(scores):
        row_top = jnp.max(scores, axis=1)
        row_total = jnp.sum(jnp.exp(scores - row_top[:, None]), axis=1)
        return (row_top, row_total)

    def weighted(scores, row_top, row_total, value_rows):
        prob_rows = (jnp.exp(scores - row_top[:, None]) / row_total[:, None]).astype(jnp.bfloat16)
        return jnp.dot(prob_rows, value_rows, preferred_element_type=jnp.float32).astype(
            jnp.bfloat16
        )

    got_keys = lax.all_to_all(key_heads[safe_asked], "ctx", split_axis=0, concat_axis=0, tiled=True)
    all_keys = jnp.concatenate([key_heads, arrived(got_keys, HD)], axis=1)

    def first_pass(head_items):
        query_head, key_rows, mask_row = head_items
        return row_stats(masked_scores(query_head, key_rows, mask_row))

    tops, totals = lax.map(first_pass, (query_heads, all_keys, remote_mask))
    got_values = lax.all_to_all(
        value_heads[safe_asked], "ctx", split_axis=0, concat_axis=0, tiled=True
    )
    all_values = jnp.concatenate([value_heads, arrived(got_values, HD)], axis=1)

    def second_pass(head_items):
        query_head, key_rows, value_rows, mask_row, row_top, row_total = head_items
        scores = masked_scores(query_head, key_rows, mask_row)
        return weighted(scores, row_top, row_total, value_rows)

    outputs = lax.map(second_pass, (query_heads, all_keys, all_values, remote_mask, tops, totals))
    merged = outputs.transpose(1, 0, 2).reshape(1, block_rows, HEADS * HD)
    merged = passed_along(merged, "pipe", 1)
    return merged


def solution(mesh):
    placed = (
        P("pipe", "ctx", None),
        P("pipe", "ctx", None),
        P("pipe", "ctx", None),
        P("pipe", None, None, None),
    )
    return jax.shard_map(
        per_device, mesh=mesh, in_specs=placed, out_specs=P("pipe", "ctx", None), check_vma=False
    )
```

profile of v0, /device:TPU:48, one launch (start us, length us, event | category | flops | bytes accessed | tf_op | source)
XLA Modules:
  0.0 575.9 jit_solution(270828523428590662)
XLA Ops:
  0.0 0.7 compare_and_fusion
  0.8 1.0 convert_reduce_fusion
  1.9 0.8 and_reduce_fusion
  2.7 2.9 copy.89
  5.6 5.5 gather_fusion
  11.1 11.6 %all-to-all-start = ((bf16[64,1,512,128]{2,3,1,0:T(8,128)(2,1)}), bf16[64,1,512,128]{2,3,1,0:T(8,128)(2,1)}, u32[]{:S(2)}, u32[]{:S(2)}) async-start(bf16[64,1,512,128]{2,3,1,0:T(8,128)(2,1)} %bitcast.98), calls=%async_computation | async-start | bytes 16777216 | tf_op jit(solution)/shard_map/all_to_all | solution.py:81
  22.7 3.9 copy.94
  26.6 7.1 %gather_fusion.2 = bf16[64,512,128]{1,2,0:T(8,128)(2,1)} fusion(bf16[16,512,128]{1,2,0:T(8,128)(2,1)} %bitcast.95, s32[1024]{0:T(1024)S(1)} %pad_clamp_fusion.1), kind=kCustom, calls=%fused_computation.2 | custom fusion | bytes 16777472 | tf_op jit(solution)/shard_map/gather | solution.py:90
  33.7 175.2 %all-to-all-done = bf16[64,1,512,128]{2,3,1,0:T(8,128)(2,1)} async-done(((bf16[64,1,512,128]{2,3,1,0:T(8,128)(2,1)}), bf16[64,1,512,128]{2,3,1,0:T(8,128)(2,1)}, u32[]{:S(2)}, u32[]{:S(2)}) %all-to-all-start) | async-done | bytes 8388640 | tf_op jit(solution)/shard_map/all_to_all | solution.py:81
  208.9 6.5 %all-to-all-start.1 = ((bf16[64,1,512,128]{2,3,1,0:T(8,128)(2,1)}), bf16[64,1,512,128]{2,3,1,0:T(8,128)(2,1)}, u32[]{:S(2)}, u32[]{:S(2)}) async-start(bf16[64,1,512,128]{2,3,1,0:T(8,128)(2,1)} %bitcast.97), calls=%async_computation.1 | async-start | bytes 16777216 | tf_op jit(solution)/shard_map/all_to_all | solution.py:89
  215.3 2.4 copy.92
  217.7 3.9 copy.97
  222.1 2.9 copy.88
  224.9 2.4 copy.98
  227.5 11.9 %copy.91 = bf16[64,1,512,128]{3,2,0,1:T(8,128)(2,1)} copy(bf16[64,1,512,128]{2,3,1,0:T(8,128)(2,1)} %all-to-all-done) | data formatting | bytes 16777216 | tf_op jit(solution)/shard_map/all_to_all | solution.py:81
  239.4 6.4 %gather_fusion.1 = bf16[32,512,128]{2,1,0:T(8,128)(2,1)} fusion(bf16[64,512,128]{2,1,0:T(8,128)(2,1)} %bitcast.100, s32[1024]{0:T(1024)S(1)} %pad_clamp_fusion), kind=kCustom, calls=%fused_computation.1 | custom fusion | bytes 8388736 | tf_op jit(solution)/shard_map/gather | solution.py:59
  245.8 155.7 %all-to-all-done.1 = bf16[64,1,512,128]{2,3,1,0:T(8,128)(2,1)} async-done(((bf16[64,1,512,128]{2,3,1,0:T(8,128)(2,1)}), bf16[64,1,512,128]{2,3,1,0:T(8,128)(2,1)}, u32[]{:S(2)}, u32[]{:S(2)}) %all-to-all-start.1) | async-done | bytes 8388640 | tf_op jit(solution)/shard_map/all_to_all | solution.py:89
  401.5 11.9 %copy.96 = bf16[64,1,512,128]{3,2,0,1:T(8,128)(2,1)} copy(bf16[64,1,512,128]{2,3,1,0:T(8,128)(2,1)} %all-to-all-done.1) | data formatting | bytes 16777216 | tf_op jit(solution)/shard_map/all_to_all | solution.py:89
  413.4 6.6 %gather_fusion.3 = bf16[32,512,128]{2,1,0:T(8,128)(2,1)} fusion(bf16[64,512,128]{2,1,0:T(8,128)(2,1)} %bitcast.99, s32[1024]{0:T(1024)S(1)} %pad_clamp_fusion), kind=kCustom, calls=%fused_computation.3 | custom fusion | bytes 8388736 | tf_op jit(solution)/shard_map/gather | solution.py:59
  420.0 8.6 %pad_maximum_fusion = (bf16[16,1536,128]{2,1,0:T(8,128)(2,1)}, bf16[16,1536,128]{2,1,0:T(8,128)(2,1)}) fusion(bf16[16,1024,128]{2,1,0:T(8,128)(2,1)} %bitcast.101, bf16[16,512,128]{2,1,0:T(8,128)(2,1)S(1)} %copy-done, bf16[16,1024,128]{2,1,0:T(8,128)(2,1)} %bitcast.102, bf16[16,512,128]{2,1,0:T(8,128)(2,1)} %copy.97), kind=kLoop, calls=%fused_computation.39 | loop fusion | flops 25165824 | bytes 25165824 | tf_op jit(solution)/shard_map/concatenate | solution.py:82
  428.5 41.8 %while.24 = (s32[]{:T(128)}, f32[16,512]{1,0:T(8,128)S(1)}, f32[16,512]{1,0:T(8,128)S(1)}, pred[16,1024]{1,0:T(8,128)(4,1)S(1)}, bf16[16,512,128]{2,1,0:T(8,128)...) while((s32[]{:T(128)}, f32[16,512]{1,0:T(8,128)S(1)}, ...), condition=%wide.region_7.8_spmd.clone, body=%wide.region_4.7_spmd.clone.sunk | while | flops 206306304 | bytes 7361642 | solution.py:88
  428.6 1.8 fusion.40
  430.4 0.6 exponential_reduce_fusion.2
  431.3 1.8 fusion.40
  433.9 1.8 fusion.40
  435.6 0.6 exponential_reduce_fusion.2
  436.5 1.8 fusion.40
  439.1 1.8 fusion.40
  441.7 1.8 fusion.40
  443.5 0.6 exponential_reduce_fusion.2
  444.3 1.8 fusion.40
  446.1 0.6 exponential_reduce_fusion.2
  446.9 1.8 fusion.40
  449.6 1.8 fusion.40
  451.3 0.6 exponential_reduce_fusion.2
  452.2 1.8 fusion.40
  454.8 1.8 fusion.40
  457.4 1.8 fusion.40
  460.0 1.8 fusion.40
  462.6 1.8 fusion.40
  465.2 1.8 fusion.40
  467.9 1.8 fusion.40
  470.3 50.1 %while.25 = (s32[]{:T(128)}, bf16[16,512,128]{2,1,0:T(8,128)(2,1)}, pred[16,1024]{1,0:T(8,128)(4,1)S(1)}, bf16[16,512,128]{2,1,0:T(8,128)(2,1)}, bf16[16,1536,12...) while((s32[]{:T(128)}, bf16[16,512,128]{2,1,0:T(8,128)(2,1)}, ...), condition=%wide.region_9.10_spmd.clone, body=%wide.region_8.9_spmd.clone.sunk | while | flops 407699456 | bytes 1593454 | solution.py:99
  470.5 3.0 fusion.44
  473.6 3.0 fusion.44
  476.8 3.0 fusion.44
  479.9 3.0 fusion.44
  483.0 3.0 fusion.44
  486.1 3.0 fusion.44
  489.3 3.0 fusion.44
  492.4 3.0 fusion.44
  495.5 3.0 fusion.44
  498.7 3.0 fusion.44
  501.8 3.0 fusion.44
  504.9 3.0 fusion.44
  508.0 3.0 fusion.44
  511.2 3.0 fusion.44
  514.3 3.0 fusion.44
  517.4 3.0 fusion.44
  520.4 2.9 copy.99
  523.4 2.3 reshape.290
  525.7 1.5 collective-permute-start
  527.2 47.4 %collective-permute-done = bf16[1,512,2048]{2,1,0:T(8,128)(2,1)S(1)} collective-permute-done((bf16[1,512,2048]{2,1,0:T(8,128)(2,1)}, bf16[1,512,2048]{2,1,0:T(8,128)(2,1)S(1)}, u32[]{:S(2)}, u32[]{:S(2)}) %collective-permute-start) | collective-permute-done | bytes 2097184 | tf_op jit(solution)/shard_map/ppermute | solution.py:14
  574.6 1.3 copy.127
  (178 shorter events, 13.0 us)
Async XLA Ops:
  11.1 197.8 %all-to-all-start = ((bf16[64,1,512,128]{2,3,1,0:T(8,128)(2,1)}), bf16[64,1,512,128]{2,3,1,0:T(8,128)(2,1)}, u32[]{:S(2)}, u32[]{:S(2)}) async-start(bf16[64,1,512,128]{2,3,1,0:T(8,128)(2,1)} %bitcast.98), calls=%async_computation | async-start | bytes 16777216 | tf_op jit(solution)/shard_map/all_to_all | solution.py:81
  208.9 192.6 %all-to-all-start.1 = ((bf16[64,1,512,128]{2,3,1,0:T(8,128)(2,1)}), bf16[64,1,512,128]{2,3,1,0:T(8,128)(2,1)}, u32[]{:S(2)}, u32[]{:S(2)}) async-start(bf16[64,1,512,128]{2,3,1,0:T(8,128)(2,1)} %bitcast.97), calls=%async_computation.1 | async-start | bytes 16777216 | tf_op jit(solution)/shard_map/all_to_all | solution.py:89
  217.7 3.9 copy-start.1
  413.4 6.6 %copy-start = (bf16[16,512,128]{2,1,0:T(8,128)(2,1)S(1)}, bf16[16,512,128]{2,1,0:T(8,128)(2,1)}, u32[]{:S(2)}) copy-start(bf16[16,512,128]{2,1,0:T(8,128)(2,1)} %copy.92) | copy-start | bytes 6291460
  525.7 48.9 %collective-permute-start = (bf16[1,512,2048]{2,1,0:T(8,128)(2,1)}, bf16[1,512,2048]{2,1,0:T(8,128)(2,1)S(1)}, u32[]{:S(2)}, u32[]{:S(2)}) collective-permute-start(bf16[1,512,2048]{2,1,0:T(8,128)(2,1)} %reshape.290), channel_id=1, source_target_pairs={{0,1},{1,2},{2,3},{3,0},{4,5},{5,6},{6,7},{7,4},{8,9},{9,10},{10,1... | collective-permute-start | bytes 6291464 | tf_op jit(solution)/shard_map/ppermute | solution.py:14
where the time goes:
time: 578 us; the launch traced here: 576 us
  waiting for transfers between devices  378 us (65%)
  local copies, waits for them, and re-layouts  78 us (13%)
  matrix products  75.8 us (13%)
  other arithmetic  23.2 us (4%)
  starting transfers between devices  19.6 us (3%)
    all_to_all x1, waiting for transfers between devices, per_device(): lax.all_to_all(key_heads[safe_asked], 'ctx', split_axis=0, concat_axis=0,...  175 us
    all_to_all x1, waiting for transfers between devices, per_device(): lax.all_to_all(value_heads[safe_asked], 'ctx', split_axis=0, concat_axis=...  156 us
    dot_general x16, matrix products, weighted(): jnp.dot(prob_rows, value_rows, preferred_element_type=jnp.float32)  47.7 us
    ppermute x1, waiting for transfers between devices, passed_along(): return lax.ppermute(value, axis, pairs)  47.4 us
    dot_general x16, matrix products, masked_scores(): lax.dot_general(query_head, key_rows, (((1,), (1,)), ((), ())), preferred...  28.1 us
    unnamed x11, local copies, waits for them, and re-layouts  13.5 us
    gather x2, local copies, waits for them, and re-layouts, arrived(): return flat_slots[flat_slot].reshape(HEADS, PICKS * block_rows, last_width)  13 us
    all_to_all x1, local copies, waits for them, and re-layouts, per_device(): lax.all_to_all(key_heads[safe_asked], 'ctx', split_axis=0, concat_axis=0,...  11.9 us
  transfers between devices with their start and end apart: 3, of which 3 were waited for; matrix products, arithmetic and copies ran while one was open for 7% of the time, Pallas kernels for 0%

commit v1 on v0

v1 whole, which is shorter than its diff:
```python
import functools

import jax
import jax.numpy as jnp
from jax import lax
from jax.experimental import pallas as pl
from jax.experimental.pallas import tpu as pltpu
from jax.sharding import PartitionSpec as P

HEADS = 16
HD = 128
PICKS = 2
MESH = pl.DeviceIdType.MESH


def passed_along(value, axis, steps):
    count = lax.axis_size(axis)
    pairs = [(source, (source + steps) % count) for source in range(count)]
    return lax.ppermute(value, axis, pairs)


def pack_kernel(asked_ref, k_ref, v_ref, out_ref):
    out_ref[0, 0] = k_ref[...]
    out_ref[0, 1] = v_ref[...]


def pack_requested(asked, keys, values):
    count = asked.shape[0]
    rows = keys.shape[0]
    grid_spec = pltpu.PrefetchScalarGridSpec(
        num_scalar_prefetch=1,
        grid=(count,),
        in_specs=[
            pl.BlockSpec((rows, HD), lambda q, asked_ref: (0, asked_ref[q])),
            pl.BlockSpec((rows, HD), lambda q, asked_ref: (0, asked_ref[q])),
        ],
        out_specs=pl.BlockSpec((1, 2, rows, HD), lambda q, asked_ref: (q, 0, 0, 0)),
    )
    return pl.pallas_call(
        pack_kernel,
        grid_spec=grid_spec,
        out_shape=jax.ShapeDtypeStruct((count, 2, rows, HD), keys.dtype),
    )(asked, keys, values)


def exchange_kernel(count, send_ref, recv_ref, send_sems, recv_sems):
    me = lax.axis_index("ctx")
    barrier = pltpu.get_barrier_semaphore()

    def greet(step, carry):
        peer = lax.rem(me + step, count)
        pl.semaphore_signal(barrier, 1, device_id={"ctx": peer}, device_id_type=MESH)
        return carry

    lax.fori_loop(1, count, greet, 0)
    pl.semaphore_wait(barrier, count - 1)

    def copy_between(source, target, slot):
        return pltpu.make_async_remote_copy(
            src_ref=send_ref.at[slot],
            dst_ref=recv_ref.at[source],
            send_sem=send_sems.at[slot],
            recv_sem=recv_sems.at[source],
            device_id={"ctx": target},
            device_id_type=MESH,
        )

    def start(step, carry):
        target = me + step

        @pl.when(target < count)
        def _():
            copy_between(me, target, target).start()

        return carry

    lax.fori_loop(1, count, start, 0)

    def finish(peer, carry):
        @pl.when(peer > me)
        def _():
            copy_between(me, peer, peer).wait_send()

        @pl.when(peer < me)
        def _():
            copy_between(peer, peer, peer).wait_recv()

        return carry

    lax.fori_loop(0, count, finish, 0)


def exchange(send):
    count = send.shape[0]
    return pl.pallas_call(
        functools.partial(exchange_kernel, count),
        out_shape=jax.ShapeDtypeStruct(send.shape, send.dtype),
        in_specs=[pl.BlockSpec(memory_space=pl.ANY)],
        out_specs=pl.BlockSpec(memory_space=pl.ANY),
        scratch_shapes=[
            pltpu.SemaphoreType.DMA((count,)),
            pltpu.SemaphoreType.DMA((count,)),
        ],
        compiler_params=pltpu.CompilerParams(collective_id=0, has_side_effects=True),
    )(send)


def attend_kernel(slot_ref, live_ref, q_ref, k_ref, v_ref, first_ref, second_ref, o_ref):
    head = pl.program_id(0)
    rows = q_ref.shape[0]
    score_scale = HD ** (-0.5)
    dims = (((1,), (1,)), ((), ()))
    query = q_ref[...]

    def scores_against(key_rows):
        raw = lax.dot_general(query, key_rows, dims, preferred_element_type=jnp.float32)
        return raw * score_scale

    row_index = lax.broadcasted_iota(jnp.int32, (rows, rows), 0)
    col_index = lax.broadcasted_iota(jnp.int32, (rows, rows), 1)
    own = jnp.where(row_index >= col_index, scores_against(k_ref[...]), -jnp.inf)
    live_first = live_ref[PICKS * head] > 0
    live_second = live_ref[PICKS * head + 1] > 0
    first = jnp.where(live_first, scores_against(first_ref[0, 0]), -jnp.inf)
    second = jnp.where(live_second, scores_against(second_ref[0, 0]), -jnp.inf)
    row_top = jnp.maximum(
        jnp.maximum(jnp.max(own, axis=1), jnp.max(first, axis=1)), jnp.max(second, axis=1)
    )[:, None]
    own = jnp.exp(own - row_top)
    first = jnp.exp(first - row_top)
    second = jnp.exp(second - row_top)
    row_total = (
        jnp.sum(own, axis=1) + jnp.sum(first, axis=1) + jnp.sum(second, axis=1)
    )[:, None]
    first_values = jnp.where(live_first, first_ref[0, 1], jnp.zeros_like(first_ref[0, 1]))
    second_values = jnp.where(live_second, second_ref[0, 1], jnp.zeros_like(second_ref[0, 1]))
    mixed = jnp.dot((own / row_total).astype(jnp.bfloat16), v_ref[...],
                    preferred_element_type=jnp.float32)
    mixed += jnp.dot((first / row_total).astype(jnp.bfloat16), first_values,
                     preferred_element_type=jnp.float32)
    mixed += jnp.dot((second / row_total).astype(jnp.bfloat16), second_values,
                     preferred_element_type=jnp.float32)
    o_ref[...] = mixed.astype(o_ref.dtype)


def attend(slots, live, queries, keys, values, received):
    rows = queries.shape[0]
    head_block = pl.BlockSpec((rows, HD), lambda h, slot_ref, live_ref: (0, h))
    grid_spec = pltpu.PrefetchScalarGridSpec(
        num_scalar_prefetch=2,
        grid=(HEADS,),
        in_specs=[
            head_block,
            head_block,
            head_block,
            pl.BlockSpec(
                (1, 2, rows, HD), lambda h, slot_ref, live_ref: (slot_ref[PICKS * h], 0, 0, 0)
            ),
            pl.BlockSpec(
                (1, 2, rows, HD),
                lambda h, slot_ref, live_ref: (slot_ref[PICKS * h + 1], 0, 0, 0),
            ),
        ],
        out_specs=head_block,
    )
    return pl.pallas_call(
        attend_kernel,
        grid_spec=grid_spec,
        out_shape=jax.ShapeDtypeStruct(queries.shape, queries.dtype),
    )(slots, live, queries, keys, values, received, received)


def per_device(queries, keys, values, picks):
    rank_here = lax.axis_index("ctx")
    every_pick = picks[0]
    head_ids = lax.broadcasted_iota(jnp.int32, every_pick.shape, 1)
    asked = jnp.sum(jnp.where(every_pick == rank_here, head_ids, 0), axis=(1, 2))
    send = pack_requested(asked.astype(jnp.int32), keys[0], values[0])
    received = exchange(send)
    chosen = lax.dynamic_index_in_dim(every_pick, rank_here, 0, keepdims=False).reshape(-1)
    live = (chosen >= 0).astype(jnp.int32)
    slots = jnp.maximum(chosen, 0).astype(jnp.int32)
    merged = attend(slots, live, queries[0], keys[0], values[0], received)
    merged = passed_along(merged[None], "pipe", 1)
    return merged


def solution(mesh):
    placed = (
        P("pipe", "ctx", None),
        P("pipe", "ctx", None),
        P("pipe", "ctx", None),
        P("pipe", None, None, None),
    )
    return jax.shard_map(
        per_device, mesh=mesh, in_specs=placed, out_specs=P("pipe", "ctx", None), check_vma=False
    )
```

time: 578 us -> 555 us (0.960)
  the two profiles are of different devices: /device:TPU:48 before, /device:TPU:1 now
where the time goes in v1:
time: 555 us; the launch traced here: 554 us
  Pallas kernels  501 us (90%)
  waiting for transfers between devices  48.1 us (9%)
    pallas_call x1, Pallas kernels, exchange(): pl.pallas_call(functools.partial(exchange_kernel, count), out_shape=jax.S...  423 us
    ppermute x1, waiting for transfers between devices, passed_along(): return lax.ppermute(value, axis, pairs)  48.1 us
    pallas_call x1, Pallas kernels, attend(): pl.pallas_call(attend_kernel, grid_spec=grid_spec, out_shape=jax.ShapeDty...  39.7 us
    pallas_call x1, Pallas kernels, pack_requested(): pl.pallas_call(pack_kernel, grid_spec=grid_spec, out_shape=jax.ShapeDtype...  37.6 us
  transfers between devices with their start and end apart: 1, of which 1 were waited for; matrix products, arithmetic and copies ran while one was open for 0% of the time, Pallas kernels for 0%

profile of v1, /device:TPU:1, one launch (start us, length us, event | category | flops | bytes accessed | tf_op | source)
XLA Modules:
  0.0 554.1 jit_solution(10583722006995249929)
XLA Ops:
  0.0 1.3 fusion.1.asked_ref
  1.3 1.4 fusion
  2.7 0.6 reshape.12.live_ref
  3.3 0.7 max.6.slot_ref
  4.0 37.6 %shard_map.46.send_ref = bf16[64,2,512,128]{3,2,1,0:T(8,128)(2,1)} custom-call(s32[64]{0:T(128)} %fusion.1.asked_ref, bf16[512,2048]{1,0:T(8,128)(2,1)} %bitcast.8, bf16[512,2048]{1,0:T(8,128)(2,1)} %bitcast.10), custom_call_target="tpu_custom_call" | custom-call | tf_op jit(solution)/shard_map/pallas_call | solution.py:39
  41.6 423.4 %shard_map.47.first_ref.second_ref = bf16[64,2,512,128]{3,2,1,0:T(8,128)(2,1)} custom-call(bf16[64,2,512,128]{3,2,1,0:T(8,128)(2,1)} %shard_map.46.send_ref), custom_call_target="tpu_custom_call" | custom-call | tf_op jit(solution)/shard_map/pallas_call | solution.py:95
  465.1 39.7 %shard_map.48 = bf16[512,2048]{1,0:T(8,128)(2,1)} custom-call(s32[32]{0:T(128)} %max.6.slot_ref, s32[32]{0:T(128)} %reshape.12.live_ref, bf16[512,2048]{1,0:T(8,128)(2,1)} %bitcast.12, bf16[512,2048]{1,0:T(8,128)(2,1)} %bitcast.9, bf16[512,2048]{1,0:T(8,128)(2,1)} %bitcast.11, bf16[64,2,512,128]{3,2,1,0:T(8,128)(2,1)} %shard_map.47.first_ref.second_ref, ...), custom_call_target="tpu_custom_call" | custom-call | tf_op jit(solution)/shard_map/pallas_call | solution.py:166
  504.7 0.0 collective-permute-start
  504.7 48.1 %collective-permute-done = bf16[1,512,2048]{2,1,0:T(8,128)(2,1)S(1)} collective-permute-done((bf16[1,512,2048]{2,1,0:T(8,128)(2,1)}, bf16[1,512,2048]{2,1,0:T(8,128)(2,1)S(1)}, u32[]{:S(2)}, u32[]{:S(2)}) %collective-permute-start) | collective-permute-done | bytes 2097184 | tf_op jit(solution)/shard_map/ppermute | solution.py:19
  552.8 1.3 copy.6
Async XLA Ops:
  504.7 48.1 %collective-permute-start = (bf16[1,512,2048]{2,1,0:T(8,128)(2,1)}, bf16[1,512,2048]{2,1,0:T(8,128)(2,1)S(1)}, u32[]{:S(2)}, u32[]{:S(2)}) collective-permute-start(bf16[1,512,2048]{2,1,0:T(8,128)(2,1)} %bitcast.13), channel_id=1, source_target_pairs={{0,1},{1,2},{2,3},{3,0},{4,5},{5,6},{6,7},{7,4},{8,9},{9,10},{10,1... | collective-permute-start | bytes 6291464 | tf_op jit(solution)/shard_map/ppermute | solution.py:19

commit v2 on v1

--- a/solution.py
+++ b/solution.py
@@ -19,25 +19,27 @@
     return lax.ppermute(value, axis, pairs)
 
 
-def pack_kernel(asked_ref, k_ref, v_ref, out_ref):
-    out_ref[0, 0] = k_ref[...]
-    out_ref[0, 1] = v_ref[...]
+def pack_kernel(group, asked_ref, k_ref, v_ref, out_ref):
+    base = pl.program_id(0) * group
+    for i in range(group):
+        column = pl.multiple_of(asked_ref[base + i] * HD, HD)
+        out_ref[i, 0] = k_ref[:, pl.ds(column, HD)]
+        out_ref[i, 1] = v_ref[:, pl.ds(column, HD)]
 
 
 def pack_requested(asked, keys, values):
     count = asked.shape[0]
-    rows = keys.shape[0]
+    rows, width = keys.shape
+    group = 8
+    whole = pl.BlockSpec((rows, width), lambda g, asked_ref: (0, 0))
     grid_spec = pltpu.PrefetchScalarGridSpec(
         num_scalar_prefetch=1,
-        grid=(count,),
-        in_specs=[
-            pl.BlockSpec((rows, HD), lambda q, asked_ref: (0, asked_ref[q])),
-            pl.BlockSpec((rows, HD), lambda q, asked_ref: (0, asked_ref[q])),
-        ],
-        out_specs=pl.BlockSpec((1, 2, rows, HD), lambda q, asked_ref: (q, 0, 0, 0)),
+        grid=(count // group,),
+        in_specs=[whole, whole],
+        out_specs=pl.BlockSpec((group, 2, rows, HD), lambda g, asked_ref: (g, 0, 0, 0)),
     )
     return pl.pallas_call(
-        pack_kernel,
+        functools.partial(pack_kernel, group),
         grid_spec=grid_spec,
         out_shape=jax.ShapeDtypeStruct((count, 2, rows, HD), keys.dtype),
     )(asked, keys, values)
@@ -129,16 +131,16 @@
     own = jnp.exp(own - row_top)
     first = jnp.exp(first - row_top)
     second = jnp.exp(second - row_top)
-    row_total = (
+    row_scale = 1.0 / (
         jnp.sum(own, axis=1) + jnp.sum(first, axis=1) + jnp.sum(second, axis=1)
     )[:, None]
     first_values = jnp.where(live_first, first_ref[0, 1], jnp.zeros_like(first_ref[0, 1]))
     second_values = jnp.where(live_second, second_ref[0, 1], jnp.zeros_like(second_ref[0, 1]))
-    mixed = jnp.dot((own / row_total).astype(jnp.bfloat16), v_ref[...],
+    mixed = jnp.dot((own * row_scale).astype(jnp.bfloat16), v_ref[...],
                     preferred_element_type=jnp.float32)
-    mixed += jnp.dot((first / row_total).astype(jnp.bfloat16), first_values,
+    mixed += jnp.dot((first * row_scale).astype(jnp.bfloat16), first_values,
                      preferred_element_type=jnp.float32)
-    mixed += jnp.dot((second / row_total).astype(jnp.bfloat16), second_values,
+    mixed += jnp.dot((second * row_scale).astype(jnp.bfloat16), second_values,
                      preferred_element_type=jnp.float32)
     o_ref[...] = mixed.astype(o_ref.dtype)
 
@@ -176,7 +178,7 @@
     head_ids = lax.broadcasted_iota(jnp.int32, every_pick.shape, 1)
     asked = jnp.sum(jnp.where(every_pick == rank_here, head_ids, 0), axis=(1, 2))
     send = pack_requested(asked.astype(jnp.int32), keys[0], values[0])
-    received = exchange(send)
+    received = lax.all_to_all(send, "ctx", split_axis=0, concat_axis=0, tiled=True)
     chosen = lax.dynamic_index_in_dim(every_pick, rank_here, 0, keepdims=False).reshape(-1)
     live = (chosen >= 0).astype(jnp.int32)
     slots = jnp.maximum(chosen, 0).astype(jnp.int32)

time: 555 us -> 487 us (0.88)
  the two profiles are of different devices: /device:TPU:1 before, /device:TPU:48 now
where the time goes in v2:
time: 487 us
  waiting for transfers between devices  418 us (86%)
  Pallas kernels  50.9 us (10%)
  starting transfers between devices  13.6 us (3%)
    all_to_all x1, waiting for transfers between devices, per_device(): lax.all_to_all(send, 'ctx', split_axis=0, concat_axis=0, tiled=True)  370 us
    ppermute x1, waiting for transfers between devices, passed_along(): return lax.ppermute(value, axis, pairs)  47.5 us
    pallas_call x1, Pallas kernels, attend(): pl.pallas_call(attend_kernel, grid_spec=grid_spec, out_shape=jax.ShapeDty...  39.7 us
    all_to_all x1, starting transfers between devices, per_device(): lax.all_to_all(send, 'ctx', split_axis=0, concat_axis=0, tiled=True)  12.2 us
    pallas_call x1, Pallas kernels, pack_requested(): pl.pallas_call(functools.partial(pack_kernel, group), grid_spec=grid_spec...  11.3 us
  transfers between devices with their start and end apart: 2, of which 2 were waited for; matrix products, arithmetic and copies ran while one was open for 0% of the time, Pallas kernels for 0%

profile of v2, /device:TPU:48, one launch (start us, length us, event | category | flops | bytes accessed | tf_op | source)
XLA Modules:
  0.0 486.8 jit_solution(10961652041515532135)
XLA Ops:
  0.0 1.3 fusion.1.asked_ref
  1.3 11.3 %shard_map.46 = bf16[64,2,512,128]{3,2,1,0:T(8,128)(2,1)} custom-call(s32[64]{0:T(128)} %fusion.1.asked_ref, bf16[512,2048]{1,0:T(8,128)(2,1)} %bitcast.8, bf16[512,2048]{1,0:T(8,128)(2,1)} %bitcast.10), custom_call_target="tpu_custom_call" | custom-call | tf_op jit(solution)/shard_map/pallas_call | solution.py:41
  12.5 0.0 copy-start
  12.5 12.2 %all-to-all-start = ((bf16[64,2,512,128]{3,2,1,0:T(8,128)(2,1)}), bf16[64,2,512,128]{3,2,1,0:T(8,128)(2,1)}, u32[]{:S(2)}, u32[]{:S(2)}) async-start(bf16[64,2,512,128]{3,2,1,0:T(8,128)(2,1)} %shard_map.46), calls=%async_computation | async-start | bytes 33554432 | tf_op jit(solution)/shard_map/all_to_all | solution.py:181
  24.8 0.0 copy-done
  24.8 0.7 fusion
  25.5 0.6 reshape.12.live_ref
  26.1 0.7 max.6.slot_ref
  26.8 370.2 %all-to-all-done.first_ref.second_ref = bf16[64,2,512,128]{3,2,1,0:T(8,128)(2,1)} async-done(((bf16[64,2,512,128]{3,2,1,0:T(8,128)(2,1)}), bf16[64,2,512,128]{3,2,1,0:T(8,128)(2,1)}, u32[]{:S(2)}, u32[]{:S(2)}) %all-to-all-start) | async-done | bytes 16777248 | tf_op jit(solution)/shard_map/all_to_all | solution.py:181
  396.9 39.7 %shard_map.47 = bf16[512,2048]{1,0:T(8,128)(2,1)} custom-call(s32[32]{0:T(128)} %max.6.slot_ref, s32[32]{0:T(128)} %reshape.12.live_ref, bf16[512,2048]{1,0:T(8,128)(2,1)} %bitcast.12, bf16[512,2048]{1,0:T(8,128)(2,1)} %bitcast.9, bf16[512,2048]{1,0:T(8,128)(2,1)} %bitcast.11, bf16[64,2,512,128]{3,2,1,0:T(8,128)(2,1)} %all-to-all-done.first_ref.second_ref, ...), custom_call_target="tpu_custom_call" | custom-call | tf_op jit(solution)/shard_map/pallas_call | solution.py:168
  436.6 1.4 collective-permute-start
  438.0 47.5 %collective-permute-done = bf16[1,512,2048]{2,1,0:T(8,128)(2,1)S(1)} collective-permute-done((bf16[1,512,2048]{2,1,0:T(8,128)(2,1)}, bf16[1,512,2048]{2,1,0:T(8,128)(2,1)S(1)}, u32[]{:S(2)}, u32[]{:S(2)}) %collective-permute-start) | collective-permute-done | bytes 2097184 | tf_op jit(solution)/shard_map/ppermute | solution.py:19
  485.5 1.3 copy.6
Async XLA Ops:
  12.5 12.2 %copy-start = (s32[1,64,16,2]{1,3,2,0:T(2,128)S(1)}, s32[1,64,16,2]{1,3,2,0:T(2,128)}, u32[]{:S(2)}) copy-start(s32[1,64,16,2]{1,3,2,0:T(2,128)} %param.7) | copy-start | bytes 24580
  12.5 384.4 %all-to-all-start = ((bf16[64,2,512,128]{3,2,1,0:T(8,128)(2,1)}), bf16[64,2,512,128]{3,2,1,0:T(8,128)(2,1)}, u32[]{:S(2)}, u32[]{:S(2)}) async-start(bf16[64,2,512,128]{3,2,1,0:T(8,128)(2,1)} %shard_map.46), calls=%async_computation | async-start | bytes 33554432 | tf_op jit(solution)/shard_map/all_to_all | solution.py:181
  436.6 48.9 %collective-permute-start = (bf16[1,512,2048]{2,1,0:T(8,128)(2,1)}, bf16[1,512,2048]{2,1,0:T(8,128)(2,1)S(1)}, u32[]{:S(2)}, u32[]{:S(2)}) collective-permute-start(bf16[1,512,2048]{2,1,0:T(8,128)(2,1)} %bitcast.13), channel_id=1, source_target_pairs={{0,1},{1,2},{2,3},{3,0},{4,5},{5,6},{6,7},{7,4},{8,9},{9,10},{10,1... | collective-permute-start | bytes 6291464 | tf_op jit(solution)/shard_map/ppermute | solution.py:19

commit v3 on v2

v3 whole, which is shorter than its diff:
```python
import functools

import jax
import jax.numpy as jnp
from jax import lax
from jax.experimental import pallas as pl
from jax.experimental.pallas import tpu as pltpu
from jax.sharding import PartitionSpec as P

HEADS = 16
HD = 128
PICKS = 2
MESH = pl.DeviceIdType.MESH


def passed_along(value, axis, steps):
    count = lax.axis_size(axis)
    pairs = [(source, (source + steps) % count) for source in range(count)]
    return lax.ppermute(value, axis, pairs)


def pack_kernel(group, count_in, wanted_ref, *refs):
    sources, out_ref = refs[:count_in], refs[count_in]
    base = pl.program_id(0) * group
    for i in range(group):
        column = pl.multiple_of(wanted_ref[base + i] * HD, HD)
        for j, source in enumerate(sources):
            out_ref[i, j] = source[:, pl.ds(column, HD)]


def pack_heads(wanted, *sources):
    count = wanted.shape[0]
    rows, width = sources[0].shape
    group = 8
    whole = pl.BlockSpec((rows, width), lambda g, wanted_ref: (0, 0))
    grid_spec = pltpu.PrefetchScalarGridSpec(
        num_scalar_prefetch=1,
        grid=(count // group,),
        in_specs=[whole] * len(sources),
        out_specs=pl.BlockSpec(
            (group, len(sources), rows, HD), lambda g, wanted_ref: (g, 0, 0, 0)
        ),
    )
    return pl.pallas_call(
        functools.partial(pack_kernel, group, len(sources)),
        grid_spec=grid_spec,
        out_shape=jax.ShapeDtypeStruct((count, len(sources), rows, HD), sources[0].dtype),
    )(wanted, *sources)


def partial_kernel(count, query_out_ref, kv_ref, part_ref, stat_ref, query_in, part_out,
                   stat_out, query_sems, part_sems, stat_sems):
    me = lax.axis_index("ctx")
    rows = part_ref.shape[1]
    score_scale = HD ** (-0.5)
    dims = (((1,), (1,)), ((), ()))
    barrier = pltpu.get_barrier_semaphore()

    def greet(step, carry):
        peer = lax.rem(me + step, count)
        pl.semaphore_signal(barrier, 1, device_id={"ctx": peer}, device_id_type=MESH)
        return carry

    lax.fori_loop(1, count, greet, 0)
    pl.semaphore_wait(barrier, count - 1)

    def query_copy(source, target):
        return pltpu.make_async_remote_copy(
            src_ref=query_out_ref.at[target, 0],
            dst_ref=query_in.at[source],
            send_sem=query_sems.at[0, target],
            recv_sem=query_sems.at[1, source],
            device_id={"ctx": target},
            device_id_type=MESH,
        )

    def part_copy(source, target):
        return pltpu.make_async_remote_copy(
            src_ref=part_out.at[target],
            dst_ref=part_ref.at[source],
            send_sem=part_sems.at[0, target],
            recv_sem=part_sems.at[1, source],
            device_id={"ctx": target},
            device_id_type=MESH,
        )

    def stat_copy(source, target):
        return pltpu.make_async_remote_copy(
            src_ref=stat_out.at[target],
            dst_ref=stat_ref.at[source],
            send_sem=stat_sems.at[0, target],
            recv_sem=stat_sems.at[1, source],
            device_id={"ctx": target},
            device_id_type=MESH,
        )

    def ask(step, carry):
        owner = me - step

        @pl.when(owner >= 0)
        def _():
            query_copy(me, owner).start()

        return carry

    lax.fori_loop(1, count, ask, 0)

    def serve(step, carry):
        asker = me + step

        @pl.when(asker < count)
        def _():
            query_copy(asker, me).wait_recv()
            scores = lax.dot_general(
                query_in[asker], kv_ref[asker, 0], dims, preferred_element_type=jnp.float32
            ) * score_scale
            row_top = jnp.max(scores, axis=1, keepdims=True)
            weights = jnp.exp(scores - row_top)
            row_total = jnp.sum(weights, axis=1, keepdims=True)
            mixed = jnp.dot(weights.astype(jnp.bfloat16), kv_ref[asker, 1],
                            preferred_element_type=jnp.float32)
            part_out[asker] = mixed.astype(part_out.dtype)
            stats = jnp.concatenate(
                [row_top, row_total, jnp.zeros((rows, 6), jnp.float32)], axis=1
            )
            stat_out[asker] = stats.T
            part_copy(me, asker).start()
            stat_copy(me, asker).start()

        return carry

    lax.fori_loop(1, count, serve, 0)

    def finish(peer, carry):
        @pl.when(peer < me)
        def _():
            query_copy(me, peer).wait_send()
            part_copy(peer, me).wait_recv()
            stat_copy(peer, me).wait_recv()

        @pl.when(peer > me)
        def _():
            part_copy(me, peer).wait_send()
            stat_copy(me, peer).wait_send()

        return carry

    lax.fori_loop(0, count, finish, 0)


def partials(query_out, kv):
    count, _, rows, _ = kv.shape
    return pl.pallas_call(
        functools.partial(partial_kernel, count),
        out_shape=(
            jax.ShapeDtypeStruct((count, rows, HD), kv.dtype),
            jax.ShapeDtypeStruct((count, 8, rows), jnp.float32),
        ),
        in_specs=[
            pl.BlockSpec(memory_space=pl.ANY),
            pl.BlockSpec(memory_space=pltpu.VMEM),
        ],
        out_specs=(pl.BlockSpec(memory_space=pl.ANY), pl.BlockSpec(memory_space=pl.ANY)),
        scratch_shapes=[
            pltpu.VMEM((count, rows, HD), kv.dtype),
            pltpu.VMEM((count, rows, HD), kv.dtype),
            pltpu.VMEM((count, 8, rows), jnp.float32),
            pltpu.SemaphoreType.DMA((2, count)),
            pltpu.SemaphoreType.DMA((2, count)),
            pltpu.SemaphoreType.DMA((2, count)),
        ],
        compiler_params=pltpu.CompilerParams(
            collective_id=0, has_side_effects=True, vmem_limit_bytes=60 * 1024 * 1024
        ),
    )(query_out, kv)


def attend_kernel(slot_ref, live_ref, q_ref, k_ref, v_ref, first_ref, second_ref,
                  first_stat_ref, second_stat_ref, o_ref):
    head = pl.program_id(0)
    rows = q_ref.shape[0]
    score_scale = HD ** (-0.5)
    dims = (((1,), (1,)), ((), ()))
    raw = lax.dot_general(q_ref[...], k_ref[...], dims, preferred_element_type=jnp.float32)
    row_index = lax.broadcasted_iota(jnp.int32, (rows, rows), 0)
    col_index = lax.broadcasted_iota(jnp.int32, (rows, rows), 1)
    own = jnp.where(row_index >= col_index, raw * score_scale, -jnp.inf)

    def remote(live, part_ref, stat_ref):
        stats = stat_ref[0].T
        top = jnp.where(live, stats[:, 0:1], -jnp.inf)
        total = jnp.where(live, stats[:, 1:2], 0.0)
        part = jnp.where(live, part_ref[0].astype(jnp.float32), 0.0)
        return top, total, part

    first_top, first_total, first_part = remote(live_ref[PICKS * head] > 0, first_ref,
                                                first_stat_ref)
    second_top, second_total, second_part = remote(live_ref[PICKS * head + 1] > 0, second_ref,
                                                   second_stat_ref)
    row_top = jnp.maximum(jnp.maximum(jnp.max(own, axis=1, keepdims=True), first_top),
                          second_top)
    own = jnp.exp(own - row_top)
    first_scale = jnp.exp(first_top - row_top)
    second_scale = jnp.exp(second_top - row_top)
    row_scale = 1.0 / (
        jnp.sum(own, axis=1, keepdims=True) + first_scale * first_total
        + second_scale * second_total
    )
    mixed = jnp.dot((own * row_scale).astype(jnp.bfloat16), v_ref[...],
                    preferred_element_type=jnp.float32)
    mixed += (first_scale * row_scale) * first_part + (second_scale * row_scale) * second_part
    o_ref[...] = mixed.astype(o_ref.dtype)


def attend(slots, live, queries, keys, values, parts, stats):
    rows = queries.shape[0]
    head_block = pl.BlockSpec((rows, HD), lambda h, slot_ref, live_ref: (0, h))

    def picked(j, shape):
        return pl.BlockSpec(
            (1,) + shape, lambda h, slot_ref, live_ref: (slot_ref[PICKS * h + j], 0, 0)
        )

    grid_spec = pltpu.PrefetchScalarGridSpec(
        num_scalar_prefetch=2,
        grid=(HEADS,),
        in_specs=[
            head_block,
            head_block,
            head_block,
            picked(0, (rows, HD)),
            picked(1, (rows, HD)),
            picked(0, (8, rows)),
            picked(1, (8, rows)),
        ],
        out_specs=head_block,
    )
    return pl.pallas_call(
        attend_kernel,
        grid_spec=grid_spec,
        out_shape=jax.ShapeDtypeStruct(queries.shape, queries.dtype),
    )(slots, live, queries, keys, values, parts, parts, stats, stats)


def per_device(queries, keys, values, picks):
    rank_here = lax.axis_index("ctx")
    every_pick = picks[0]
    count = every_pick.shape[0]
    head_ids = lax.broadcasted_iota(jnp.int32, every_pick.shape, 1)
    asked = jnp.sum(jnp.where(every_pick == rank_here, head_ids, 0), axis=(1, 2))
    kv = pack_heads(asked.astype(jnp.int32), keys[0], values[0])
    chosen = lax.dynamic_index_in_dim(every_pick, rank_here, 0, keepdims=False).reshape(-1)
    owners = lax.broadcasted_iota(jnp.int32, (count, HEADS * PICKS), 0)
    wanted = jnp.sum(
        jnp.where(chosen[None, :] == owners, jnp.repeat(lax.iota(jnp.int32, HEADS), PICKS), 0),
        axis=1,
    )
    query_out = pack_heads(wanted.astype(jnp.int32), queries[0])
    parts, stats = partials(query_out, kv)
    live = (chosen >= 0).astype(jnp.int32)
    slots = jnp.maximum(chosen, 0).astype(jnp.int32)
    merged = attend(slots, live, queries[0], keys[0], values[0], parts, stats)
    merged = passed_along(merged[None], "pipe", 1)
    return merged


def solution(mesh):
    placed = (
        P("pipe", "ctx", None),
        P("pipe", "ctx", None),
        P("pipe", "ctx", None),
        P("pipe", None, None, None),
    )
    return jax.shard_map(
        per_device, mesh=mesh, in_specs=placed, out_specs=P("pipe", "ctx", None), check_vma=False
    )
```

time: 487 us -> 503 us (1.033)
  the two profiles are of different devices: /device:TPU:48 before, /device:TPU:249 now
where the time goes in v3:
time: 503 us
  Pallas kernels  448 us (89%)
  waiting for transfers between devices  48.2 us (10%)
    pallas_call x1, Pallas kernels, partials(): pl.pallas_call(functools.partial(partial_kernel, count), out_shape=(jax.S...  395 us
    ppermute x1, waiting for transfers between devices, passed_along(): return lax.ppermute(value, axis, pairs)  48.2 us
    pallas_call x1, Pallas kernels, attend(): pl.pallas_call(attend_kernel, grid_spec=grid_spec, out_shape=jax.ShapeDty...  33.4 us
    pallas_call x2, Pallas kernels, pack_heads(): pl.pallas_call(functools.partial(pack_kernel, group, len(sources)), grid_...  19.8 us
  transfers between devices with their start and end apart: 1, of which 1 were waited for; matrix products, arithmetic and copies ran while one was open for 0% of the time, Pallas kernels for 0%

profile of v3, /device:TPU:249, one launch (start us, length us, event | category | flops | bytes accessed | tf_op | source)
XLA Modules:
  0.0 502.6 jit_solution(16204855619533097194)
XLA Ops:
  0.0 1.3 fusion.wanted_ref
  1.3 1.1 dynamic-slice_reduce_fusion
  2.5 0.1 reshape.13
  2.6 0.5 broadcast_maximum_fusion.slot_ref
  3.1 0.5 compare_convert_fusion.live_ref
  3.6 0.1 reshape.14
  3.7 0.6 select_reduce_fusion.wanted_ref
  4.3 7.8 %shard_map.46.query_out_ref = bf16[64,1,512,128]{3,2,1,0:T(8,128)(2,1)} custom-call(s32[64]{0:T(128)} %select_reduce_fusion.wanted_ref, bf16[512,2048]{1,0:T(8,128)(2,1)} %bitcast.12), custom_call_target="tpu_custom_call" | custom-call | tf_op jit(solution)/shard_map/pallas_call | solution.py:44
  12.1 12.0 %shard_map.47.kv_ref = bf16[64,2,512,128]{3,2,1,0:T(8,128)(2,1)} custom-call(s32[64]{0:T(128)} %fusion.wanted_ref, bf16[512,2048]{1,0:T(8,128)(2,1)} %bitcast.8, bf16[512,2048]{1,0:T(8,128)(2,1)} %bitcast.10), custom_call_target="tpu_custom_call" | custom-call | tf_op jit(solution)/shard_map/pallas_call | solution.py:44
  24.1 395.1 %shard_map.48 = (bf16[64,512,128]{2,1,0:T(8,128)(2,1)}, f32[64,8,512]{2,1,0:T(8,128)}) custom-call(bf16[64,1,512,128]{3,2,1,0:T(8,128)(2,1)} %shard_map.46.query_out_ref, bf16[64,2,512,128]{3,2,1,0:T(8,128)(2,1)} %shard_map.47.kv_ref), custom_call_target="tpu_custom_call" | custom-call | tf_op jit(solution)/shard_map/pallas_call | solution.py:153
  419.3 33.4 %shard_map.49 = bf16[512,2048]{1,0:T(8,128)(2,1)} custom-call(s32[32]{0:T(128)} %broadcast_maximum_fusion.slot_ref, s32[32]{0:T(128)} %compare_convert_fusion.live_ref, bf16[512,2048]{1,0:T(8,128)(2,1)} %bitcast.13, bf16[512,2048]{1,0:T(8,128)(2,1)} %bitcast.9, bf16[512,2048]{1,0:T(8,128)(2,1)} %bitcast.11, ...), custom_call_target="tpu_custom_call" | custom-call | tf_op jit(solution)/shard_map/pallas_call | solution.py:238
  452.6 0.4 collective-permute-start
  453.1 48.2 %collective-permute-done = bf16[1,512,2048]{2,1,0:T(8,128)(2,1)S(1)} collective-permute-done((bf16[1,512,2048]{2,1,0:T(8,128)(2,1)}, bf16[1,512,2048]{2,1,0:T(8,128)(2,1)S(1)}, u32[]{:S(2)}, u32[]{:S(2)}) %collective-permute-start) | collective-permute-done | bytes 2097184 | tf_op jit(solution)/shard_map/ppermute | solution.py:19
  501.2 1.3 copy.6
  (1 shorter events, 0.0 us)
Async XLA Ops:
  452.6 48.6 %collective-permute-start = (bf16[1,512,2048]{2,1,0:T(8,128)(2,1)}, bf16[1,512,2048]{2,1,0:T(8,128)(2,1)S(1)}, u32[]{:S(2)}, u32[]{:S(2)}) collective-permute-start(bf16[1,512,2048]{2,1,0:T(8,128)(2,1)} %bitcast.14), channel_id=1, source_target_pairs={{0,1},{1,2},{2,3},{3,0},{4,5},{5,6},{6,7},{7,4},{8,9},{9,10},{10,1... | collective-permute-start | bytes 6291464 | tf_op jit(solution)/shard_map/ppermute | solution.py:19

commit v4 on v3

--- a/solution.py
+++ b/solution.py
@@ -94,16 +94,14 @@
             device_id_type=MESH,
         )
 
-    def ask(step, carry):
-        owner = me - step
-
-        @pl.when(owner >= 0)
+    def ask(owner, carry):
+        @pl.when(owner < me)
         def _():
             query_copy(me, owner).start()
 
         return carry
 
-    lax.fori_loop(1, count, ask, 0)
+    lax.fori_loop(0, count, ask, 0)
 
     def serve(step, carry):
         asker = me + step

time: 503 us -> 528 us (1.050)
  Pallas kernels: 448 us -> 470 us
    pallas_call x1, Pallas kernels: 395 us -> 417 us  [partials(): pl.pallas_call(functools.partial(partial_kernel, count), out_shape=(jax.S...]
where the time goes in v4:
time: 528 us
  Pallas kernels  470 us (89%)
  waiting for transfers between devices  49.3 us (9%)
    pallas_call x1, Pallas kernels, partials(): pl.pallas_call(functools.partial(partial_kernel, count), out_shape=(jax.S...  417 us
    ppermute x1, waiting for transfers between devices, passed_along(): return lax.ppermute(value, axis, pairs)  49.3 us
    pallas_call x1, Pallas kernels, attend(): pl.pallas_call(attend_kernel, grid_spec=grid_spec, out_shape=jax.ShapeDty...  33.4 us
    pallas_call x2, Pallas kernels, pack_heads(): pl.pallas_call(functools.partial(pack_kernel, group, len(sources)), grid_...  19.8 us
  transfers between devices with their start and end apart: 1, of which 1 were waited for; matrix products, arithmetic and copies ran while one was open for 0% of the time, Pallas kernels for 0%

profile of v4, /device:TPU:249, one launch (start us, length us, event | category | flops | bytes accessed | tf_op | source)
XLA Modules:
  0.0 528.0 jit_solution(5142333662820770833)
XLA Ops:
  0.0 1.3 fusion.wanted_ref
  1.3 1.1 dynamic-slice_reduce_fusion
  2.5 0.1 reshape.13
  2.6 0.5 broadcast_maximum_fusion.slot_ref
  3.1 0.5 compare_convert_fusion.live_ref
  3.6 0.1 reshape.14
  3.7 0.6 select_reduce_fusion.wanted_ref
  4.3 7.8 %shard_map.46.query_out_ref = bf16[64,1,512,128]{3,2,1,0:T(8,128)(2,1)} custom-call(s32[64]{0:T(128)} %select_reduce_fusion.wanted_ref, bf16[512,2048]{1,0:T(8,128)(2,1)} %bitcast.12), custom_call_target="tpu_custom_call" | custom-call | tf_op jit(solution)/shard_map/pallas_call | solution.py:44
  12.1 12.0 %shard_map.47.kv_ref = bf16[64,2,512,128]{3,2,1,0:T(8,128)(2,1)} custom-call(s32[64]{0:T(128)} %fusion.wanted_ref, bf16[512,2048]{1,0:T(8,128)(2,1)} %bitcast.8, bf16[512,2048]{1,0:T(8,128)(2,1)} %bitcast.10), custom_call_target="tpu_custom_call" | custom-call | tf_op jit(solution)/shard_map/pallas_call | solution.py:44
  24.1 417.1 %shard_map.48 = (bf16[64,512,128]{2,1,0:T(8,128)(2,1)}, f32[64,8,512]{2,1,0:T(8,128)}) custom-call(bf16[64,1,512,128]{3,2,1,0:T(8,128)(2,1)} %shard_map.46.query_out_ref, bf16[64,2,512,128]{3,2,1,0:T(8,128)(2,1)} %shard_map.47.kv_ref), custom_call_target="tpu_custom_call" | custom-call | tf_op jit(solution)/shard_map/pallas_call | solution.py:151
  441.2 33.4 %shard_map.49 = bf16[512,2048]{1,0:T(8,128)(2,1)} custom-call(s32[32]{0:T(128)} %broadcast_maximum_fusion.slot_ref, s32[32]{0:T(128)} %compare_convert_fusion.live_ref, bf16[512,2048]{1,0:T(8,128)(2,1)} %bitcast.13, bf16[512,2048]{1,0:T(8,128)(2,1)} %bitcast.9, bf16[512,2048]{1,0:T(8,128)(2,1)} %bitcast.11, ...), custom_call_target="tpu_custom_call" | custom-call | tf_op jit(solution)/shard_map/pallas_call | solution.py:236
  474.5 2.9 collective-permute-start
  477.5 49.3 %collective-permute-done = bf16[1,512,2048]{2,1,0:T(8,128)(2,1)S(1)} collective-permute-done((bf16[1,512,2048]{2,1,0:T(8,128)(2,1)}, bf16[1,512,2048]{2,1,0:T(8,128)(2,1)S(1)}, u32[]{:S(2)}, u32[]{:S(2)}) %collective-permute-start) | collective-permute-done | bytes 2097184 | tf_op jit(solution)/shard_map/ppermute | solution.py:19
  526.7 1.3 copy.6
  (1 shorter events, 0.0 us)
Async XLA Ops:
  474.5 52.2 %collective-permute-start = (bf16[1,512,2048]{2,1,0:T(8,128)(2,1)}, bf16[1,512,2048]{2,1,0:T(8,128)(2,1)S(1)}, u32[]{:S(2)}, u32[]{:S(2)}) collective-permute-start(bf16[1,512,2048]{2,1,0:T(8,128)(2,1)} %bitcast.14), channel_id=1, source_target_pairs={{0,1},{1,2},{2,3},{3,0},{4,5},{5,6},{6,7},{7,4},{8,9},{9,10},{10,1... | collective-permute-start | bytes 6291464 | tf_op jit(solution)/shard_map/ppermute | solution.py:19

commit v5 on v4

--- a/solution.py
+++ b/solution.py
@@ -10,6 +10,7 @@
 HEADS = 16
 HD = 128
 PICKS = 2
+ROUNDS = 4
 MESH = pl.DeviceIdType.MESH
 
 
@@ -93,15 +94,6 @@
             device_id={"ctx": target},
             device_id_type=MESH,
         )
-
-    def ask(owner, carry):
-        @pl.when(owner < me)
-        def _():
-            query_copy(me, owner).start()
-
-        return carry
-
-    lax.fori_loop(0, count, ask, 0)
 
     def serve(step, carry):
         asker = me + step
@@ -127,12 +119,35 @@
 
         return carry
 
-    lax.fori_loop(1, count, serve, 0)
+    for round_index in range(ROUNDS):
+        def ask(i, carry, round_index=round_index):
+            owner = i * ROUNDS + round_index
+
+            @pl.when(owner < me)
+            def _():
+                query_copy(me, owner).start()
+
+            return carry
+
+        def asked(i, carry, round_index=round_index):
+            owner = i * ROUNDS + round_index
+
+            @pl.when(owner < me)
+            def _():
+                query_copy(me, owner).wait_send()
+
+            return carry
+
+        lax.fori_loop(0, count // ROUNDS, ask, 0)
+        lax.fori_loop(0, count // ROUNDS, asked, 0)
+
+        @pl.when(lax.rem(me, ROUNDS) == round_index)
+        def _():
+            lax.fori_loop(1, count, serve, 0)
 
     def finish(peer, carry):
         @pl.when(peer < me)
         def _():
-            query_copy(me, peer).wait_send()
             part_copy(peer, me).wait_recv()
             stat_copy(peer, me).wait_recv()
 

time: 528 us -> 564 us (1.068)
  Pallas kernels: 470 us -> 509 us
    pallas_call x1, Pallas kernels: 417 us -> 456 us  [partials(): pl.pallas_call(functools.partial(partial_kernel, count), out_shape=(jax.S...]
where the time goes in v5:
time: 564 us; the launch traced here: 563 us
  Pallas kernels  509 us (90%)
  waiting for transfers between devices  47.3 us (8%)
    pallas_call x1, Pallas kernels, partials(): pl.pallas_call(functools.partial(partial_kernel, count), out_shape=(jax.S...  456 us
    ppermute x1, waiting for transfers between devices, passed_along(): return lax.ppermute(value, axis, pairs)  47.3 us
    pallas_call x1, Pallas kernels, attend(): pl.pallas_call(attend_kernel, grid_spec=grid_spec, out_shape=jax.ShapeDty...  33.4 us
    pallas_call x2, Pallas kernels, pack_heads(): pl.pallas_call(functools.partial(pack_kernel, group, len(sources)), grid_...  19.8 us
  transfers between devices with their start and end apart: 1, of which 1 were waited for; matrix products, arithmetic and copies ran while one was open for 0% of the time, Pallas kernels for 0%

profile of v5, /device:TPU:249, one launch (start us, length us, event | category | flops | bytes accessed | tf_op | source)
XLA Modules:
  0.0 563.2 jit_solution(6995220187135284382)
XLA Ops:
  0.0 1.3 fusion.wanted_ref
  1.3 1.1 dynamic-slice_reduce_fusion
  2.5 0.1 reshape.13
  2.6 0.5 broadcast_maximum_fusion.slot_ref
  3.1 0.5 compare_convert_fusion.live_ref
  3.6 0.1 reshape.14
  3.7 0.6 select_reduce_fusion.wanted_ref
  4.3 7.8 %shard_map.46.query_out_ref = bf16[64,1,512,128]{3,2,1,0:T(8,128)(2,1)} custom-call(s32[64]{0:T(128)} %select_reduce_fusion.wanted_ref, bf16[512,2048]{1,0:T(8,128)(2,1)} %bitcast.12), custom_call_target="tpu_custom_call" | custom-call | tf_op jit(solution)/shard_map/pallas_call | solution.py:45
  12.1 12.0 %shard_map.47.kv_ref = bf16[64,2,512,128]{3,2,1,0:T(8,128)(2,1)} custom-call(s32[64]{0:T(128)} %fusion.wanted_ref, bf16[512,2048]{1,0:T(8,128)(2,1)} %bitcast.8, bf16[512,2048]{1,0:T(8,128)(2,1)} %bitcast.10), custom_call_target="tpu_custom_call" | custom-call | tf_op jit(solution)/shard_map/pallas_call | solution.py:45
  24.1 456.1 %shard_map.48 = (bf16[64,512,128]{2,1,0:T(8,128)(2,1)}, f32[64,8,512]{2,1,0:T(8,128)}) custom-call(bf16[64,1,512,128]{3,2,1,0:T(8,128)(2,1)} %shard_map.46.query_out_ref, bf16[64,2,512,128]{3,2,1,0:T(8,128)(2,1)} %shard_map.47.kv_ref), custom_call_target="tpu_custom_call" | custom-call | tf_op jit(solution)/shard_map/pallas_call | solution.py:166
  480.2 33.4 %shard_map.49 = bf16[512,2048]{1,0:T(8,128)(2,1)} custom-call(s32[32]{0:T(128)} %broadcast_maximum_fusion.slot_ref, s32[32]{0:T(128)} %compare_convert_fusion.live_ref, bf16[512,2048]{1,0:T(8,128)(2,1)} %bitcast.13, bf16[512,2048]{1,0:T(8,128)(2,1)} %bitcast.9, bf16[512,2048]{1,0:T(8,128)(2,1)} %bitcast.11, ...), custom_call_target="tpu_custom_call" | custom-call | tf_op jit(solution)/shard_map/pallas_call | solution.py:251
  513.6 1.0 collective-permute-start
  514.6 47.3 %collective-permute-done = bf16[1,512,2048]{2,1,0:T(8,128)(2,1)S(1)} collective-permute-done((bf16[1,512,2048]{2,1,0:T(8,128)(2,1)}, bf16[1,512,2048]{2,1,0:T(8,128)(2,1)S(1)}, u32[]{:S(2)}, u32[]{:S(2)}) %collective-permute-start) | collective-permute-done | bytes 2097184 | tf_op jit(solution)/shard_map/ppermute | solution.py:20
  561.9 1.3 copy.6
  (1 shorter events, 0.0 us)
Async XLA Ops:
  513.6 48.3 %collective-permute-start = (bf16[1,512,2048]{2,1,0:T(8,128)(2,1)}, bf16[1,512,2048]{2,1,0:T(8,128)(2,1)S(1)}, u32[]{:S(2)}, u32[]{:S(2)}) collective-permute-start(bf16[1,512,2048]{2,1,0:T(8,128)(2,1)} %bitcast.14), channel_id=1, source_target_pairs={{0,1},{1,2},{2,3},{3,0},{4,5},{5,6},{6,7},{7,4},{8,9},{9,10},{10,1... | collective-permute-start | bytes 6291464 | tf_op jit(solution)/shard_map/ppermute | solution.py:20

commit v6 on v3

--- a/solution.py
+++ b/solution.py
@@ -48,10 +48,18 @@
     )(wanted, *sources)
 
 
-def partial_kernel(count, query_out_ref, kv_ref, part_ref, stat_ref, query_in, part_out,
-                   stat_out, query_sems, part_sems, stat_sems):
+def split_exact(value):
+    high = value.astype(jnp.bfloat16)
+    rest = value - high.astype(jnp.float32)
+    middle = rest.astype(jnp.bfloat16)
+    low = (rest - middle.astype(jnp.float32)).astype(jnp.bfloat16)
+    return [high, middle, low]
+
+
+def partial_kernel(count, query_out_ref, kv_ref, part_ref, query_in, part_out, query_sems,
+                   part_sems):
     me = lax.axis_index("ctx")
-    rows = part_ref.shape[1]
+    rows = query_in.shape[1]
     score_scale = HD ** (-0.5)
     dims = (((1,), (1,)), ((), ()))
     barrier = pltpu.get_barrier_semaphore()
@@ -84,16 +92,6 @@
             device_id_type=MESH,
         )
 
-    def stat_copy(source, target):
-        return pltpu.make_async_remote_copy(
-            src_ref=stat_out.at[target],
-            dst_ref=stat_ref.at[source],
-            send_sem=stat_sems.at[0, target],
-            recv_sem=stat_sems.at[1, source],
-            device_id={"ctx": target},
-            device_id_type=MESH,
-        )
-
     def ask(step, carry):
         owner = me - step
 
@@ -112,20 +110,20 @@
         def _():
             query_copy(asker, me).wait_recv()
             scores = lax.dot_general(
-                query_in[asker], kv_ref[asker, 0], dims, preferred_element_type=jnp.float32
+                kv_ref[asker, 0], query_in[asker], dims, preferred_element_type=jnp.float32
             ) * score_scale
-            row_top = jnp.max(scores, axis=1, keepdims=True)
+            row_top = jnp.max(scores, axis=0, keepdims=True)
             weights = jnp.exp(scores - row_top)
-            row_total = jnp.sum(weights, axis=1, keepdims=True)
-            mixed = jnp.dot(weights.astype(jnp.bfloat16), kv_ref[asker, 1],
-                            preferred_element_type=jnp.float32)
-            part_out[asker] = mixed.astype(part_out.dtype)
-            stats = jnp.concatenate(
-                [row_top, row_total, jnp.zeros((rows, 6), jnp.float32)], axis=1
+            row_total = jnp.sum(weights, axis=0, keepdims=True)
+            mixed = lax.dot_general(
+                kv_ref[asker, 1], weights.astype(jnp.bfloat16), (((0,), (0,)), ((), ())),
+                preferred_element_type=jnp.float32,
             )
-            stat_out[asker] = stats.T
+            part_out[asker, :HD, :] = mixed.astype(part_out.dtype)
+            pieces = split_exact(row_top) + split_exact(row_total)
+            pieces.append(jnp.zeros((16 - len(pieces), rows), jnp.bfloat16))
+            part_out[asker, HD:, :] = jnp.concatenate(pieces, axis=0)
             part_copy(me, asker).start()
-            stat_copy(me, asker).start()
 
         return carry
 
@@ -136,12 +134,10 @@
         def _():
             query_copy(me, peer).wait_send()
             part_copy(peer, me).wait_recv()
-            stat_copy(peer, me).wait_recv()
 
         @pl.when(peer > me)
         def _():
             part_copy(me, peer).wait_send()
-            stat_copy(me, peer).wait_send()
 
         return carry
 
@@ -152,20 +148,15 @@
     count, _, rows, _ = kv.shape
     return pl.pallas_call(
         functools.partial(partial_kernel, count),
-        out_shape=(
-            jax.ShapeDtypeStruct((count, rows, HD), kv.dtype),
-            jax.ShapeDtypeStruct((count, 8, rows), jnp.float32),
-        ),
+        out_shape=jax.ShapeDtypeStruct((count, HD + 16, rows), kv.dtype),
         in_specs=[
             pl.BlockSpec(memory_space=pl.ANY),
             pl.BlockSpec(memory_space=pltpu.VMEM),
         ],
-        out_specs=(pl.BlockSpec(memory_space=pl.ANY), pl.BlockSpec(memory_space=pl.ANY)),
+        out_specs=pl.BlockSpec(memory_space=pl.ANY),
         scratch_shapes=[
             pltpu.VMEM((count, rows, HD), kv.dtype),
-            pltpu.VMEM((count, rows, HD), kv.dtype),
-            pltpu.VMEM((count, 8, rows), jnp.float32),
-            pltpu.SemaphoreType.DMA((2, count)),
+            pltpu.VMEM((count, HD + 16, rows), kv.dtype),
             pltpu.SemaphoreType.DMA((2, count)),
             pltpu.SemaphoreType.DMA((2, count)),
         ],
@@ -175,8 +166,7 @@
     )(query_out, kv)
 
 
-def attend_kernel(slot_ref, live_ref, q_ref, k_ref, v_ref, first_ref, second_ref,
-                  first_stat_ref, second_stat_ref, o_ref):
+def attend_kernel(slot_ref, live_ref, q_ref, k_ref, v_ref, first_ref, second_ref, o_ref):
     head = pl.program_id(0)
     rows = q_ref.shape[0]
     score_scale = HD ** (-0.5)
@@ -186,17 +176,19 @@
     col_index = lax.broadcasted_iota(jnp.int32, (rows, rows), 1)
     own = jnp.where(row_index >= col_index, raw * score_scale, -jnp.inf)
 
-    def remote(live, part_ref, stat_ref):
-        stats = stat_ref[0].T
+    def remote(live, part_ref):
+        slab = part_ref[0]
+        coded = slab[HD:, :].astype(jnp.float32)
+        top_row = coded[0:1] + coded[1:2] + coded[2:3]
+        total_row = coded[3:4] + coded[4:5] + coded[5:6]
+        stats = jnp.concatenate([top_row, total_row, coded[6:12]], axis=0).T
         top = jnp.where(live, stats[:, 0:1], -jnp.inf)
         total = jnp.where(live, stats[:, 1:2], 0.0)
-        part = jnp.where(live, part_ref[0].astype(jnp.float32), 0.0)
+        part = jnp.where(live, slab[:HD, :].astype(jnp.float32).T, 0.0)
         return top, total, part
 
-    first_top, first_total, first_part = remote(live_ref[PICKS * head] > 0, first_ref,
-                                                first_stat_ref)
-    second_top, second_total, second_part = remote(live_ref[PICKS * head + 1] > 0, second_ref,
-                                                   second_stat_ref)
+    first_top, first_total, first_part = remote(live_ref[PICKS * head] > 0, first_ref)
+    second_top, second_total, second_part = remote(live_ref[PICKS * head + 1] > 0, second_ref)
     row_top = jnp.maximum(jnp.maximum(jnp.max(own, axis=1, keepdims=True), first_top),
                           second_top)
     own = jnp.exp(own - row_top)
@@ -212,7 +204,7 @@
     o_ref[...] = mixed.astype(o_ref.dtype)
 
 
-def attend(slots, live, queries, keys, values, parts, stats):
+def attend(slots, live, queries, keys, values, parts):
     rows = queries.shape[0]
     head_block = pl.BlockSpec((rows, HD), lambda h, slot_ref, live_ref: (0, h))
 
@@ -228,10 +220,8 @@
             head_block,
             head_block,
             head_block,
-            picked(0, (rows, HD)),
-            picked(1, (rows, HD)),
-            picked(0, (8, rows)),
-            picked(1, (8, rows)),
+            picked(0, (HD + 16, rows)),
+            picked(1, (HD + 16, rows)),
         ],
         out_specs=head_block,
     )
@@ -239,7 +229,7 @@
         attend_kernel,
         grid_spec=grid_spec,
         out_shape=jax.ShapeDtypeStruct(queries.shape, queries.dtype),
-    )(slots, live, queries, keys, values, parts, parts, stats, stats)
+    )(slots, live, queries, keys, values, parts, parts)
 
 
 def per_device(queries, keys, values, picks):
@@ -256,10 +246,10 @@
         axis=1,
     )
     query_out = pack_heads(wanted.astype(jnp.int32), queries[0])
-    parts, stats = partials(query_out, kv)
+    parts = partials(query_out, kv)
     live = (chosen >= 0).astype(jnp.int32)
     slots = jnp.maximum(chosen, 0).astype(jnp.int32)
-    merged = attend(slots, live, queries[0], keys[0], values[0], parts, stats)
+    merged = attend(slots, live, queries[0], keys[0], values[0], parts)
     merged = passed_along(merged[None], "pipe", 1)
     return merged
 

time: 503 us -> 499 us (level)
  no operation moved by 1% of the time
where the time goes in v6:
time: 499 us
  Pallas kernels  445 us (89%)
  waiting for transfers between devices  46.8 us (9%)
    pallas_call x1, Pallas kernels, partials(): pl.pallas_call(functools.partial(partial_kernel, count), out_shape=jax.Sh...  391 us
    ppermute x1, waiting for transfers between devices, passed_along(): return lax.ppermute(value, axis, pairs)  46.8 us
    pallas_call x1, Pallas kernels, attend(): pl.pallas_call(attend_kernel, grid_spec=grid_spec, out_shape=jax.ShapeDty...  33.9 us
    pallas_call x2, Pallas kernels, pack_heads(): pl.pallas_call(functools.partial(pack_kernel, group, len(sources)), grid_...  19.7 us
  transfers between devices with their start and end apart: 1, of which 1 were waited for; matrix products, arithmetic and copies ran while one was open for 0% of the time, Pallas kernels for 0%

profile of v6, /device:TPU:249, one launch (start us, length us, event | category | flops | bytes accessed | tf_op | source)
XLA Modules:
  0.0 499.1 jit_solution(3541374197257223700)
XLA Ops:
  0.0 1.3 fusion.wanted_ref
  1.3 1.1 dynamic-slice_reduce_fusion
  2.4 0.1 reshape.13
  2.5 0.5 broadcast_maximum_fusion.slot_ref
  3.0 0.5 compare_convert_fusion.live_ref
  3.6 0.1 reshape.14
  3.6 0.6 select_reduce_fusion.wanted_ref
  4.2 7.7 %shard_map.46.query_out_ref = bf16[64,1,512,128]{3,2,1,0:T(8,128)(2,1)} custom-call(s32[64]{0:T(128)} %select_reduce_fusion.wanted_ref, bf16[512,2048]{1,0:T(8,128)(2,1)} %bitcast.12), custom_call_target="tpu_custom_call" | custom-call | tf_op jit(solution)/shard_map/pallas_call | solution.py:44
  12.0 12.0 %shard_map.47.kv_ref = bf16[64,2,512,128]{3,2,1,0:T(8,128)(2,1)} custom-call(s32[64]{0:T(128)} %fusion.wanted_ref, bf16[512,2048]{1,0:T(8,128)(2,1)} %bitcast.8, bf16[512,2048]{1,0:T(8,128)(2,1)} %bitcast.10), custom_call_target="tpu_custom_call" | custom-call | tf_op jit(solution)/shard_map/pallas_call | solution.py:44
  24.0 391.5 %shard_map.48.first_ref.second_ref = bf16[64,144,512]{2,1,0:T(8,128)(2,1)} custom-call(bf16[64,1,512,128]{3,2,1,0:T(8,128)(2,1)} %shard_map.46.query_out_ref, bf16[64,2,512,128]{3,2,1,0:T(8,128)(2,1)} %shard_map.47.kv_ref), custom_call_target="tpu_custom_call" | custom-call | tf_op jit(solution)/shard_map/pallas_call | solution.py:149
  415.5 33.9 %shard_map.49 = bf16[512,2048]{1,0:T(8,128)(2,1)} custom-call(s32[32]{0:T(128)} %broadcast_maximum_fusion.slot_ref, s32[32]{0:T(128)} %compare_convert_fusion.live_ref, bf16[512,2048]{1,0:T(8,128)(2,1)} %bitcast.13, bf16[512,2048]{1,0:T(8,128)(2,1)} %bitcast.9, bf16[512,2048]{1,0:T(8,128)(2,1)} %bitcast.11, ...), custom_call_target="tpu_custom_call" | custom-call | tf_op jit(solution)/shard_map/pallas_call | solution.py:228
  449.4 1.5 collective-permute-start
  450.9 46.8 %collective-permute-done = bf16[1,512,2048]{2,1,0:T(8,128)(2,1)S(1)} collective-permute-done((bf16[1,512,2048]{2,1,0:T(8,128)(2,1)}, bf16[1,512,2048]{2,1,0:T(8,128)(2,1)S(1)}, u32[]{:S(2)}, u32[]{:S(2)}) %collective-permute-start) | collective-permute-done | bytes 2097184 | tf_op jit(solution)/shard_map/ppermute | solution.py:19
  497.7 1.3 copy.6
  (1 shorter events, 0.0 us)
Async XLA Ops:
  449.4 48.3 %collective-permute-start = (bf16[1,512,2048]{2,1,0:T(8,128)(2,1)}, bf16[1,512,2048]{2,1,0:T(8,128)(2,1)S(1)}, u32[]{:S(2)}, u32[]{:S(2)}) collective-permute-start(bf16[1,512,2048]{2,1,0:T(8,128)(2,1)} %bitcast.14), channel_id=1, source_target_pairs={{0,1},{1,2},{2,3},{3,0},{4,5},{5,6},{6,7},{7,4},{8,9},{9,10},{10,1... | collective-permute-start | bytes 6291464 | tf_op jit(solution)/shard_map/ppermute | solution.py:19

commit v7 on v2

--- a/solution.py
+++ b/solution.py
@@ -107,8 +107,9 @@
     )(send)
 
 
-def attend_kernel(slot_ref, live_ref, q_ref, k_ref, v_ref, first_ref, second_ref, o_ref):
-    head = pl.program_id(0)
+def attend_kernel(first_head, slot_ref, live_ref, q_ref, k_ref, v_ref, first_ref, second_ref,
+                  o_ref):
+    head = pl.program_id(0) + first_head
     rows = q_ref.shape[0]
     score_scale = HD ** (-0.5)
     dims = (((1,), (1,)), ((), ()))
@@ -145,30 +146,31 @@
     o_ref[...] = mixed.astype(o_ref.dtype)
 
 
-def attend(slots, live, queries, keys, values, received):
+def attend(first_head, heads, slots, live, queries, keys, values, received):
     rows = queries.shape[0]
-    head_block = pl.BlockSpec((rows, HD), lambda h, slot_ref, live_ref: (0, h))
+    head_block = pl.BlockSpec((rows, HD), lambda h, slot_ref, live_ref: (0, h + first_head))
+
+    def picked(j):
+        return pl.BlockSpec(
+            (1, 2, rows, HD),
+            lambda h, slot_ref, live_ref: (slot_ref[PICKS * (h + first_head) + j], 0, 0, 0),
+        )
+
     grid_spec = pltpu.PrefetchScalarGridSpec(
         num_scalar_prefetch=2,
-        grid=(HEADS,),
-        in_specs=[
-            head_block,
-            head_block,
-            head_block,
-            pl.BlockSpec(
-                (1, 2, rows, HD), lambda h, slot_ref, live_ref: (slot_ref[PICKS * h], 0, 0, 0)
-            ),
-            pl.BlockSpec(
-                (1, 2, rows, HD),
-                lambda h, slot_ref, live_ref: (slot_ref[PICKS * h + 1], 0, 0, 0),
-            ),
-        ],
-        out_specs=head_block,
-    )
+        grid=(heads,),
+        in_specs=[head_block, head_block, head_block, picked(0), picked(1)],
+        out_specs=pl.BlockSpec((rows, HD), lambda h, slot_ref, live_ref: (0, h)),
+    )
+    flops = 4 * heads * rows * 3 * rows * HD
     return pl.pallas_call(
-        attend_kernel,
+        functools.partial(attend_kernel, first_head),
         grid_spec=grid_spec,
-        out_shape=jax.ShapeDtypeStruct(queries.shape, queries.dtype),
+        out_shape=jax.ShapeDtypeStruct((rows, heads * HD), queries.dtype),
+        cost_estimate=pl.CostEstimate(
+            flops=flops, transcendentals=heads * rows * 3 * rows,
+            bytes_accessed=heads * rows * HD * 2 * 8,
+        ),
     )(slots, live, queries, keys, values, received, received)
 
 
@@ -182,9 +184,16 @@
     chosen = lax.dynamic_index_in_dim(every_pick, rank_here, 0, keepdims=False).reshape(-1)
     live = (chosen >= 0).astype(jnp.int32)
     slots = jnp.maximum(chosen, 0).astype(jnp.int32)
-    merged = attend(slots, live, queries[0], keys[0], values[0], received)
-    merged = passed_along(merged[None], "pipe", 1)
-    return merged
+    groups = 4
+    heads = HEADS // groups
+    sent = [
+        passed_along(
+            attend(g * heads, heads, slots, live, queries[0], keys[0], values[0], received)[None],
+            "pipe", 1,
+        )
+        for g in range(groups)
+    ]
+    return jnp.concatenate(sent, axis=2)
 
 
 def solution(mesh):

time: 487 us -> 465 us (0.955)
  waiting for transfers between devices: 418 us -> 384 us
  Pallas kernels: 50.9 us -> 58.6 us
    ppermute x1 -> x4, waiting for transfers between devices: 47.5 us -> 13.9 us  [passed_along(): return lax.ppermute(value, axis, pairs)]
    pallas_call x1 -> x4, Pallas kernels: 39.7 us -> 47.3 us  [attend(): pl.pallas_call(functools.partial(attend_kernel, first_head), grid_spec=gr...]
  transfers between devices with their start and end apart: 2 -> 5, of which waited for: 2 -> 3; matrix products, arithmetic and copies ran while one was open for 0% -> 0% of each run, Pallas kernels for 0% -> 8%
where the time goes in v7:
time: 465 us; the launch traced here: 464 us
  waiting for transfers between devices  384 us (83%)
  Pallas kernels  58.6 us (13%)
  starting transfers between devices  16.7 us (4%)
    all_to_all x1, waiting for transfers between devices, per_device(): lax.all_to_all(send, 'ctx', split_axis=0, concat_axis=0, tiled=True)  370 us
    pallas_call x4, Pallas kernels, attend(): pl.pallas_call(functools.partial(attend_kernel, first_head), grid_spec=gr...  47.3 us
    ppermute x4, waiting for transfers between devices, passed_along(): return lax.ppermute(value, axis, pairs)  13.9 us
    all_to_all x1, starting transfers between devices, per_device(): lax.all_to_all(send, 'ctx', split_axis=0, concat_axis=0, tiled=True)  12.1 us
    pallas_call x1, Pallas kernels, pack_requested(): pl.pallas_call(functools.partial(pack_kernel, group), grid_spec=grid_spec...  11.3 us
  transfers between devices with their start and end apart: 5, of which 3 were waited for; matrix products, arithmetic and copies ran while one was open for 0% of the time, Pallas kernels for 8%

profile of v7, /device:TPU:48, one launch (start us, length us, event | category | flops | bytes accessed | tf_op | source)
XLA Modules:
  0.0 464.4 jit_solution(2616287025868836228)
XLA Ops:
  0.0 1.3 fusion.1.asked_ref
  1.3 11.3 %shard_map.46 = bf16[64,2,512,128]{3,2,1,0:T(8,128)(2,1)} custom-call(s32[64]{0:T(128)} %fusion.1.asked_ref, bf16[512,2048]{1,0:T(8,128)(2,1)} %bitcast.11, bf16[512,2048]{1,0:T(8,128)(2,1)} %bitcast.16), custom_call_target="tpu_custom_call" | custom-call | tf_op jit(solution)/shard_map/pallas_call | solution.py:41
  12.6 0.0 copy-start
  12.6 12.1 %all-to-all-start = ((bf16[64,2,512,128]{3,2,1,0:T(8,128)(2,1)}), bf16[64,2,512,128]{3,2,1,0:T(8,128)(2,1)}, u32[]{:S(2)}, u32[]{:S(2)}) async-start(bf16[64,2,512,128]{3,2,1,0:T(8,128)(2,1)} %shard_map.46), calls=%async_computation | async-start | bytes 33554432 | tf_op jit(solution)/shard_map/all_to_all | solution.py:183
  24.7 0.0 copy-done
  24.7 0.7 fusion
  25.4 0.7 max.6.slot_ref
  26.1 0.6 reshape.12.live_ref
  26.7 370.2 %all-to-all-done.first_ref.second_ref = bf16[64,2,512,128]{3,2,1,0:T(8,128)(2,1)} async-done(((bf16[64,2,512,128]{3,2,1,0:T(8,128)(2,1)}), bf16[64,2,512,128]{3,2,1,0:T(8,128)(2,1)}, u32[]{:S(2)}, u32[]{:S(2)}) %all-to-all-start) | async-done | bytes 16777248 | tf_op jit(solution)/shard_map/all_to_all | solution.py:183
  396.9 11.8 %shard_map.47 = bf16[512,512]{1,0:T(8,128)(2,1)} custom-call(s32[32]{0:T(128)} %max.6.slot_ref, s32[32]{0:T(128)} %reshape.12.live_ref, bf16[512,2048]{1,0:T(8,128)(2,1)} %bitcast.21, bf16[512,2048]{1,0:T(8,128)(2,1)} %bitcast.12, bf16[512,2048]{1,0:T(8,128)(2,1)} %bitcast.17, bf16[64,2,512,128]{3,2,1,0:T(8,128)(2,1)} %all-to-all-done.first_ref.second_ref, ...), custom_call_target="tpu_custom_call" | custom-call | flops 1610612736 | bytes 4194304 | tf_op jit(solution)/shard_map/pallas_call | solution.py:166
  408.7 1.5 collective-permute-start
  410.2 11.8 %shard_map.48 = bf16[512,512]{1,0:T(8,128)(2,1)} custom-call(s32[32]{0:T(128)} %max.6.slot_ref, s32[32]{0:T(128)} %reshape.12.live_ref, bf16[512,2048]{1,0:T(8,128)(2,1)} %bitcast.22, bf16[512,2048]{1,0:T(8,128)(2,1)} %bitcast.13, bf16[512,2048]{1,0:T(8,128)(2,1)} %bitcast.18, bf16[64,2,512,128]{3,2,1,0:T(8,128)(2,1)} %all-to-all-done.first_ref.second_ref, ...), custom_call_target="tpu_custom_call" | custom-call | flops 1610612736 | bytes 4194304 | tf_op jit(solution)/shard_map/pallas_call | solution.py:166
  422.0 1.5 collective-permute-start.1
  423.6 11.8 %shard_map.49 = bf16[512,512]{1,0:T(8,128)(2,1)} custom-call(s32[32]{0:T(128)} %max.6.slot_ref, s32[32]{0:T(128)} %reshape.12.live_ref, bf16[512,2048]{1,0:T(8,128)(2,1)} %bitcast.23, bf16[512,2048]{1,0:T(8,128)(2,1)} %bitcast.14, bf16[512,2048]{1,0:T(8,128)(2,1)} %bitcast.19, bf16[64,2,512,128]{3,2,1,0:T(8,128)(2,1)} %all-to-all-done.first_ref.second_ref, ...), custom_call_target="tpu_custom_call" | custom-call | flops 1610612736 | bytes 4194304 | tf_op jit(solution)/shard_map/pallas_call | solution.py:166
  435.4 1.2 collective-permute-start.2
  436.6 11.8 %shard_map.50 = bf16[512,512]{1,0:T(8,128)(2,1)} custom-call(s32[32]{0:T(128)} %max.6.slot_ref, s32[32]{0:T(128)} %reshape.12.live_ref, bf16[512,2048]{1,0:T(8,128)(2,1)} %bitcast.24, bf16[512,2048]{1,0:T(8,128)(2,1)} %bitcast.15, bf16[512,2048]{1,0:T(8,128)(2,1)} %bitcast.20, bf16[64,2,512,128]{3,2,1,0:T(8,128)(2,1)} %all-to-all-done.first_ref.second_ref, ...), custom_call_target="tpu_custom_call" | custom-call | flops 1610612736 | bytes 4194304 | tf_op jit(solution)/shard_map/pallas_call | solution.py:166
  448.4 0.5 collective-permute-start.3
  448.8 0.0 collective-permute-done
  448.8 0.0 collective-permute-done.1
  448.8 1.2 collective-permute-done.2
  450.0 12.7 %collective-permute-done.3 = bf16[1,512,512]{2,1,0:T(8,128)(2,1)S(1)} collective-permute-done((bf16[1,512,512]{2,1,0:T(8,128)(2,1)}, bf16[1,512,512]{2,1,0:T(8,128)(2,1)S(1)}, u32[]{:S(2)}, u32[]{:S(2)}) %collective-permute-start.3) | collective-permute-done | bytes 524320 | tf_op jit(solution)/shard_map/ppermute | solution.py:19
  462.7 1.6 pad_maximum_fusion
Async XLA Ops:
  12.6 12.1 %copy-start = (s32[1,64,16,2]{1,3,2,0:T(2,128)S(1)}, s32[1,64,16,2]{1,3,2,0:T(2,128)}, u32[]{:S(2)}) copy-start(s32[1,64,16,2]{1,3,2,0:T(2,128)} %param.7) | copy-start | bytes 24580
  12.6 384.3 %all-to-all-start = ((bf16[64,2,512,128]{3,2,1,0:T(8,128)(2,1)}), bf16[64,2,512,128]{3,2,1,0:T(8,128)(2,1)}, u32[]{:S(2)}, u32[]{:S(2)}) async-start(bf16[64,2,512,128]{3,2,1,0:T(8,128)(2,1)} %shard_map.46), calls=%async_computation | async-start | bytes 33554432 | tf_op jit(solution)/shard_map/all_to_all | solution.py:183
  408.7 40.1 %collective-permute-start = (bf16[1,512,512]{2,1,0:T(8,128)(2,1)}, bf16[1,512,512]{2,1,0:T(8,128)(2,1)S(1)}, u32[]{:S(2)}, u32[]{:S(2)}) collective-permute-start(bf16[1,512,512]{2,1,0:T(8,128)(2,1)} %bitcast.25), channel_id=1, source_target_pairs={{0,1},{1,2},{2,3},{3,0},{4,5},{5,6},{6,7},{7,4},{8,9},{9,10},{10,1... | collective-permute-start | bytes 1572872 | tf_op jit(solution)/shard_map/ppermute | solution.py:19
  422.0 26.8 %collective-permute-start.1 = (bf16[1,512,512]{2,1,0:T(8,128)(2,1)}, bf16[1,512,512]{2,1,0:T(8,128)(2,1)S(1)}, u32[]{:S(2)}, u32[]{:S(2)}) collective-permute-start(bf16[1,512,512]{2,1,0:T(8,128)(2,1)} %bitcast.26), channel_id=1, source_target_pairs={{0,1},{1,2},{2,3},{3,0},{4,5},{5,6},{6,7},{7,4},{8,9},{9,10},{10,1... | collective-permute-start | bytes 1572872 | tf_op jit(solution)/shard_map/ppermute | solution.py:19
  435.4 14.7 %collective-permute-start.2 = (bf16[1,512,512]{2,1,0:T(8,128)(2,1)}, bf16[1,512,512]{2,1,0:T(8,128)(2,1)S(1)}, u32[]{:S(2)}, u32[]{:S(2)}) collective-permute-start(bf16[1,512,512]{2,1,0:T(8,128)(2,1)} %bitcast.27), channel_id=1, source_target_pairs={{0,1},{1,2},{2,3},{3,0},{4,5},{5,6},{6,7},{7,4},{8,9},{9,10},{10,1... | collective-permute-start | bytes 1572872 | tf_op jit(solution)/shard_map/ppermute | solution.py:19
  448.4 14.4 %collective-permute-start.3 = (bf16[1,512,512]{2,1,0:T(8,128)(2,1)}, bf16[1,512,512]{2,1,0:T(8,128)(2,1)S(1)}, u32[]{:S(2)}, u32[]{:S(2)}) collective-permute-start(bf16[1,512,512]{2,1,0:T(8,128)(2,1)} %bitcast.28), channel_id=1, source_target_pairs={{0,1},{1,2},{2,3},{3,0},{4,5},{5,6},{6,7},{7,4},{8,9},{9,10},{10,1... | collective-permute-start | bytes 1572872 | tf_op jit(solution)/shard_map/ppermute | solution.py:19

commit v8 on v7

--- a/solution.py
+++ b/solution.py
@@ -107,38 +107,72 @@
     )(send)
 
 
-def attend_kernel(first_head, slot_ref, live_ref, q_ref, k_ref, v_ref, first_ref, second_ref,
-                  o_ref):
-    head = pl.program_id(0) + first_head
+def own_kernel(q_ref, k_ref, v_ref, part_ref, stat_ref):
     rows = q_ref.shape[0]
     score_scale = HD ** (-0.5)
     dims = (((1,), (1,)), ((), ()))
+    raw = lax.dot_general(q_ref[...], k_ref[...], dims, preferred_element_type=jnp.float32)
+    row_index = lax.broadcasted_iota(jnp.int32, (rows, rows), 0)
+    col_index = lax.broadcasted_iota(jnp.int32, (rows, rows), 1)
+    own = jnp.where(row_index >= col_index, raw * score_scale, -jnp.inf)
+    row_top = jnp.max(own, axis=1, keepdims=True)
+    weights = jnp.exp(own - row_top)
+    row_total = jnp.sum(weights, axis=1, keepdims=True)
+    part_ref[...] = jnp.dot(weights, v_ref[...].astype(jnp.float32),
+                            precision=lax.Precision.HIGHEST, preferred_element_type=jnp.float32)
+    lane = lax.broadcasted_iota(jnp.int32, (rows, HD), 1)
+    stat_ref[...] = jnp.where(lane == 0, row_top, jnp.where(lane == 1, row_total, 0.0))
+
+
+def own_attention(queries, keys, values):
+    rows = queries.shape[0]
+    head_block = pl.BlockSpec((rows, HD), lambda h: (0, h))
+    return pl.pallas_call(
+        own_kernel,
+        grid=(HEADS,),
+        in_specs=[head_block, head_block, head_block],
+        out_specs=(head_block, head_block),
+        out_shape=(
+            jax.ShapeDtypeStruct(queries.shape, jnp.float32),
+            jax.ShapeDtypeStruct(queries.shape, jnp.float32),
+        ),
+        cost_estimate=pl.CostEstimate(
+            flops=4 * HEADS * rows * rows * HD, transcendentals=HEADS * rows * rows,
+            bytes_accessed=HEADS * rows * HD * 22,
+        ),
+    )(queries, keys, values)
+
+
+def attend_kernel(first_head, slot_ref, live_ref, q_ref, own_part_ref, own_stat_ref, first_ref,
+                  second_ref, o_ref):
+    head = pl.program_id(0) + first_head
+    score_scale = HD ** (-0.5)
+    dims = (((1,), (1,)), ((), ()))
     query = q_ref[...]
 
     def scores_against(key_rows):
         raw = lax.dot_general(query, key_rows, dims, preferred_element_type=jnp.float32)
         return raw * score_scale
 
-    row_index = lax.broadcasted_iota(jnp.int32, (rows, rows), 0)
-    col_index = lax.broadcasted_iota(jnp.int32, (rows, rows), 1)
-    own = jnp.where(row_index >= col_index, scores_against(k_ref[...]), -jnp.inf)
     live_first = live_ref[PICKS * head] > 0
     live_second = live_ref[PICKS * head + 1] > 0
     first = jnp.where(live_first, scores_against(first_ref[0, 0]), -jnp.inf)
     second = jnp.where(live_second, scores_against(second_ref[0, 0]), -jnp.inf)
+    own_top = own_stat_ref[:, 0:1]
     row_top = jnp.maximum(
-        jnp.maximum(jnp.max(own, axis=1), jnp.max(first, axis=1)), jnp.max(second, axis=1)
-    )[:, None]
-    own = jnp.exp(own - row_top)
+        jnp.maximum(own_top, jnp.max(first, axis=1, keepdims=True)),
+        jnp.max(second, axis=1, keepdims=True),
+    )
+    own_scale = jnp.exp(own_top - row_top)
     first = jnp.exp(first - row_top)
     second = jnp.exp(second - row_top)
     row_scale = 1.0 / (
-        jnp.sum(own, axis=1) + jnp.sum(first, axis=1) + jnp.sum(second, axis=1)
-    )[:, None]
+        own_scale * own_stat_ref[:, 1:2] + jnp.sum(first, axis=1, keepdims=True)
+        + jnp.sum(second, axis=1, keepdims=True)
+    )
     first_values = jnp.where(live_first, first_ref[0, 1], jnp.zeros_like(first_ref[0, 1]))
     second_values = jnp.where(live_second, second_ref[0, 1], jnp.zeros_like(second_ref[0, 1]))
-    mixed = jnp.dot((own * row_scale).astype(jnp.bfloat16), v_ref[...],
-                    preferred_element_type=jnp.float32)
+    mixed = (own_scale * row_scale) * own_part_ref[...]
     mixed += jnp.dot((first * row_scale).astype(jnp.bfloat16), first_values,
                      preferred_element_type=jnp.float32)
     mixed += jnp.dot((second * row_scale).astype(jnp.bfloat16), second_values,
@@ -146,7 +180,7 @@
     o_ref[...] = mixed.astype(o_ref.dtype)
 
 
-def attend(first_head, heads, slots, live, queries, keys, values, received):
+def attend(first_head, heads, slots, live, queries, own_part, own_stat, received):
     rows = queries.shape[0]
     head_block = pl.BlockSpec((rows, HD), lambda h, slot_ref, live_ref: (0, h + first_head))
 
@@ -162,16 +196,16 @@
         in_specs=[head_block, head_block, head_block, picked(0), picked(1)],
         out_specs=pl.BlockSpec((rows, HD), lambda h, slot_ref, live_ref: (0, h)),
     )
-    flops = 4 * heads * rows * 3 * rows * HD
+    flops = 4 * heads * rows * 2 * rows * HD
     return pl.pallas_call(
         functools.partial(attend_kernel, first_head),
         grid_spec=grid_spec,
         out_shape=jax.ShapeDtypeStruct((rows, heads * HD), queries.dtype),
         cost_estimate=pl.CostEstimate(
-            flops=flops, transcendentals=heads * rows * 3 * rows,
+            flops=flops, transcendentals=heads * rows * 2 * rows,
             bytes_accessed=heads * rows * HD * 2 * 8,
         ),
-    )(slots, live, queries, keys, values, received, received)
+    )(slots, live, queries, own_part, own_stat, received, received)
 
 
 def per_device(queries, keys, values, picks):
@@ -184,11 +218,12 @@
     chosen = lax.dynamic_index_in_dim(every_pick, rank_here, 0, keepdims=False).reshape(-1)
     live = (chosen >= 0).astype(jnp.int32)
     slots = jnp.maximum(chosen, 0).astype(jnp.int32)
+    own_part, own_stat = own_attention(queries[0], keys[0], values[0])
     groups = 4
     heads = HEADS // groups
     sent = [
         passed_along(
-            attend(g * heads, heads, slots, live, queries[0], keys[0], values[0], received)[None],
+            attend(g * heads, heads, slots, live, queries[0], own_part, own_stat, received)[None],
             "pipe", 1,
         )
         for g in range(groups)

time: 465 us -> 491 us (1.056)
  Pallas kernels: 58.6 us -> 110 us
  waiting for transfers between devices: 384 us -> 358 us
    all_to_all x1, waiting for transfers between devices: 370 us -> 344 us  [per_device(): lax.all_to_all(send, 'ctx', split_axis=0, concat_axis=0, tiled=True)]
    pallas_call x0 -> x1, Pallas kernels: none -> 26.1 us  [own_attention(): pl.pallas_call(own_kernel, grid=(HEADS,), in_specs=[head_block, head_bloc...]
    pallas_call x4, Pallas kernels: 47.3 us -> 72.8 us  [attend(): pl.pallas_call(functools.partial(attend_kernel, first_head), grid_spec=gr...]
  transfers between devices with their start and end apart: 5 -> 5, of which waited for: 3 -> 2; matrix products, arithmetic and copies ran while one was open for 0% -> 0% of each run, Pallas kernels for 8% -> 16%
where the time goes in v8:
time: 491 us; the launch traced here: 490 us
  waiting for transfers between devices  358 us (73%)
  Pallas kernels  110 us (22%)
  starting transfers between devices  17.2 us (4%)
    all_to_all x1, waiting for transfers between devices, per_device(): lax.all_to_all(send, 'ctx', split_axis=0, concat_axis=0, tiled=True)  344 us
    pallas_call x4, Pallas kernels, attend(): pl.pallas_call(functools.partial(attend_kernel, first_head), grid_spec=gr...  72.8 us
    pallas_call x1, Pallas kernels, own_attention(): pl.pallas_call(own_kernel, grid=(HEADS,), in_specs=[head_block, head_bloc...  26.1 us
    ppermute x4, waiting for transfers between devices, passed_along(): return lax.ppermute(value, axis, pairs)  13.9 us
    all_to_all x1, starting transfers between devices, per_device(): lax.all_to_all(send, 'ctx', split_axis=0, concat_axis=0, tiled=True)  12.4 us
    pallas_call x1, Pallas kernels, pack_requested(): pl.pallas_call(functools.partial(pack_kernel, group), grid_spec=grid_spec...  11.3 us
  transfers between devices with their start and end apart: 5, of which 2 were waited for; matrix products, arithmetic and copies ran while one was open for 0% of the time, Pallas kernels for 16%

profile of v8, /device:TPU:48, one launch (start us, length us, event | category | flops | bytes accessed | tf_op | source)
XLA Modules:
  0.0 490.3 jit_solution(12572368018081743935)
XLA Ops:
  0.0 1.3 fusion.1.asked_ref
  1.3 11.3 %shard_map.47 = bf16[64,2,512,128]{3,2,1,0:T(8,128)(2,1)} custom-call(s32[64]{0:T(128)} %fusion.1.asked_ref, bf16[512,2048]{1,0:T(8,128)(2,1)} %bitcast.16, bf16[512,2048]{1,0:T(8,128)(2,1)} %bitcast.18), custom_call_target="tpu_custom_call" | custom-call | tf_op jit(solution)/shard_map/pallas_call | solution.py:41
  12.5 0.0 copy-start
  12.5 12.4 %all-to-all-start = ((bf16[64,2,512,128]{3,2,1,0:T(8,128)(2,1)}), bf16[64,2,512,128]{3,2,1,0:T(8,128)(2,1)}, u32[]{:S(2)}, u32[]{:S(2)}) async-start(bf16[64,2,512,128]{3,2,1,0:T(8,128)(2,1)} %shard_map.47), calls=%async_computation | async-start | bytes 33554432 | tf_op jit(solution)/shard_map/all_to_all | solution.py:217
  25.0 0.0 copy-done
  25.0 0.7 fusion
  25.7 0.7 reshape.12.live_ref
  26.3 0.7 max.6.slot_ref
  27.0 26.1 %shard_map.46 = (f32[512,2048]{1,0:T(8,128)}, f32[512,2048]{1,0:T(8,128)}) custom-call(bf16[512,2048]{1,0:T(8,128)(2,1)} %bitcast.11, bf16[512,2048]{1,0:T(8,128)(2,1)} %bitcast.17, bf16[512,2048]{1,0:T(8,128)(2,1)} %bitcast.19), custom_call_target="tpu_custom_call" | custom-call | flops 2147483648 | bytes 23068672 | tf_op jit(solution)/shard_map/pallas_call | solution.py:130
  53.1 344.0 %all-to-all-done.first_ref.second_ref = bf16[64,2,512,128]{3,2,1,0:T(8,128)(2,1)} async-done(((bf16[64,2,512,128]{3,2,1,0:T(8,128)(2,1)}), bf16[64,2,512,128]{3,2,1,0:T(8,128)(2,1)}, u32[]{:S(2)}, u32[]{:S(2)}) %all-to-all-start) | async-done | bytes 16777248 | tf_op jit(solution)/shard_map/all_to_all | solution.py:217
  397.1 18.2 %shard_map.49 = bf16[512,512]{1,0:T(8,128)(2,1)} custom-call(s32[32]{0:T(128)} %max.6.slot_ref, s32[32]{0:T(128)} %reshape.12.live_ref, bf16[512,2048]{1,0:T(8,128)(2,1)} %bitcast.12, f32[512,2048]{1,0:T(8,128)} %get-tuple-element.7.own_part_ref, f32[512,2048]{1,0:T(8,128)} %get-tuple-element.8.own_stat_ref, ...), custom_call_target="tpu_custom_call" | custom-call | flops 1073741824 | bytes 4194304 | tf_op jit(solution)/shard_map/pallas_call | solution.py:200
  415.3 1.5 collective-permute-start.1
  416.9 18.2 %shard_map.48 = bf16[512,512]{1,0:T(8,128)(2,1)} custom-call(s32[32]{0:T(128)} %max.6.slot_ref, s32[32]{0:T(128)} %reshape.12.live_ref, bf16[512,2048]{1,0:T(8,128)(2,1)} %bitcast.13, f32[512,2048]{1,0:T(8,128)} %get-tuple-element.7.own_part_ref, f32[512,2048]{1,0:T(8,128)} %get-tuple-element.8.own_stat_ref, ...), custom_call_target="tpu_custom_call" | custom-call | flops 1073741824 | bytes 4194304 | tf_op jit(solution)/shard_map/pallas_call | solution.py:200
  435.1 1.5 collective-permute-start
  436.6 18.2 %shard_map.50 = bf16[512,512]{1,0:T(8,128)(2,1)} custom-call(s32[32]{0:T(128)} %max.6.slot_ref, s32[32]{0:T(128)} %reshape.12.live_ref, bf16[512,2048]{1,0:T(8,128)(2,1)} %bitcast.14, f32[512,2048]{1,0:T(8,128)} %get-tuple-element.7.own_part_ref, f32[512,2048]{1,0:T(8,128)} %get-tuple-element.8.own_stat_ref, ...), custom_call_target="tpu_custom_call" | custom-call | flops 1073741824 | bytes 4194304 | tf_op jit(solution)/shard_map/pallas_call | solution.py:200
  454.7 1.5 collective-permute-start.2
  456.3 18.3 %shard_map.51 = bf16[512,512]{1,0:T(8,128)(2,1)} custom-call(s32[32]{0:T(128)} %max.6.slot_ref, s32[32]{0:T(128)} %reshape.12.live_ref, bf16[512,2048]{1,0:T(8,128)(2,1)} %bitcast.15, f32[512,2048]{1,0:T(8,128)} %get-tuple-element.7.own_part_ref, f32[512,2048]{1,0:T(8,128)} %get-tuple-element.8.own_stat_ref, ...), custom_call_target="tpu_custom_call" | custom-call | flops 1073741824 | bytes 4194304 | tf_op jit(solution)/shard_map/pallas_call | solution.py:200
  474.6 0.2 collective-permute-start.3
  474.8 0.0 collective-permute-done.1
  474.8 0.0 collective-permute-done
  474.8 0.0 collective-permute-done.2
  474.8 13.9 %collective-permute-done.3 = bf16[1,512,512]{2,1,0:T(8,128)(2,1)S(1)} collective-permute-done((bf16[1,512,512]{2,1,0:T(8,128)(2,1)}, bf16[1,512,512]{2,1,0:T(8,128)(2,1)S(1)}, u32[]{:S(2)}, u32[]{:S(2)}) %collective-permute-start.3) | collective-permute-done | bytes 524320 | tf_op jit(solution)/shard_map/ppermute | solution.py:19
  488.7 1.6 pad_maximum_fusion
Async XLA Ops:
  12.5 12.4 %copy-start = (s32[1,64,16,2]{1,3,2,0:T(2,128)S(1)}, s32[1,64,16,2]{1,3,2,0:T(2,128)}, u32[]{:S(2)}) copy-start(s32[1,64,16,2]{1,3,2,0:T(2,128)} %param.7) | copy-start | bytes 24580
  12.5 384.6 %all-to-all-start = ((bf16[64,2,512,128]{3,2,1,0:T(8,128)(2,1)}), bf16[64,2,512,128]{3,2,1,0:T(8,128)(2,1)}, u32[]{:S(2)}, u32[]{:S(2)}) async-start(bf16[64,2,512,128]{3,2,1,0:T(8,128)(2,1)} %shard_map.47), calls=%async_computation | async-start | bytes 33554432 | tf_op jit(solution)/shard_map/all_to_all | solution.py:217
  415.3 59.5 %collective-permute-start.1 = (bf16[1,512,512]{2,1,0:T(8,128)(2,1)}, bf16[1,512,512]{2,1,0:T(8,128)(2,1)S(1)}, u32[]{:S(2)}, u32[]{:S(2)}) collective-permute-start(bf16[1,512,512]{2,1,0:T(8,128)(2,1)} %bitcast.20), channel_id=1, source_target_pairs={{0,1},{1,2},{2,3},{3,0},{4,5},{5,6},{6,7},{7,4},{8,9},{9,10},{10,1... | collective-permute-start | bytes 1572872 | tf_op jit(solution)/shard_map/ppermute | solution.py:19
  435.1 39.7 %collective-permute-start = (bf16[1,512,512]{2,1,0:T(8,128)(2,1)}, bf16[1,512,512]{2,1,0:T(8,128)(2,1)S(1)}, u32[]{:S(2)}, u32[]{:S(2)}) collective-permute-start(bf16[1,512,512]{2,1,0:T(8,128)(2,1)} %bitcast.21), channel_id=1, source_target_pairs={{0,1},{1,2},{2,3},{3,0},{4,5},{5,6},{6,7},{7,4},{8,9},{9,10},{10,1... | collective-permute-start | bytes 1572872 | tf_op jit(solution)/shard_map/ppermute | solution.py:19
  454.7 20.0 %collective-permute-start.2 = (bf16[1,512,512]{2,1,0:T(8,128)(2,1)}, bf16[1,512,512]{2,1,0:T(8,128)(2,1)S(1)}, u32[]{:S(2)}, u32[]{:S(2)}) collective-permute-start(bf16[1,512,512]{2,1,0:T(8,128)(2,1)} %bitcast.22), channel_id=1, source_target_pairs={{0,1},{1,2},{2,3},{3,0},{4,5},{5,6},{6,7},{7,4},{8,9},{9,10},{10,1... | collective-permute-start | bytes 1572872 | tf_op jit(solution)/shard_map/ppermute | solution.py:19
  474.6 14.1 %collective-permute-start.3 = (bf16[1,512,512]{2,1,0:T(8,128)(2,1)}, bf16[1,512,512]{2,1,0:T(8,128)(2,1)S(1)}, u32[]{:S(2)}, u32[]{:S(2)}) collective-permute-start(bf16[1,512,512]{2,1,0:T(8,128)(2,1)} %bitcast.23), channel_id=1, source_target_pairs={{0,1},{1,2},{2,3},{3,0},{4,5},{5,6},{6,7},{7,4},{8,9},{9,10},{10,1... | collective-permute-start | bytes 1572872 | tf_op jit(solution)/shard_map/ppermute | solution.py:19

commit v9 on v7

--- a/solution.py
+++ b/solution.py
@@ -122,10 +122,10 @@
     row_index = lax.broadcasted_iota(jnp.int32, (rows, rows), 0)
     col_index = lax.broadcasted_iota(jnp.int32, (rows, rows), 1)
     own = jnp.where(row_index >= col_index, scores_against(k_ref[...]), -jnp.inf)
-    live_first = live_ref[PICKS * head] > 0
-    live_second = live_ref[PICKS * head + 1] > 0
-    first = jnp.where(live_first, scores_against(first_ref[0, 0]), -jnp.inf)
-    second = jnp.where(live_second, scores_against(second_ref[0, 0]), -jnp.inf)
+    first_bias = jnp.where(live_ref[PICKS * head] > 0, 0.0, -jnp.inf)
+    second_bias = jnp.where(live_ref[PICKS * head + 1] > 0, 0.0, -jnp.inf)
+    first = scores_against(first_ref[0, 0]) + first_bias
+    second = scores_against(second_ref[0, 0]) + second_bias
     row_top = jnp.maximum(
         jnp.maximum(jnp.max(own, axis=1), jnp.max(first, axis=1)), jnp.max(second, axis=1)
     )[:, None]
@@ -135,13 +135,11 @@
     row_scale = 1.0 / (
         jnp.sum(own, axis=1) + jnp.sum(first, axis=1) + jnp.sum(second, axis=1)
     )[:, None]
-    first_values = jnp.where(live_first, first_ref[0, 1], jnp.zeros_like(first_ref[0, 1]))
-    second_values = jnp.where(live_second, second_ref[0, 1], jnp.zeros_like(second_ref[0, 1]))
     mixed = jnp.dot((own * row_scale).astype(jnp.bfloat16), v_ref[...],
                     preferred_element_type=jnp.float32)
-    mixed += jnp.dot((first * row_scale).astype(jnp.bfloat16), first_values,
+    mixed += jnp.dot((first * row_scale).astype(jnp.bfloat16), first_ref[0, 1],
                      preferred_element_type=jnp.float32)
-    mixed += jnp.dot((second * row_scale).astype(jnp.bfloat16), second_values,
+    mixed += jnp.dot((second * row_scale).astype(jnp.bfloat16), second_ref[0, 1],
                      preferred_element_type=jnp.float32)
     o_ref[...] = mixed.astype(o_ref.dtype)
 
@@ -184,14 +182,14 @@
     chosen = lax.dynamic_index_in_dim(every_pick, rank_here, 0, keepdims=False).reshape(-1)
     live = (chosen >= 0).astype(jnp.int32)
     slots = jnp.maximum(chosen, 0).astype(jnp.int32)
-    groups = 4
-    heads = HEADS // groups
+    sizes = (2, 4, 4, 4, 2)
+    starts = [sum(sizes[:g]) for g in range(len(sizes))]
     sent = [
         passed_along(
-            attend(g * heads, heads, slots, live, queries[0], keys[0], values[0], received)[None],
+            attend(first, heads, slots, live, queries[0], keys[0], values[0], received)[None],
             "pipe", 1,
         )
-        for g in range(groups)
+        for first, heads in zip(starts, sizes)
     ]
     return jnp.concatenate(sent, axis=2)
 

time: 465 us -> 465 us (level)
    ppermute x4 -> x5, waiting for transfers between devices: 13.9 us -> 10.6 us  [passed_along(): return lax.ppermute(value, axis, pairs)]
    pallas_call x4 -> x5, Pallas kernels: 47.3 us -> 49.5 us  [attend(): pl.pallas_call(functools.partial(attend_kernel, first_head), grid_spec=gr...]
  transfers between devices with their start and end apart: 5 -> 6, of which waited for: 3 -> 3; matrix products, arithmetic and copies ran while one was open for 0% -> 0% of each run, Pallas kernels for 8% -> 9%
where the time goes in v9:
time: 465 us; the launch traced here: 464 us
  waiting for transfers between devices  381 us (82%)
  Pallas kernels  60.8 us (13%)
  starting transfers between devices  18.6 us (4%)
    all_to_all x1, waiting for transfers between devices, per_device(): lax.all_to_all(send, 'ctx', split_axis=0, concat_axis=0, tiled=True)  370 us
    pallas_call x5, Pallas kernels, attend(): pl.pallas_call(functools.partial(attend_kernel, first_head), grid_spec=gr...  49.5 us
    all_to_all x1, starting transfers between devices, per_device(): lax.all_to_all(send, 'ctx', split_axis=0, concat_axis=0, tiled=True)  12.4 us
    pallas_call x1, Pallas kernels, pack_requested(): pl.pallas_call(functools.partial(pack_kernel, group), grid_spec=grid_spec...  11.3 us
    ppermute x5, waiting for transfers between devices, passed_along(): return lax.ppermute(value, axis, pairs)  10.6 us
  transfers between devices with their start and end apart: 6, of which 3 were waited for; matrix products, arithmetic and copies ran while one was open for 0% of the time, Pallas kernels for 9%

profile of v9, /device:TPU:48, one launch (start us, length us, event | category | flops | bytes accessed | tf_op | source)
XLA Modules:
  0.0 464.4 jit_solution(7718479377189805707)
XLA Ops:
  0.0 1.3 fusion.1.asked_ref
  1.3 11.3 %shard_map.46 = bf16[64,2,512,128]{3,2,1,0:T(8,128)(2,1)} custom-call(s32[64]{0:T(128)} %fusion.1.asked_ref, bf16[512,2048]{1,0:T(8,128)(2,1)} %bitcast.12, bf16[512,2048]{1,0:T(8,128)(2,1)} %bitcast.18), custom_call_target="tpu_custom_call" | custom-call | tf_op jit(solution)/shard_map/pallas_call | solution.py:41
  12.5 0.0 copy-start
  12.5 12.4 %all-to-all-start = ((bf16[64,2,512,128]{3,2,1,0:T(8,128)(2,1)}), bf16[64,2,512,128]{3,2,1,0:T(8,128)(2,1)}, u32[]{:S(2)}, u32[]{:S(2)}) async-start(bf16[64,2,512,128]{3,2,1,0:T(8,128)(2,1)} %shard_map.46), calls=%async_computation | async-start | bytes 33554432 | tf_op jit(solution)/shard_map/all_to_all | solution.py:181
  25.0 0.0 copy-done
  25.0 0.7 fusion
  25.7 0.7 max.6.slot_ref
  26.4 0.7 reshape.12.live_ref
  27.0 370.1 %all-to-all-done.first_ref.second_ref = bf16[64,2,512,128]{3,2,1,0:T(8,128)(2,1)} async-done(((bf16[64,2,512,128]{3,2,1,0:T(8,128)(2,1)}), bf16[64,2,512,128]{3,2,1,0:T(8,128)(2,1)}, u32[]{:S(2)}, u32[]{:S(2)}) %all-to-all-start) | async-done | bytes 16777248 | tf_op jit(solution)/shard_map/all_to_all | solution.py:181
  397.2 7.1 %shard_map.47 = bf16[512,256]{1,0:T(8,128)(2,1)} custom-call(s32[32]{0:T(128)} %max.6.slot_ref, s32[32]{0:T(128)} %reshape.12.live_ref, bf16[512,2048]{1,0:T(8,128)(2,1)} %bitcast.24, bf16[512,2048]{1,0:T(8,128)(2,1)} %bitcast.13, bf16[512,2048]{1,0:T(8,128)(2,1)} %bitcast.19, bf16[64,2,512,128]{3,2,1,0:T(8,128)(2,1)} %all-to-all-done.first_ref.second_ref, ...), custom_call_target="tpu_custom_call" | custom-call | flops 805306368 | bytes 2097152 | tf_op jit(solution)/shard_map/pallas_call | solution.py:164
  404.3 1.5 collective-permute-start
  405.8 11.7 %shard_map.48 = bf16[512,512]{1,0:T(8,128)(2,1)} custom-call(s32[32]{0:T(128)} %max.6.slot_ref, s32[32]{0:T(128)} %reshape.12.live_ref, bf16[512,2048]{1,0:T(8,128)(2,1)} %bitcast.25, bf16[512,2048]{1,0:T(8,128)(2,1)} %bitcast.14, bf16[512,2048]{1,0:T(8,128)(2,1)} %bitcast.20, bf16[64,2,512,128]{3,2,1,0:T(8,128)(2,1)} %all-to-all-done.first_ref.second_ref, ...), custom_call_target="tpu_custom_call" | custom-call | flops 1610612736 | bytes 4194304 | tf_op jit(solution)/shard_map/pallas_call | solution.py:164
  417.5 1.6 collective-permute-start.1
  419.1 11.7 %shard_map.49 = bf16[512,512]{1,0:T(8,128)(2,1)} custom-call(s32[32]{0:T(128)} %max.6.slot_ref, s32[32]{0:T(128)} %reshape.12.live_ref, bf16[512,2048]{1,0:T(8,128)(2,1)} %bitcast.26, bf16[512,2048]{1,0:T(8,128)(2,1)} %bitcast.15, bf16[512,2048]{1,0:T(8,128)(2,1)} %bitcast.21, bf16[64,2,512,128]{3,2,1,0:T(8,128)(2,1)} %all-to-all-done.first_ref.second_ref, ...), custom_call_target="tpu_custom_call" | custom-call | flops 1610612736 | bytes 4194304 | tf_op jit(solution)/shard_map/pallas_call | solution.py:164
  430.8 1.2 collective-permute-start.2
  432.0 11.7 %shard_map.50 = bf16[512,512]{1,0:T(8,128)(2,1)} custom-call(s32[32]{0:T(128)} %max.6.slot_ref, s32[32]{0:T(128)} %reshape.12.live_ref, bf16[512,2048]{1,0:T(8,128)(2,1)} %bitcast.27, bf16[512,2048]{1,0:T(8,128)(2,1)} %bitcast.16, bf16[512,2048]{1,0:T(8,128)(2,1)} %bitcast.22, bf16[64,2,512,128]{3,2,1,0:T(8,128)(2,1)} %all-to-all-done.first_ref.second_ref, ...), custom_call_target="tpu_custom_call" | custom-call | flops 1610612736 | bytes 4194304 | tf_op jit(solution)/shard_map/pallas_call | solution.py:164
  443.7 0.5 collective-permute-start.3
  444.2 7.2 %shard_map.51 = bf16[512,256]{1,0:T(8,128)(2,1)} custom-call(s32[32]{0:T(128)} %max.6.slot_ref, s32[32]{0:T(128)} %reshape.12.live_ref, bf16[512,2048]{1,0:T(8,128)(2,1)} %bitcast.28, bf16[512,2048]{1,0:T(8,128)(2,1)} %bitcast.17, bf16[512,2048]{1,0:T(8,128)(2,1)} %bitcast.23, bf16[64,2,512,128]{3,2,1,0:T(8,128)(2,1)} %all-to-all-done.first_ref.second_ref, ...), custom_call_target="tpu_custom_call" | custom-call | flops 805306368 | bytes 2097152 | tf_op jit(solution)/shard_map/pallas_call | solution.py:164
  451.4 1.5 collective-permute-start.4
  452.8 0.0 collective-permute-done
  452.9 0.0 collective-permute-done.1
  452.9 0.1 constant_dynamic-update-slice_fusion.3
  452.9 0.0 collective-permute-done.2
  452.9 0.1 constant_dynamic-update-slice_fusion.2
  453.0 7.0 %collective-permute-done.3 = bf16[1,512,512]{2,1,0:T(8,128)(2,1)S(1)} collective-permute-done((bf16[1,512,512]{2,1,0:T(8,128)(2,1)}, bf16[1,512,512]{2,1,0:T(8,128)(2,1)S(1)}, u32[]{:S(2)}, u32[]{:S(2)}) %collective-permute-start.3) | collective-permute-done | bytes 524320 | tf_op jit(solution)/shard_map/ppermute | solution.py:19
  460.0 0.1 constant_dynamic-update-slice_fusion.1
  460.1 0.0 copy-start.1
  460.1 3.6 collective-permute-done.4
  463.7 0.0 copy-done.1
  463.7 0.7 constant_dynamic-update-slice_fusion
  (1 shorter events, 0.0 us)
Async XLA Ops:
  12.5 12.5 %copy-start = (s32[1,64,16,2]{1,3,2,0:T(2,128)S(1)}, s32[1,64,16,2]{1,3,2,0:T(2,128)}, u32[]{:S(2)}) copy-start(s32[1,64,16,2]{1,3,2,0:T(2,128)} %param.7) | copy-start | bytes 24580
  12.5 384.6 %all-to-all-start = ((bf16[64,2,512,128]{3,2,1,0:T(8,128)(2,1)}), bf16[64,2,512,128]{3,2,1,0:T(8,128)(2,1)}, u32[]{:S(2)}, u32[]{:S(2)}) async-start(bf16[64,2,512,128]{3,2,1,0:T(8,128)(2,1)} %shard_map.46), calls=%async_computation | async-start | bytes 33554432 | tf_op jit(solution)/shard_map/all_to_all | solution.py:181
  404.3 48.5 %collective-permute-start = (bf16[1,512,256]{2,1,0:T(8,128)(2,1)}, bf16[1,512,256]{2,1,0:T(8,128)(2,1)S(1)}, u32[]{:S(2)}, u32[]{:S(2)}) collective-permute-start(bf16[1,512,256]{2,1,0:T(8,128)(2,1)} %bitcast.33), channel_id=1, source_target_pairs={{0,1},{1,2},{2,3},{3,0},{4,5},{5,6},{6,7},{7,4},{8,9},{9,10},{10,1... | collective-permute-start | bytes 786440 | tf_op jit(solution)/shard_map/ppermute | solution.py:19
  417.5 35.4 %collective-permute-start.1 = (bf16[1,512,512]{2,1,0:T(8,128)(2,1)}, bf16[1,512,512]{2,1,0:T(8,128)(2,1)S(1)}, u32[]{:S(2)}, u32[]{:S(2)}) collective-permute-start(bf16[1,512,512]{2,1,0:T(8,128)(2,1)} %bitcast.31), channel_id=1, source_target_pairs={{0,1},{1,2},{2,3},{3,0},{4,5},{5,6},{6,7},{7,4},{8,9},{9,10},{10,1... | collective-permute-start | bytes 1572872 | tf_op jit(solution)/shard_map/ppermute | solution.py:19
  430.8 22.1 %collective-permute-start.2 = (bf16[1,512,512]{2,1,0:T(8,128)(2,1)}, bf16[1,512,512]{2,1,0:T(8,128)(2,1)S(1)}, u32[]{:S(2)}, u32[]{:S(2)}) collective-permute-start(bf16[1,512,512]{2,1,0:T(8,128)(2,1)} %bitcast.30), channel_id=1, source_target_pairs={{0,1},{1,2},{2,3},{3,0},{4,5},{5,6},{6,7},{7,4},{8,9},{9,10},{10,1... | collective-permute-start | bytes 1572872 | tf_op jit(solution)/shard_map/ppermute | solution.py:19
  443.7 16.3 %collective-permute-start.3 = (bf16[1,512,512]{2,1,0:T(8,128)(2,1)}, bf16[1,512,512]{2,1,0:T(8,128)(2,1)S(1)}, u32[]{:S(2)}, u32[]{:S(2)}) collective-permute-start(bf16[1,512,512]{2,1,0:T(8,128)(2,1)} %bitcast.29), channel_id=1, source_target_pairs={{0,1},{1,2},{2,3},{3,0},{4,5},{5,6},{6,7},{7,4},{8,9},{9,10},{10,1... | collective-permute-start | bytes 1572872 | tf_op jit(solution)/shard_map/ppermute | solution.py:19
  451.4 12.3 %collective-permute-start.4 = (bf16[1,512,256]{2,1,0:T(8,128)(2,1)}, bf16[1,512,256]{2,1,0:T(8,128)(2,1)S(1)}, u32[]{:S(2)}, u32[]{:S(2)}) collective-permute-start(bf16[1,512,256]{2,1,0:T(8,128)(2,1)} %bitcast.32), channel_id=1, source_target_pairs={{0,1},{1,2},{2,3},{3,0},{4,5},{5,6},{6,7},{7,4},{8,9},{9,10},{10,1... | collective-permute-start | bytes 786440 | tf_op jit(solution)/shard_map/ppermute | solution.py:19
  460.1 3.6 copy-start.1

commit v10 on v2

--- a/solution.py
+++ b/solution.py
@@ -107,9 +107,22 @@
     )(send)
 
 
-def attend_kernel(slot_ref, live_ref, q_ref, k_ref, v_ref, first_ref, second_ref, o_ref):
+def attend_kernel(live_ref, q_ref, k_ref, v_ref, picked_ref, o_ref, out_buf, sems):
     head = pl.program_id(0)
+    heads = pl.num_programs(0)
     rows = q_ref.shape[0]
+    pipe_size = lax.axis_size("pipe")
+    here = lax.axis_index("pipe")
+    after = lax.rem(here + 1, pipe_size)
+    before = lax.rem(here + pipe_size - 1, pipe_size)
+
+    @pl.when(head == 0)
+    def _():
+        barrier = pltpu.get_barrier_semaphore()
+        for peer in (before, after):
+            pl.semaphore_signal(barrier, 1, device_id={"pipe": peer}, device_id_type=MESH)
+        pl.semaphore_wait(barrier, 2)
+
     score_scale = HD ** (-0.5)
     dims = (((1,), (1,)), ((), ()))
     query = q_ref[...]
@@ -121,10 +134,10 @@
     row_index = lax.broadcasted_iota(jnp.int32, (rows, rows), 0)
     col_index = lax.broadcasted_iota(jnp.int32, (rows, rows), 1)
     own = jnp.where(row_index >= col_index, scores_against(k_ref[...]), -jnp.inf)
-    live_first = live_ref[PICKS * head] > 0
-    live_second = live_ref[PICKS * head + 1] > 0
-    first = jnp.where(live_first, scores_against(first_ref[0, 0]), -jnp.inf)
-    second = jnp.where(live_second, scores_against(second_ref[0, 0]), -jnp.inf)
+    first_bias = jnp.where(live_ref[PICKS * head] > 0, 0.0, -jnp.inf)
+    second_bias = jnp.where(live_ref[PICKS * head + 1] > 0, 0.0, -jnp.inf)
+    first = scores_against(picked_ref[0, 0]) + first_bias
+    second = scores_against(picked_ref[1, 0]) + second_bias
     row_top = jnp.maximum(
         jnp.maximum(jnp.max(own, axis=1), jnp.max(first, axis=1)), jnp.max(second, axis=1)
     )[:, None]
@@ -134,42 +147,60 @@
     row_scale = 1.0 / (
         jnp.sum(own, axis=1) + jnp.sum(first, axis=1) + jnp.sum(second, axis=1)
     )[:, None]
-    first_values = jnp.where(live_first, first_ref[0, 1], jnp.zeros_like(first_ref[0, 1]))
-    second_values = jnp.where(live_second, second_ref[0, 1], jnp.zeros_like(second_ref[0, 1]))
     mixed = jnp.dot((own * row_scale).astype(jnp.bfloat16), v_ref[...],
                     preferred_element_type=jnp.float32)
-    mixed += jnp.dot((first * row_scale).astype(jnp.bfloat16), first_values,
+    mixed += jnp.dot((first * row_scale).astype(jnp.bfloat16), picked_ref[0, 1],
                      preferred_element_type=jnp.float32)
-    mixed += jnp.dot((second * row_scale).astype(jnp.bfloat16), second_values,
+    mixed += jnp.dot((second * row_scale).astype(jnp.bfloat16), picked_ref[1, 1],
                      preferred_element_type=jnp.float32)
-    o_ref[...] = mixed.astype(o_ref.dtype)
-
-
-def attend(slots, live, queries, keys, values, received):
+    out_buf[head] = mixed.astype(out_buf.dtype)
+
+    def relay(slot):
+        return pltpu.make_async_remote_copy(
+            src_ref=out_buf.at[slot],
+            dst_ref=o_ref.at[:, pl.ds(pl.multiple_of(slot * HD, HD), HD)],
+            send_sem=sems.at[0, slot],
+            recv_sem=sems.at[1, slot],
+            device_id={"pipe": after},
+            device_id_type=MESH,
+        )
+
+    relay(head).start()
+
+    @pl.when(head == heads - 1)
+    def _():
+        def finish(slot, carry):
+            relay(slot).wait_send()
+            relay(slot).wait_recv()
+            return carry
+
+        lax.fori_loop(0, heads, finish, 0)
+
+
+def attend_and_pass(live, queries, keys, values, picked):
     rows = queries.shape[0]
-    head_block = pl.BlockSpec((rows, HD), lambda h, slot_ref, live_ref: (0, h))
+    head_block = pl.BlockSpec((rows, HD), lambda h, live_ref: (0, h))
     grid_spec = pltpu.PrefetchScalarGridSpec(
-        num_scalar_prefetch=2,
+        num_scalar_prefetch=1,
         grid=(HEADS,),
         in_specs=[
             head_block,
             head_block,
             head_block,
-            pl.BlockSpec(
-                (1, 2, rows, HD), lambda h, slot_ref, live_ref: (slot_ref[PICKS * h], 0, 0, 0)
-            ),
-            pl.BlockSpec(
-                (1, 2, rows, HD),
-                lambda h, slot_ref, live_ref: (slot_ref[PICKS * h + 1], 0, 0, 0),
-            ),
+            pl.BlockSpec((PICKS, 2, rows, HD), lambda h, live_ref: (h, 0, 0, 0)),
         ],
-        out_specs=head_block,
+        out_specs=pl.BlockSpec(memory_space=pl.ANY),
+        scratch_shapes=[
+            pltpu.VMEM((HEADS, rows, HD), queries.dtype),
+            pltpu.SemaphoreType.DMA((2, HEADS)),
+        ],
     )
     return pl.pallas_call(
         attend_kernel,
         grid_spec=grid_spec,
         out_shape=jax.ShapeDtypeStruct(queries.shape, queries.dtype),
-    )(slots, live, queries, keys, values, received, received)
+        compiler_params=pltpu.CompilerParams(collective_id=0, has_side_effects=True),
+    )(live, queries, keys, values, picked)
 
 
 def per_device(queries, keys, values, picks):
@@ -182,9 +213,9 @@
     chosen = lax.dynamic_index_in_dim(every_pick, rank_here, 0, keepdims=False).reshape(-1)
     live = (chosen >= 0).astype(jnp.int32)
     slots = jnp.maximum(chosen, 0).astype(jnp.int32)
-    merged = attend(slots, live, queries[0], keys[0], values[0], received)
-    merged = passed_along(merged[None], "pipe", 1)
-    return merged
+    picked = jnp.take(received, slots, axis=0)
+    merged = attend_and_pass(live, queries[0], keys[0], values[0], picked)
+    return merged[None]
 
 
 def solution(mesh):

time: 487 us -> 472 us (0.969)
  waiting for transfers between devices: 418 us -> 370 us
  Pallas kernels: 50.9 us -> 65 us
  local copies, waits for them, and re-layouts: 2.62 us -> 14.6 us
  other arithmetic: 1.95 us -> 9.86 us
    ppermute x1 -> x0, waiting for transfers between devices: 47.5 us -> none  [passed_along(): return lax.ppermute(value, axis, pairs)]
    pallas_call x1, Pallas kernels: 39.7 us -> 53.6 us  [attend_and_pass(): pl.pallas_call(attend_kernel, grid_spec=grid_spec, out_shape=jax.ShapeDty...]
    gather x0 -> x1, local copies, waits for them, and re-layouts: none -> 10.7 us  [per_device(): picked = jnp.take(received, slots, axis=0)]
    select_n x0 -> x1, other arithmetic: none -> 7.47 us  [per_device(): picked = jnp.take(received, slots, axis=0)]
  transfers between devices with their start and end apart: 2 -> 1, of which waited for: 2 -> 1; matrix products, arithmetic and copies ran while one was open for 0% -> 0% of each run, Pallas kernels for 0% -> 0%
where the time goes in v10:
time: 472 us
  waiting for transfers between devices  370 us (78%)
  Pallas kernels  65 us (14%)
  local copies, waits for them, and re-layouts  14.6 us (3%)
  starting transfers between devices  12 us (3%)
  other arithmetic  9.86 us (2%)
    all_to_all x1, waiting for transfers between devices, per_device(): lax.all_to_all(send, 'ctx', split_axis=0, concat_axis=0, tiled=True)  370 us
    pallas_call x1, Pallas kernels, attend_and_pass(): pl.pallas_call(attend_kernel, grid_spec=grid_spec, out_shape=jax.ShapeDty...  53.6 us
    all_to_all x1, starting transfers between devices, per_device(): lax.all_to_all(send, 'ctx', split_axis=0, concat_axis=0, tiled=True)  12 us
    pallas_call x1, Pallas kernels, pack_requested(): pl.pallas_call(functools.partial(pack_kernel, group), grid_spec=grid_spec...  11.4 us
    gather x1, local copies, waits for them, and re-layouts, per_device(): picked = jnp.take(received, slots, axis=0)  10.7 us
  transfers between devices with their start and end apart: 1, of which 1 were waited for; matrix products, arithmetic and copies ran while one was open for 0% of the time, Pallas kernels for 0%

profile of v10, /device:TPU:48, one launch (start us, length us, event | category | flops | bytes accessed | tf_op | source)
XLA Modules:
  0.0 471.8 jit_solution(1369067535321141617)
XLA Ops:
  0.0 1.3 fusion.1.asked_ref
  1.3 11.4 %shard_map.46 = bf16[64,2,512,128]{3,2,1,0:T(8,128)(2,1)} custom-call(s32[64]{0:T(128)} %fusion.1.asked_ref, bf16[512,2048]{1,0:T(8,128)(2,1)} %bitcast.8, bf16[512,2048]{1,0:T(8,128)(2,1)} %bitcast.10), custom_call_target="tpu_custom_call" | custom-call | tf_op jit(solution)/shard_map/pallas_call | solution.py:41
  12.7 0.0 copy-start
  12.7 12.0 %all-to-all-start = ((bf16[64,2,512,128]{3,2,1,0:T(8,128)(2,1)}), bf16[64,2,512,128]{3,2,1,0:T(8,128)(2,1)}, u32[]{:S(2)}, u32[]{:S(2)}) async-start(bf16[64,2,512,128]{3,2,1,0:T(8,128)(2,1)} %shard_map.46), calls=%async_computation | async-start | bytes 33554432 | tf_op jit(solution)/shard_map/all_to_all | solution.py:212
  24.7 0.0 copy-done
  24.7 0.4 compare_reduce_fusion
  25.1 0.1 le.16
  25.3 0.7 maximum_reduce_fusion
  25.9 0.1 reshape.35
  26.0 0.6 reshape.32.live_ref
  26.6 370.2 %all-to-all-done = bf16[64,2,512,128]{3,2,1,0:T(8,128)(2,1)} async-done(((bf16[64,2,512,128]{3,2,1,0:T(8,128)(2,1)}), bf16[64,2,512,128]{3,2,1,0:T(8,128)(2,1)}, u32[]{:S(2)}, u32[]{:S(2)}) %all-to-all-start) | async-done | bytes 16777248 | tf_op jit(solution)/shard_map/all_to_all | solution.py:212
  396.9 10.7 %gather_fusion = bf16[32,2,512,128]{3,2,1,0:T(8,128)(2,1)} fusion(bf16[64,2,512,128]{3,2,1,0:T(8,128)(2,1)} %all-to-all-done, s32[1024]{0:T(1024)S(1)} %pad_clamp_fusion), kind=kCustom, calls=%fused_computation | custom fusion | bytes 16777344 | tf_op jit(solution)/shard_map/jit(_take)/gather | solution.py:216
  407.6 7.5 %broadcast_select_fusion.picked_ref = bf16[32,2,512,128]{3,2,1,0:T(8,128)(2,1)} fusion(bf16[32,2,512,128]{3,2,1,0:T(8,128)(2,1)} %gather_fusion, pred[32]{0:T(512)(128)(4,1)S(1)} %le.16), kind=kLoop, calls=%fused_computation.1 | loop fusion | flops 4194304 | bytes 16777248 | tf_op jit(solution)/shard_map/jit(_take)/select_n | solution.py:216
  415.1 53.6 %shard_map.47 = bf16[512,2048]{1,0:T(8,128)(2,1)} custom-call(s32[32]{0:T(128)} %reshape.32.live_ref, bf16[512,2048]{1,0:T(8,128)(2,1)} %bitcast.13, bf16[512,2048]{1,0:T(8,128)(2,1)} %bitcast.9, bf16[512,2048]{1,0:T(8,128)(2,1)} %bitcast.11, bf16[32,2,512,128]{3,2,1,0:T(8,128)(2,1)} %broadcast_select_fusion.picked_ref), custom_call_target="tpu_custom_call" | custom-call | tf_op jit(solution)/shard_map/pallas_call | solution.py:198
  468.7 3.2 copy.6
  (1 shorter events, 0.0 us)
Async XLA Ops:
  12.7 12.0 %copy-start = (s32[1,64,16,2]{1,3,2,0:T(2,128)S(1)}, s32[1,64,16,2]{1,3,2,0:T(2,128)}, u32[]{:S(2)}) copy-start(s32[1,64,16,2]{1,3,2,0:T(2,128)} %param.7) | copy-start | bytes 24580
  12.7 384.2 %all-to-all-start = ((bf16[64,2,512,128]{3,2,1,0:T(8,128)(2,1)}), bf16[64,2,512,128]{3,2,1,0:T(8,128)(2,1)}, u32[]{:S(2)}, u32[]{:S(2)}) async-start(bf16[64,2,512,128]{3,2,1,0:T(8,128)(2,1)} %shard_map.46), calls=%async_computation | async-start | bytes 33554432 | tf_op jit(solution)/shard_map/all_to_all | solution.py:212

commit v11 on v10

--- a/solution.py
+++ b/solution.py
@@ -203,6 +203,26 @@
     )(live, queries, keys, values, picked)
 
 
+def gather_kernel(slot_ref, source_ref, out_ref):
+    out_ref[...] = source_ref[...]
+
+
+def gather_slots(slots, received):
+    count = slots.shape[0]
+    block = (1,) + received.shape[1:]
+    grid_spec = pltpu.PrefetchScalarGridSpec(
+        num_scalar_prefetch=1,
+        grid=(count,),
+        in_specs=[pl.BlockSpec(block, lambda i, slot_ref: (slot_ref[i], 0, 0, 0))],
+        out_specs=pl.BlockSpec(block, lambda i, slot_ref: (i, 0, 0, 0)),
+    )
+    return pl.pallas_call(
+        gather_kernel,
+        grid_spec=grid_spec,
+        out_shape=jax.ShapeDtypeStruct((count,) + received.shape[1:], received.dtype),
+    )(slots, received)
+
+
 def per_device(queries, keys, values, picks):
     rank_here = lax.axis_index("ctx")
     every_pick = picks[0]
@@ -213,7 +233,7 @@
     chosen = lax.dynamic_index_in_dim(every_pick, rank_here, 0, keepdims=False).reshape(-1)
     live = (chosen >= 0).astype(jnp.int32)
     slots = jnp.maximum(chosen, 0).astype(jnp.int32)
-    picked = jnp.take(received, slots, axis=0)
+    picked = gather_slots(slots, received)
     merged = attend_and_pass(live, queries[0], keys[0], values[0], picked)
     return merged[None]
 

time: 472 us -> 473 us (level)
  Pallas kernels: 65 us -> 83.3 us
  local copies, waits for them, and re-layouts: 14.6 us -> 4.43 us
  other arithmetic: 9.86 us -> 1.95 us
    pallas_call x0 -> x1, Pallas kernels: none -> 17.6 us  [gather_slots(): pl.pallas_call(gather_kernel, grid_spec=grid_spec, out_shape=jax.ShapeDty...]
    gather x1 -> x0, local copies, waits for them, and re-layouts: 10.7 us -> none  [per_device(): picked = jnp.take(received, slots, axis=0)]
    select_n x1 -> x0, other arithmetic: 7.47 us -> none  [per_device(): picked = jnp.take(received, slots, axis=0)]
where the time goes in v11:
time: 473 us; the launch traced here: 472 us
  waiting for transfers between devices  370 us (78%)
  Pallas kernels  83.3 us (18%)
  starting transfers between devices  12.1 us (3%)
    all_to_all x1, waiting for transfers between devices, per_device(): lax.all_to_all(send, 'ctx', split_axis=0, concat_axis=0, tiled=True)  370 us
    pallas_call x1, Pallas kernels, attend_and_pass(): pl.pallas_call(attend_kernel, grid_spec=grid_spec, out_shape=jax.ShapeDty...  54.4 us
    pallas_call x1, Pallas kernels, gather_slots(): pl.pallas_call(gather_kernel, grid_spec=grid_spec, out_shape=jax.ShapeDty...  17.6 us
    all_to_all x1, starting transfers between devices, per_device(): lax.all_to_all(send, 'ctx', split_axis=0, concat_axis=0, tiled=True)  12.1 us
    pallas_call x1, Pallas kernels, pack_requested(): pl.pallas_call(functools.partial(pack_kernel, group), grid_spec=grid_spec...  11.3 us
  transfers between devices with their start and end apart: 1, of which 1 were waited for; matrix products, arithmetic and copies ran while one was open for 0% of the time, Pallas kernels for 0%

profile of v11, /device:TPU:48, one launch (start us, length us, event | category | flops | bytes accessed | tf_op | source)
XLA Modules:
  0.0 472.0 jit_solution(13468273116682135739)
XLA Ops:
  0.0 1.3 fusion.1.asked_ref
  1.3 11.3 %shard_map.46 = bf16[64,2,512,128]{3,2,1,0:T(8,128)(2,1)} custom-call(s32[64]{0:T(128)} %fusion.1.asked_ref, bf16[512,2048]{1,0:T(8,128)(2,1)} %bitcast.8, bf16[512,2048]{1,0:T(8,128)(2,1)} %bitcast.10), custom_call_target="tpu_custom_call" | custom-call | tf_op jit(solution)/shard_map/pallas_call | solution.py:41
  12.6 0.0 copy-start
  12.6 12.1 %all-to-all-start = ((bf16[64,2,512,128]{3,2,1,0:T(8,128)(2,1)}), bf16[64,2,512,128]{3,2,1,0:T(8,128)(2,1)}, u32[]{:S(2)}, u32[]{:S(2)}) async-start(bf16[64,2,512,128]{3,2,1,0:T(8,128)(2,1)} %shard_map.46), calls=%async_computation | async-start | bytes 33554432 | tf_op jit(solution)/shard_map/all_to_all | solution.py:232
  24.7 0.0 copy-done
  24.7 0.7 maximum_reduce_fusion
  25.4 0.7 max.6.slot_ref
  26.1 0.6 reshape.12.live_ref
  26.7 370.2 %all-to-all-done.source_ref = bf16[64,2,512,128]{3,2,1,0:T(8,128)(2,1)} async-done(((bf16[64,2,512,128]{3,2,1,0:T(8,128)(2,1)}), bf16[64,2,512,128]{3,2,1,0:T(8,128)(2,1)}, u32[]{:S(2)}, u32[]{:S(2)}) %all-to-all-start) | async-done | bytes 16777248 | tf_op jit(solution)/shard_map/all_to_all | solution.py:232
  396.9 17.6 %shard_map.47.picked_ref = bf16[32,2,512,128]{3,2,1,0:T(8,128)(2,1)} custom-call(s32[32]{0:T(128)} %max.6.slot_ref, bf16[64,2,512,128]{3,2,1,0:T(8,128)(2,1)} %all-to-all-done.source_ref), custom_call_target="tpu_custom_call" | custom-call | tf_op jit(solution)/shard_map/pallas_call | solution.py:219
  414.5 54.4 %shard_map.48 = bf16[512,2048]{1,0:T(8,128)(2,1)} custom-call(s32[32]{0:T(128)} %reshape.12.live_ref, bf16[512,2048]{1,0:T(8,128)(2,1)} %bitcast.13, bf16[512,2048]{1,0:T(8,128)(2,1)} %bitcast.9, bf16[512,2048]{1,0:T(8,128)(2,1)} %bitcast.11, bf16[32,2,512,128]{3,2,1,0:T(8,128)(2,1)} %shard_map.47.picked_ref), custom_call_target="tpu_custom_call" | custom-call | tf_op jit(solution)/shard_map/pallas_call | solution.py:198
  468.9 3.2 copy.6
Async XLA Ops:
  12.6 12.1 %copy-start = (s32[1,64,16,2]{1,3,2,0:T(2,128)S(1)}, s32[1,64,16,2]{1,3,2,0:T(2,128)}, u32[]{:S(2)}) copy-start(s32[1,64,16,2]{1,3,2,0:T(2,128)} %param.7) | copy-start | bytes 24580
  12.6 384.3 %all-to-all-start = ((bf16[64,2,512,128]{3,2,1,0:T(8,128)(2,1)}), bf16[64,2,512,128]{3,2,1,0:T(8,128)(2,1)}, u32[]{:S(2)}, u32[]{:S(2)}) async-start(bf16[64,2,512,128]{3,2,1,0:T(8,128)(2,1)} %shard_map.46), calls=%async_computation | async-start | bytes 33554432 | tf_op jit(solution)/shard_map/all_to_all | solution.py:232

commit v12 on v11

--- a/solution.py
+++ b/solution.py
@@ -203,18 +203,32 @@
     )(live, queries, keys, values, picked)
 
 
-def gather_kernel(slot_ref, source_ref, out_ref):
-    out_ref[...] = source_ref[...]
+def gather_kernel(slot_ref, source_ref, out_ref, sems):
+    count = out_ref.shape[0]
+
+    def copy(i):
+        return pltpu.make_async_copy(source_ref.at[slot_ref[i]], out_ref.at[i], sems.at[i])
+
+    def start(i, carry):
+        copy(i).start()
+        return carry
+
+    def finish(i, carry):
+        copy(i).wait()
+        return carry
+
+    lax.fori_loop(0, count, start, 0)
+    lax.fori_loop(0, count, finish, 0)
 
 
 def gather_slots(slots, received):
     count = slots.shape[0]
-    block = (1,) + received.shape[1:]
     grid_spec = pltpu.PrefetchScalarGridSpec(
         num_scalar_prefetch=1,
-        grid=(count,),
-        in_specs=[pl.BlockSpec(block, lambda i, slot_ref: (slot_ref[i], 0, 0, 0))],
-        out_specs=pl.BlockSpec(block, lambda i, slot_ref: (i, 0, 0, 0)),
+        grid=(1,),
+        in_specs=[pl.BlockSpec(memory_space=pl.ANY)],
+        out_specs=pl.BlockSpec(memory_space=pl.ANY),
+        scratch_shapes=[pltpu.SemaphoreType.DMA((count,))],
     )
     return pl.pallas_call(
         gather_kernel,

time: 473 us -> 710 us (1.50)
  Pallas kernels: 83.3 us -> 321 us
    pallas_call x1, Pallas kernels: 17.6 us -> 256 us  [gather_slots(): pl.pallas_call(gather_kernel, grid_spec=grid_spec, out_shape=jax.ShapeDty...]
where the time goes in v12:
time: 710 us
  waiting for transfers between devices  370 us (52%)
  Pallas kernels  321 us (45%)
  starting transfers between devices  12 us (2%)
    all_to_all x1, waiting for transfers between devices, per_device(): lax.all_to_all(send, 'ctx', split_axis=0, concat_axis=0, tiled=True)  370 us
    pallas_call x1, Pallas kernels, gather_slots(): pl.pallas_call(gather_kernel, grid_spec=grid_spec, out_shape=jax.ShapeDty...  256 us
    pallas_call x1, Pallas kernels, attend_and_pass(): pl.pallas_call(attend_kernel, grid_spec=grid_spec, out_shape=jax.ShapeDty...  53.6 us
  transfers between devices with their start and end apart: 1, of which 1 were waited for; matrix products, arithmetic and copies ran while one was open for 0% of the time, Pallas kernels for 0%

profile of v12, /device:TPU:48, one launch (start us, length us, event | category | flops | bytes accessed | tf_op | source)
XLA Modules:
  0.0 709.9 jit_solution(10238574409597353502)
XLA Ops:
  0.0 1.3 fusion.1.asked_ref
  1.3 11.4 %shard_map.46 = bf16[64,2,512,128]{3,2,1,0:T(8,128)(2,1)} custom-call(s32[64]{0:T(128)} %fusion.1.asked_ref, bf16[512,2048]{1,0:T(8,128)(2,1)} %bitcast.8, bf16[512,2048]{1,0:T(8,128)(2,1)} %bitcast.10), custom_call_target="tpu_custom_call" | custom-call | tf_op jit(solution)/shard_map/pallas_call | solution.py:41
  12.7 0.0 copy-start
  12.7 12.0 %all-to-all-start = ((bf16[64,2,512,128]{3,2,1,0:T(8,128)(2,1)}), bf16[64,2,512,128]{3,2,1,0:T(8,128)(2,1)}, u32[]{:S(2)}, u32[]{:S(2)}) async-start(bf16[64,2,512,128]{3,2,1,0:T(8,128)(2,1)} %shard_map.46), calls=%async_computation | async-start | bytes 33554432 | tf_op jit(solution)/shard_map/all_to_all | solution.py:246
  24.7 0.0 copy-done
  24.8 0.7 maximum_reduce_fusion
  25.4 0.7 max.6.slot_ref
  26.1 0.6 reshape.12.live_ref
  26.7 370.2 %all-to-all-done.source_ref = bf16[64,2,512,128]{3,2,1,0:T(8,128)(2,1)} async-done(((bf16[64,2,512,128]{3,2,1,0:T(8,128)(2,1)}), bf16[64,2,512,128]{3,2,1,0:T(8,128)(2,1)}, u32[]{:S(2)}, u32[]{:S(2)}) %all-to-all-start) | async-done | bytes 16777248 | tf_op jit(solution)/shard_map/all_to_all | solution.py:246
  396.9 256.2 %shard_map.47.picked_ref = bf16[32,2,512,128]{3,2,1,0:T(8,128)(2,1)} custom-call(s32[32]{0:T(128)} %max.6.slot_ref, bf16[64,2,512,128]{3,2,1,0:T(8,128)(2,1)} %all-to-all-done.source_ref), custom_call_target="tpu_custom_call" | custom-call | tf_op jit(solution)/shard_map/pallas_call | solution.py:233
  653.1 53.6 %shard_map.48 = bf16[512,2048]{1,0:T(8,128)(2,1)} custom-call(s32[32]{0:T(128)} %reshape.12.live_ref, bf16[512,2048]{1,0:T(8,128)(2,1)} %bitcast.13, bf16[512,2048]{1,0:T(8,128)(2,1)} %bitcast.9, bf16[512,2048]{1,0:T(8,128)(2,1)} %bitcast.11, bf16[32,2,512,128]{3,2,1,0:T(8,128)(2,1)} %shard_map.47.picked_ref), custom_call_target="tpu_custom_call" | custom-call | tf_op jit(solution)/shard_map/pallas_call | solution.py:198
  706.7 3.2 copy.6
Async XLA Ops:
  12.7 12.1 %copy-start = (s32[1,64,16,2]{1,3,2,0:T(2,128)S(1)}, s32[1,64,16,2]{1,3,2,0:T(2,128)}, u32[]{:S(2)}) copy-start(s32[1,64,16,2]{1,3,2,0:T(2,128)} %param.7) | copy-start | bytes 24580
  12.7 384.2 %all-to-all-start = ((bf16[64,2,512,128]{3,2,1,0:T(8,128)(2,1)}), bf16[64,2,512,128]{3,2,1,0:T(8,128)(2,1)}, u32[]{:S(2)}, u32[]{:S(2)}) async-start(bf16[64,2,512,128]{3,2,1,0:T(8,128)(2,1)} %shard_map.46), calls=%async_computation | async-start | bytes 33554432 | tf_op jit(solution)/shard_map/all_to_all | solution.py:246

commit v13 on v10

--- a/solution.py
+++ b/solution.py
@@ -107,7 +107,7 @@
     )(send)
 
 
-def attend_kernel(live_ref, q_ref, k_ref, v_ref, picked_ref, o_ref, out_buf, sems):
+def attend_kernel(slot_ref, live_ref, q_ref, k_ref, v_ref, received_ref, o_ref, out_buf, sems):
     head = pl.program_id(0)
     heads = pl.num_programs(0)
     rows = q_ref.shape[0]
@@ -136,8 +136,10 @@
     own = jnp.where(row_index >= col_index, scores_against(k_ref[...]), -jnp.inf)
     first_bias = jnp.where(live_ref[PICKS * head] > 0, 0.0, -jnp.inf)
     second_bias = jnp.where(live_ref[PICKS * head + 1] > 0, 0.0, -jnp.inf)
-    first = scores_against(picked_ref[0, 0]) + first_bias
-    second = scores_against(picked_ref[1, 0]) + second_bias
+    first_block = received_ref[slot_ref[PICKS * head]]
+    second_block = received_ref[slot_ref[PICKS * head + 1]]
+    first = scores_against(first_block[0]) + first_bias
+    second = scores_against(second_block[0]) + second_bias
     row_top = jnp.maximum(
         jnp.maximum(jnp.max(own, axis=1), jnp.max(first, axis=1)), jnp.max(second, axis=1)
     )[:, None]
@@ -149,9 +151,9 @@
     )[:, None]
     mixed = jnp.dot((own * row_scale).astype(jnp.bfloat16), v_ref[...],
                     preferred_element_type=jnp.float32)
-    mixed += jnp.dot((first * row_scale).astype(jnp.bfloat16), picked_ref[0, 1],
+    mixed += jnp.dot((first * row_scale).astype(jnp.bfloat16), first_block[1],
                      preferred_element_type=jnp.float32)
-    mixed += jnp.dot((second * row_scale).astype(jnp.bfloat16), picked_ref[1, 1],
+    mixed += jnp.dot((second * row_scale).astype(jnp.bfloat16), second_block[1],
                      preferred_element_type=jnp.float32)
     out_buf[head] = mixed.astype(out_buf.dtype)
 
@@ -177,17 +179,17 @@
         lax.fori_loop(0, heads, finish, 0)
 
 
-def attend_and_pass(live, queries, keys, values, picked):
+def attend_and_pass(slots, live, queries, keys, values, received):
     rows = queries.shape[0]
-    head_block = pl.BlockSpec((rows, HD), lambda h, live_ref: (0, h))
+    head_block = pl.BlockSpec((rows, HD), lambda h, slot_ref, live_ref: (0, h))
     grid_spec = pltpu.PrefetchScalarGridSpec(
-        num_scalar_prefetch=1,
+        num_scalar_prefetch=2,
         grid=(HEADS,),
         in_specs=[
             head_block,
             head_block,
             head_block,
-            pl.BlockSpec((PICKS, 2, rows, HD), lambda h, live_ref: (h, 0, 0, 0)),
+            pl.BlockSpec(memory_space=pltpu.VMEM),
         ],
         out_specs=pl.BlockSpec(memory_space=pl.ANY),
         scratch_shapes=[
@@ -199,8 +201,10 @@
         attend_kernel,
         grid_spec=grid_spec,
         out_shape=jax.ShapeDtypeStruct(queries.shape, queries.dtype),
-        compiler_params=pltpu.CompilerParams(collective_id=0, has_side_effects=True),
-    )(live, queries, keys, values, picked)
+        compiler_params=pltpu.CompilerParams(
+            collective_id=0, has_side_effects=True, vmem_limit_bytes=48 * 1024 * 1024
+        ),
+    )(slots, live, queries, keys, values, received)
 
 
 def per_device(queries, keys, values, picks):
@@ -213,8 +217,7 @@
     chosen = lax.dynamic_index_in_dim(every_pick, rank_here, 0, keepdims=False).reshape(-1)
     live = (chosen >= 0).astype(jnp.int32)
     slots = jnp.maximum(chosen, 0).astype(jnp.int32)
-    picked = jnp.take(received, slots, axis=0)
-    merged = attend_and_pass(live, queries[0], keys[0], values[0], picked)
+    merged = attend_and_pass(slots, live, queries[0], keys[0], values[0], received)
     return merged[None]
 
 

time: 472 us -> 457 us (0.968)
  local copies, waits for them, and re-layouts: 14.6 us -> 1.51 us
  other arithmetic: 9.86 us -> 1.95 us
    gather x1 -> x0, local copies, waits for them, and re-layouts: 10.7 us -> none  [per_device(): picked = jnp.take(received, slots, axis=0)]
    select_n x1 -> x0, other arithmetic: 7.47 us -> none  [per_device(): picked = jnp.take(received, slots, axis=0)]
where the time goes in v13:
time: 457 us; the launch traced here: 456 us
  waiting for transfers between devices  371 us (81%)
  Pallas kernels  69.5 us (15%)
  starting transfers between devices  12.1 us (3%)
    all_to_all x1, waiting for transfers between devices, per_device(): lax.all_to_all(send, 'ctx', split_axis=0, concat_axis=0, tiled=True)  371 us
    pallas_call x1, Pallas kernels, attend_and_pass(): pl.pallas_call(attend_kernel, grid_spec=grid_spec, out_shape=jax.ShapeDty...  58.1 us
    all_to_all x1, starting transfers between devices, per_device(): lax.all_to_all(send, 'ctx', split_axis=0, concat_axis=0, tiled=True)  12.1 us
    pallas_call x1, Pallas kernels, pack_requested(): pl.pallas_call(functools.partial(pack_kernel, group), grid_spec=grid_spec...  11.4 us
  transfers between devices with their start and end apart: 1, of which 1 were waited for; matrix products, arithmetic and copies ran while one was open for 0% of the time, Pallas kernels for 0%

profile of v13, /device:TPU:48, one launch (start us, length us, event | category | flops | bytes accessed | tf_op | source)
XLA Modules:
  0.0 456.4 jit_solution(2988613603315931170)
XLA Ops:
  0.0 1.3 fusion.1.asked_ref
  1.3 11.4 %shard_map.46 = bf16[64,2,512,128]{3,2,1,0:T(8,128)(2,1)} custom-call(s32[64]{0:T(128)} %fusion.1.asked_ref, bf16[512,2048]{1,0:T(8,128)(2,1)} %bitcast.10, bf16[512,2048]{1,0:T(8,128)(2,1)} %bitcast.12), custom_call_target="tpu_custom_call" | custom-call | tf_op jit(solution)/shard_map/pallas_call | solution.py:41
  12.6 0.0 copy-start.1
  12.6 0.0 copy-start
  12.6 12.1 %all-to-all-start = ((bf16[64,2,512,128]{3,2,1,0:T(8,128)(2,1)}), bf16[64,2,512,128]{3,2,1,0:T(8,128)(2,1)}, u32[]{:S(2)}, u32[]{:S(2)}) async-start(bf16[64,2,512,128]{3,2,1,0:T(8,128)(2,1)} %shard_map.46), calls=%async_computation | async-start | bytes 33554432 | tf_op jit(solution)/shard_map/all_to_all | solution.py:216
  24.7 0.0 copy-done.1
  24.7 0.7 fusion
  25.4 0.1 reshape.12.live_ref
  25.5 0.1 max.6.slot_ref
  25.6 371.3 %all-to-all-done.received_ref = bf16[64,2,512,128]{3,2,1,0:T(8,128)(2,1)} async-done(((bf16[64,2,512,128]{3,2,1,0:T(8,128)(2,1)}), bf16[64,2,512,128]{3,2,1,0:T(8,128)(2,1)}, u32[]{:S(2)}, u32[]{:S(2)}) %all-to-all-start) | async-done | bytes 16777248 | tf_op jit(solution)/shard_map/all_to_all | solution.py:216
  396.9 0.0 copy-done
  396.9 58.1 %shard_map.47 = bf16[512,2048]{1,0:T(8,128)(2,1)S(1)} custom-call(s32[32]{0:T(128)S(1)} %max.6.slot_ref, s32[32]{0:T(128)S(1)} %reshape.12.live_ref, bf16[512,2048]{1,0:T(8,128)(2,1)S(1)} %bitcast.9, bf16[512,2048]{1,0:T(8,128)(2,1)} %bitcast.11, bf16[512,2048]{1,0:T(8,128)(2,1)} %bitcast.13, bf16[64,2,512,128]{3,2,1,0:T(8,128)(2,1)} %all-to-all-done.received_ref), custom_call_target="tpu_custom_call" | custom-call | tf_op jit(solution)/shard_map/pallas_call | solution.py:200
  455.0 1.3 copy.6
Async XLA Ops:
  12.6 12.1 %copy-start.1 = (s32[1,64,16,2]{1,3,2,0:T(2,128)S(1)}, s32[1,64,16,2]{1,3,2,0:T(2,128)}, u32[]{:S(2)}) copy-start(s32[1,64,16,2]{1,3,2,0:T(2,128)} %param.7) | copy-start | bytes 24580
  12.6 384.3 %copy-start = (bf16[1,512,2048]{2,1,0:T(8,128)(2,1)S(1)}, bf16[1,512,2048]{2,1,0:T(8,128)(2,1)}, u32[]{:S(2)}) copy-start(bf16[1,512,2048]{2,1,0:T(8,128)(2,1)} %param.4) | copy-start | bytes 6291460
  12.6 384.3 %all-to-all-start = ((bf16[64,2,512,128]{3,2,1,0:T(8,128)(2,1)}), bf16[64,2,512,128]{3,2,1,0:T(8,128)(2,1)}, u32[]{:S(2)}, u32[]{:S(2)}) async-start(bf16[64,2,512,128]{3,2,1,0:T(8,128)(2,1)} %shard_map.46), calls=%async_computation | async-start | bytes 33554432 | tf_op jit(solution)/shard_map/all_to_all | solution.py:216

commit v14 on v13

--- a/solution.py
+++ b/solution.py
@@ -125,37 +125,41 @@
 
     score_scale = HD ** (-0.5)
     dims = (((1,), (1,)), ((), ()))
-    query = q_ref[...]
-
-    def scores_against(key_rows):
-        raw = lax.dot_general(query, key_rows, dims, preferred_element_type=jnp.float32)
-        return raw * score_scale
-
-    row_index = lax.broadcasted_iota(jnp.int32, (rows, rows), 0)
-    col_index = lax.broadcasted_iota(jnp.int32, (rows, rows), 1)
-    own = jnp.where(row_index >= col_index, scores_against(k_ref[...]), -jnp.inf)
     first_bias = jnp.where(live_ref[PICKS * head] > 0, 0.0, -jnp.inf)
     second_bias = jnp.where(live_ref[PICKS * head + 1] > 0, 0.0, -jnp.inf)
     first_block = received_ref[slot_ref[PICKS * head]]
     second_block = received_ref[slot_ref[PICKS * head + 1]]
-    first = scores_against(first_block[0]) + first_bias
-    second = scores_against(second_block[0]) + second_bias
-    row_top = jnp.maximum(
-        jnp.maximum(jnp.max(own, axis=1), jnp.max(first, axis=1)), jnp.max(second, axis=1)
-    )[:, None]
-    own = jnp.exp(own - row_top)
-    first = jnp.exp(first - row_top)
-    second = jnp.exp(second - row_top)
-    row_scale = 1.0 / (
-        jnp.sum(own, axis=1) + jnp.sum(first, axis=1) + jnp.sum(second, axis=1)
-    )[:, None]
-    mixed = jnp.dot((own * row_scale).astype(jnp.bfloat16), v_ref[...],
-                    preferred_element_type=jnp.float32)
-    mixed += jnp.dot((first * row_scale).astype(jnp.bfloat16), first_block[1],
-                     preferred_element_type=jnp.float32)
-    mixed += jnp.dot((second * row_scale).astype(jnp.bfloat16), second_block[1],
-                     preferred_element_type=jnp.float32)
-    out_buf[head] = mixed.astype(out_buf.dtype)
+    half = rows // 2
+    for part in range(2):
+        low = part * half
+        width = low + half
+        query = q_ref[low:low + half, :]
+
+        def scores_against(key_rows, query=query):
+            raw = lax.dot_general(query, key_rows, dims, preferred_element_type=jnp.float32)
+            return raw * score_scale
+
+        row_index = lax.broadcasted_iota(jnp.int32, (half, width), 0) + low
+        col_index = lax.broadcasted_iota(jnp.int32, (half, width), 1)
+        own = jnp.where(row_index >= col_index, scores_against(k_ref[:width, :]), -jnp.inf)
+        first = scores_against(first_block[0]) + first_bias
+        second = scores_against(second_block[0]) + second_bias
+        row_top = jnp.maximum(
+            jnp.maximum(jnp.max(own, axis=1), jnp.max(first, axis=1)), jnp.max(second, axis=1)
+        )[:, None]
+        own = jnp.exp(own - row_top)
+        first = jnp.exp(first - row_top)
+        second = jnp.exp(second - row_top)
+        row_scale = 1.0 / (
+            jnp.sum(own, axis=1) + jnp.sum(first, axis=1) + jnp.sum(second, axis=1)
+        )[:, None]
+        mixed = jnp.dot((own * row_scale).astype(jnp.bfloat16), v_ref[:width, :],
+                        preferred_element_type=jnp.float32)
+        mixed += jnp.dot((first * row_scale).astype(jnp.bfloat16), first_block[1],
+                         preferred_element_type=jnp.float32)
+        mixed += jnp.dot((second * row_scale).astype(jnp.bfloat16), second_block[1],
+                         preferred_element_type=jnp.float32)
+        out_buf[head, low:low + half, :] = mixed.astype(out_buf.dtype)
 
     def relay(slot):
         return pltpu.make_async_remote_copy(

time: 457 us -> 456 us (level)
  no operation moved by 1% of the time
where the time goes in v14:
time: 456 us
  waiting for transfers between devices  371 us (81%)
  Pallas kernels  69 us (15%)
  starting transfers between devices  12.1 us (3%)
    all_to_all x1, waiting for transfers between devices, per_device(): lax.all_to_all(send, 'ctx', split_axis=0, concat_axis=0, tiled=True)  371 us
    pallas_call x1, Pallas kernels, attend_and_pass(): pl.pallas_call(attend_kernel, grid_spec=grid_spec, out_shape=jax.ShapeDty...  57.6 us
    all_to_all x1, starting transfers between devices, per_device(): lax.all_to_all(send, 'ctx', split_axis=0, concat_axis=0, tiled=True)  12.1 us
    pallas_call x1, Pallas kernels, pack_requested(): pl.pallas_call(functools.partial(pack_kernel, group), grid_spec=grid_spec...  11.4 us
  transfers between devices with their start and end apart: 1, of which 1 were waited for; matrix products, arithmetic and copies ran while one was open for 0% of the time, Pallas kernels for 0%

profile of v14, /device:TPU:48, one launch (start us, length us, event | category | flops | bytes accessed | tf_op | source)
XLA Modules:
  0.0 455.9 jit_solution(13367708041922246544)
XLA Ops:
  0.0 1.3 fusion.1.asked_ref
  1.3 11.4 %shard_map.46 = bf16[64,2,512,128]{3,2,1,0:T(8,128)(2,1)} custom-call(s32[64]{0:T(128)} %fusion.1.asked_ref, bf16[512,2048]{1,0:T(8,128)(2,1)} %bitcast.10, bf16[512,2048]{1,0:T(8,128)(2,1)} %bitcast.12), custom_call_target="tpu_custom_call" | custom-call | tf_op jit(solution)/shard_map/pallas_call | solution.py:41
  12.6 0.0 copy-start.1
  12.6 0.0 copy-start
  12.6 12.1 %all-to-all-start = ((bf16[64,2,512,128]{3,2,1,0:T(8,128)(2,1)}), bf16[64,2,512,128]{3,2,1,0:T(8,128)(2,1)}, u32[]{:S(2)}, u32[]{:S(2)}) async-start(bf16[64,2,512,128]{3,2,1,0:T(8,128)(2,1)} %shard_map.46), calls=%async_computation | async-start | bytes 33554432 | tf_op jit(solution)/shard_map/all_to_all | solution.py:220
  24.7 0.0 copy-done.1
  24.7 0.7 fusion
  25.4 0.1 reshape.12.live_ref
  25.5 0.1 max.6.slot_ref
  25.6 371.3 %all-to-all-done.received_ref = bf16[64,2,512,128]{3,2,1,0:T(8,128)(2,1)} async-done(((bf16[64,2,512,128]{3,2,1,0:T(8,128)(2,1)}), bf16[64,2,512,128]{3,2,1,0:T(8,128)(2,1)}, u32[]{:S(2)}, u32[]{:S(2)}) %all-to-all-start) | async-done | bytes 16777248 | tf_op jit(solution)/shard_map/all_to_all | solution.py:220
  396.9 0.0 copy-done
  396.9 57.6 %shard_map.47 = bf16[512,2048]{1,0:T(8,128)(2,1)S(1)} custom-call(s32[32]{0:T(128)S(1)} %max.6.slot_ref, s32[32]{0:T(128)S(1)} %reshape.12.live_ref, bf16[512,2048]{1,0:T(8,128)(2,1)S(1)} %bitcast.9, bf16[512,2048]{1,0:T(8,128)(2,1)} %bitcast.11, bf16[512,2048]{1,0:T(8,128)(2,1)} %bitcast.13, bf16[64,2,512,128]{3,2,1,0:T(8,128)(2,1)} %all-to-all-done.received_ref), custom_call_target="tpu_custom_call" | custom-call | tf_op jit(solution)/shard_map/pallas_call | solution.py:204
  454.5 1.3 copy.6
Async XLA Ops:
  12.6 12.1 %copy-start.1 = (s32[1,64,16,2]{1,3,2,0:T(2,128)S(1)}, s32[1,64,16,2]{1,3,2,0:T(2,128)}, u32[]{:S(2)}) copy-start(s32[1,64,16,2]{1,3,2,0:T(2,128)} %param.7) | copy-start | bytes 24580
  12.6 384.3 %copy-start = (bf16[1,512,2048]{2,1,0:T(8,128)(2,1)S(1)}, bf16[1,512,2048]{2,1,0:T(8,128)(2,1)}, u32[]{:S(2)}) copy-start(bf16[1,512,2048]{2,1,0:T(8,128)(2,1)} %param.4) | copy-start | bytes 6291460
  12.6 384.3 %all-to-all-start = ((bf16[64,2,512,128]{3,2,1,0:T(8,128)(2,1)}), bf16[64,2,512,128]{3,2,1,0:T(8,128)(2,1)}, u32[]{:S(2)}, u32[]{:S(2)}) async-start(bf16[64,2,512,128]{3,2,1,0:T(8,128)(2,1)} %shard_map.46), calls=%async_computation | async-start | bytes 33554432 | tf_op jit(solution)/shard_map/all_to_all | solution.py:220

commit v15 on v14

--- a/solution.py
+++ b/solution.py
@@ -19,30 +19,28 @@
     return lax.ppermute(value, axis, pairs)
 
 
-def pack_kernel(group, asked_ref, k_ref, v_ref, out_ref):
+def pack_kernel(group, asked_ref, source_ref, out_ref):
     base = pl.program_id(0) * group
     for i in range(group):
         column = pl.multiple_of(asked_ref[base + i] * HD, HD)
-        out_ref[i, 0] = k_ref[:, pl.ds(column, HD)]
-        out_ref[i, 1] = v_ref[:, pl.ds(column, HD)]
-
-
-def pack_requested(asked, keys, values):
+        out_ref[i] = source_ref[:, pl.ds(column, HD)]
+
+
+def pack_requested(asked, source):
     count = asked.shape[0]
-    rows, width = keys.shape
+    rows, width = source.shape
     group = 8
-    whole = pl.BlockSpec((rows, width), lambda g, asked_ref: (0, 0))
     grid_spec = pltpu.PrefetchScalarGridSpec(
         num_scalar_prefetch=1,
         grid=(count // group,),
-        in_specs=[whole, whole],
-        out_specs=pl.BlockSpec((group, 2, rows, HD), lambda g, asked_ref: (g, 0, 0, 0)),
+        in_specs=[pl.BlockSpec((rows, width), lambda g, asked_ref: (0, 0))],
+        out_specs=pl.BlockSpec((group, rows, HD), lambda g, asked_ref: (g, 0, 0)),
     )
     return pl.pallas_call(
         functools.partial(pack_kernel, group),
         grid_spec=grid_spec,
-        out_shape=jax.ShapeDtypeStruct((count, 2, rows, HD), keys.dtype),
-    )(asked, keys, values)
+        out_shape=jax.ShapeDtypeStruct((count, rows, HD), source.dtype),
+    )(asked, source)
 
 
 def exchange_kernel(count, send_ref, recv_ref, send_sems, recv_sems):
@@ -107,7 +105,8 @@
     )(send)
 
 
-def attend_kernel(slot_ref, live_ref, q_ref, k_ref, v_ref, received_ref, o_ref, out_buf, sems):
+def attend_kernel(slot_ref, live_ref, q_ref, k_ref, v_ref, got_keys_ref, got_values_ref, o_ref,
+                  out_buf, sems):
     head = pl.program_id(0)
     heads = pl.num_programs(0)
     rows = q_ref.shape[0]
@@ -127,8 +126,10 @@
     dims = (((1,), (1,)), ((), ()))
     first_bias = jnp.where(live_ref[PICKS * head] > 0, 0.0, -jnp.inf)
     second_bias = jnp.where(live_ref[PICKS * head + 1] > 0, 0.0, -jnp.inf)
-    first_block = received_ref[slot_ref[PICKS * head]]
-    second_block = received_ref[slot_ref[PICKS * head + 1]]
+    first_slot = slot_ref[PICKS * head]
+    second_slot = slot_ref[PICKS * head + 1]
+    first_block = (got_keys_ref[first_slot], got_values_ref[first_slot])
+    second_block = (got_keys_ref[second_slot], got_values_ref[second_slot])
     half = rows // 2
     for part in range(2):
         low = part * half
@@ -183,7 +184,7 @@
         lax.fori_loop(0, heads, finish, 0)
 
 
-def attend_and_pass(slots, live, queries, keys, values, received):
+def attend_and_pass(slots, live, queries, keys, values, got_keys, got_values):
     rows = queries.shape[0]
     head_block = pl.BlockSpec((rows, HD), lambda h, slot_ref, live_ref: (0, h))
     grid_spec = pltpu.PrefetchScalarGridSpec(
@@ -194,6 +195,7 @@
             head_block,
             head_block,
             pl.BlockSpec(memory_space=pltpu.VMEM),
+            pl.BlockSpec(memory_space=pltpu.VMEM),
         ],
         out_specs=pl.BlockSpec(memory_space=pl.ANY),
         scratch_shapes=[
@@ -208,7 +210,7 @@
         compiler_params=pltpu.CompilerParams(
             collective_id=0, has_side_effects=True, vmem_limit_bytes=48 * 1024 * 1024
         ),
-    )(slots, live, queries, keys, values, received)
+    )(slots, live, queries, keys, values, got_keys, got_values)
 
 
 def per_device(queries, keys, values, picks):
@@ -216,12 +218,15 @@
     every_pick = picks[0]
     head_ids = lax.broadcasted_iota(jnp.int32, every_pick.shape, 1)
     asked = jnp.sum(jnp.where(every_pick == rank_here, head_ids, 0), axis=(1, 2))
-    send = pack_requested(asked.astype(jnp.int32), keys[0], values[0])
-    received = lax.all_to_all(send, "ctx", split_axis=0, concat_axis=0, tiled=True)
+    asked = asked.astype(jnp.int32)
+    got_keys = lax.all_to_all(pack_requested(asked, keys[0]), "ctx", split_axis=0, concat_axis=0,
+                              tiled=True)
+    got_values = lax.all_to_all(pack_requested(asked, values[0]), "ctx", split_axis=0,
+                                concat_axis=0, tiled=True)
     chosen = lax.dynamic_index_in_dim(every_pick, rank_here, 0, keepdims=False).reshape(-1)
     live = (chosen >= 0).astype(jnp.int32)
     slots = jnp.maximum(chosen, 0).astype(jnp.int32)
-    merged = attend_and_pass(slots, live, queries[0], keys[0], values[0], received)
+    merged = attend_and_pass(slots, live, queries[0], keys[0], values[0], got_keys, got_values)
     return merged[None]
 
 

time: 456 us -> 459 us (level)
  waiting for transfers between devices: 371 us -> 364 us
  starting transfers between devices: 12.1 us -> 18.2 us
    all_to_all x1 -> x2, waiting for transfers between devices: 371 us -> 364 us  [the longest x1 185 us: per_device(): lax.all_to_all(pack_requested(asked, values[0]), 'ctx', split_axis=0, con...]
    all_to_all x1 -> x2, starting transfers between devices: 12.1 us -> 18.2 us  [the longest x1 11.8 us: per_device(): lax.all_to_all(pack_requested(asked, keys[0]), 'ctx', split_axis=0, conca...]
    pallas_call x1 -> x2, Pallas kernels: 11.4 us -> 15.5 us  [pack_requested(): pl.pallas_call(functools.partial(pack_kernel, group), grid_spec=grid_spec...]
  transfers between devices with their start and end apart: 1 -> 2, of which waited for: 1 -> 2; matrix products, arithmetic and copies ran while one was open for 0% -> 0% of each run, Pallas kernels for 0% -> 2%
where the time goes in v15:
time: 459 us
  waiting for transfers between devices  364 us (79%)
  Pallas kernels  73.1 us (16%)
  starting transfers between devices  18.2 us (4%)
    all_to_all x1, waiting for transfers between devices, per_device(): lax.all_to_all(pack_requested(asked, values[0]), 'ctx', split_axis=0, con...  185 us
    all_to_all x1, waiting for transfers between devices, per_device(): lax.all_to_all(pack_requested(asked, keys[0]), 'ctx', split_axis=0, conca...  178 us
    pallas_call x1, Pallas kernels, attend_and_pass(): pl.pallas_call(attend_kernel, grid_spec=grid_spec, out_shape=jax.ShapeDty...  57.6 us
    pallas_call x2, Pallas kernels, pack_requested(): pl.pallas_call(functools.partial(pack_kernel, group), grid_spec=grid_spec...  15.5 us
    all_to_all x1, starting transfers between devices, per_device(): lax.all_to_all(pack_requested(asked, keys[0]), 'ctx', split_axis=0, conca...  11.8 us
  transfers between devices with their start and end apart: 2, of which 2 were waited for; matrix products, arithmetic and copies ran while one was open for 0% of the time, Pallas kernels for 2%

profile of v15, /device:TPU:48, one launch (start us, length us, event | category | flops | bytes accessed | tf_op | source)
XLA Modules:
  0.0 458.6 jit_solution(10593674549143989031)
XLA Ops:
  0.0 1.3 fusion.1.asked_ref
  1.3 7.8 %shard_map.46 = bf16[64,512,128]{2,1,0:T(8,128)(2,1)} custom-call(s32[64]{0:T(128)} %fusion.1.asked_ref, bf16[512,2048]{1,0:T(8,128)(2,1)} %bitcast.10), custom_call_target="tpu_custom_call" | custom-call | tf_op jit(solution)/shard_map/pallas_call | solution.py:39
  9.1 11.8 %all-to-all-start = ((bf16[64,512,128]{2,1,0:T(8,128)(2,1)}), bf16[64,512,128]{2,1,0:T(8,128)(2,1)}, u32[]{:S(2)}, u32[]{:S(2)}) async-start(bf16[64,512,128]{2,1,0:T(8,128)(2,1)} %shard_map.46), calls=%async_computation | async-start | bytes 16777216 | tf_op jit(solution)/shard_map/all_to_all | solution.py:222
  20.9 7.7 %shard_map.47 = bf16[64,512,128]{2,1,0:T(8,128)(2,1)} custom-call(s32[64]{0:T(128)} %fusion.1.asked_ref, bf16[512,2048]{1,0:T(8,128)(2,1)} %bitcast.12), custom_call_target="tpu_custom_call" | custom-call | tf_op jit(solution)/shard_map/pallas_call | solution.py:39
  28.6 0.0 copy-start.1
  28.6 0.0 copy-start
  28.6 178.5 %all-to-all-done.got_keys_ref = bf16[64,512,128]{2,1,0:T(8,128)(2,1)} async-done(((bf16[64,512,128]{2,1,0:T(8,128)(2,1)}), bf16[64,512,128]{2,1,0:T(8,128)(2,1)}, u32[]{:S(2)}, u32[]{:S(2)}) %all-to-all-start) | async-done | bytes 8388640 | tf_op jit(solution)/shard_map/all_to_all | solution.py:222
  207.0 6.5 %all-to-all-start.1 = ((bf16[64,512,128]{2,1,0:T(8,128)(2,1)}), bf16[64,512,128]{2,1,0:T(8,128)(2,1)}, u32[]{:S(2)}, u32[]{:S(2)}) async-start(bf16[64,512,128]{2,1,0:T(8,128)(2,1)} %shard_map.47), calls=%async_computation.1 | async-start | bytes 16777216 | tf_op jit(solution)/shard_map/all_to_all | solution.py:224
  213.5 0.0 copy-done.1
  213.5 0.7 fusion
  214.2 0.1 reshape.12.live_ref
  214.3 0.1 max.6.slot_ref
  214.4 185.3 %all-to-all-done.1.got_values_ref = bf16[64,512,128]{2,1,0:T(8,128)(2,1)} async-done(((bf16[64,512,128]{2,1,0:T(8,128)(2,1)}), bf16[64,512,128]{2,1,0:T(8,128)(2,1)}, u32[]{:S(2)}, u32[]{:S(2)}) %all-to-all-start.1) | async-done | bytes 8388640 | tf_op jit(solution)/shard_map/all_to_all | solution.py:224
  399.7 0.0 copy-done
  399.7 57.6 %shard_map.48 = bf16[512,2048]{1,0:T(8,128)(2,1)S(1)} custom-call(s32[32]{0:T(128)S(1)} %max.6.slot_ref, s32[32]{0:T(128)S(1)} %reshape.12.live_ref, bf16[512,2048]{1,0:T(8,128)(2,1)S(1)} %bitcast.9, bf16[512,2048]{1,0:T(8,128)(2,1)} %bitcast.11, bf16[512,2048]{1,0:T(8,128)(2,1)} %bitcast.13, bf16[64,512,128]{2,1,0:T(8,128)(2,1)} %all-to-all-done.got_keys_ref, ...), custom_call_target="tpu_custom_call" | custom-call | tf_op jit(solution)/shard_map/pallas_call | solution.py:206
  457.3 1.3 copy.6
Async XLA Ops:
  9.1 198.0 %all-to-all-start = ((bf16[64,512,128]{2,1,0:T(8,128)(2,1)}), bf16[64,512,128]{2,1,0:T(8,128)(2,1)}, u32[]{:S(2)}, u32[]{:S(2)}) async-start(bf16[64,512,128]{2,1,0:T(8,128)(2,1)} %shard_map.46), calls=%async_computation | async-start | bytes 16777216 | tf_op jit(solution)/shard_map/all_to_all | solution.py:222
  28.6 184.9 %copy-start.1 = (s32[1,64,16,2]{1,3,2,0:T(2,128)S(1)}, s32[1,64,16,2]{1,3,2,0:T(2,128)}, u32[]{:S(2)}) copy-start(s32[1,64,16,2]{1,3,2,0:T(2,128)} %param.7) | copy-start | bytes 24580
  28.6 371.1 %copy-start = (bf16[1,512,2048]{2,1,0:T(8,128)(2,1)S(1)}, bf16[1,512,2048]{2,1,0:T(8,128)(2,1)}, u32[]{:S(2)}) copy-start(bf16[1,512,2048]{2,1,0:T(8,128)(2,1)} %param.4) | copy-start | bytes 6291460
  207.0 192.6 %all-to-all-start.1 = ((bf16[64,512,128]{2,1,0:T(8,128)(2,1)}), bf16[64,512,128]{2,1,0:T(8,128)(2,1)}, u32[]{:S(2)}, u32[]{:S(2)}) async-start(bf16[64,512,128]{2,1,0:T(8,128)(2,1)} %shard_map.47), calls=%async_computation.1 | async-start | bytes 16777216 | tf_op jit(solution)/shard_map/all_to_all | solution.py:224

commit v16 on v14

--- a/solution.py
+++ b/solution.py
@@ -30,7 +30,7 @@
 def pack_requested(asked, keys, values):
     count = asked.shape[0]
     rows, width = keys.shape
-    group = 8
+    group = 16
     whole = pl.BlockSpec((rows, width), lambda g, asked_ref: (0, 0))
     grid_spec = pltpu.PrefetchScalarGridSpec(
         num_scalar_prefetch=1,

time: 456 us -> 456 us (level)
  no operation moved by 1% of the time
where the time goes in v16:
time: 456 us
  waiting for transfers between devices  371 us (81%)
  Pallas kernels  68.5 us (15%)
  starting transfers between devices  12.5 us (3%)
    all_to_all x1, waiting for transfers between devices, per_device(): lax.all_to_all(send, 'ctx', split_axis=0, concat_axis=0, tiled=True)  371 us
    pallas_call x1, Pallas kernels, attend_and_pass(): pl.pallas_call(attend_kernel, grid_spec=grid_spec, out_shape=jax.ShapeDty...  57.6 us
    all_to_all x1, starting transfers between devices, per_device(): lax.all_to_all(send, 'ctx', split_axis=0, concat_axis=0, tiled=True)  12.5 us
    pallas_call x1, Pallas kernels, pack_requested(): pl.pallas_call(functools.partial(pack_kernel, group), grid_spec=grid_spec...  10.9 us
  transfers between devices with their start and end apart: 1, of which 1 were waited for; matrix products, arithmetic and copies ran while one was open for 0% of the time, Pallas kernels for 0%

profile of v16, /device:TPU:48, one launch (start us, length us, event | category | flops | bytes accessed | tf_op | source)
XLA Modules:
  0.0 455.7 jit_solution(415427471623358826)
XLA Ops:
  0.0 1.3 fusion.1.asked_ref
  1.3 10.9 %shard_map.46 = bf16[64,2,512,128]{3,2,1,0:T(8,128)(2,1)} custom-call(s32[64]{0:T(128)} %fusion.1.asked_ref, bf16[512,2048]{1,0:T(8,128)(2,1)} %bitcast.10, bf16[512,2048]{1,0:T(8,128)(2,1)} %bitcast.12), custom_call_target="tpu_custom_call" | custom-call | tf_op jit(solution)/shard_map/pallas_call | solution.py:41
  12.1 0.0 copy-start.1
  12.1 0.0 copy-start
  12.1 12.5 %all-to-all-start = ((bf16[64,2,512,128]{3,2,1,0:T(8,128)(2,1)}), bf16[64,2,512,128]{3,2,1,0:T(8,128)(2,1)}, u32[]{:S(2)}, u32[]{:S(2)}) async-start(bf16[64,2,512,128]{3,2,1,0:T(8,128)(2,1)} %shard_map.46), calls=%async_computation | async-start | bytes 33554432 | tf_op jit(solution)/shard_map/all_to_all | solution.py:220
  24.6 0.0 copy-done.1
  24.6 0.7 fusion
  25.3 0.1 reshape.12.live_ref
  25.4 0.1 max.6.slot_ref
  25.5 371.3 %all-to-all-done.received_ref = bf16[64,2,512,128]{3,2,1,0:T(8,128)(2,1)} async-done(((bf16[64,2,512,128]{3,2,1,0:T(8,128)(2,1)}), bf16[64,2,512,128]{3,2,1,0:T(8,128)(2,1)}, u32[]{:S(2)}, u32[]{:S(2)}) %all-to-all-start) | async-done | bytes 16777248 | tf_op jit(solution)/shard_map/all_to_all | solution.py:220
  396.8 0.0 copy-done
  396.8 57.6 %shard_map.47 = bf16[512,2048]{1,0:T(8,128)(2,1)S(1)} custom-call(s32[32]{0:T(128)S(1)} %max.6.slot_ref, s32[32]{0:T(128)S(1)} %reshape.12.live_ref, bf16[512,2048]{1,0:T(8,128)(2,1)S(1)} %bitcast.9, bf16[512,2048]{1,0:T(8,128)(2,1)} %bitcast.11, bf16[512,2048]{1,0:T(8,128)(2,1)} %bitcast.13, bf16[64,2,512,128]{3,2,1,0:T(8,128)(2,1)} %all-to-all-done.received_ref), custom_call_target="tpu_custom_call" | custom-call | tf_op jit(solution)/shard_map/pallas_call | solution.py:204
  454.4 1.3 copy.6
Async XLA Ops:
  12.1 12.5 %copy-start.1 = (s32[1,64,16,2]{1,3,2,0:T(2,128)S(1)}, s32[1,64,16,2]{1,3,2,0:T(2,128)}, u32[]{:S(2)}) copy-start(s32[1,64,16,2]{1,3,2,0:T(2,128)} %param.7) | copy-start | bytes 24580
  12.1 384.7 %copy-start = (bf16[1,512,2048]{2,1,0:T(8,128)(2,1)S(1)}, bf16[1,512,2048]{2,1,0:T(8,128)(2,1)}, u32[]{:S(2)}) copy-start(bf16[1,512,2048]{2,1,0:T(8,128)(2,1)} %param.4) | copy-start | bytes 6291460
  12.1 384.7 %all-to-all-start = ((bf16[64,2,512,128]{3,2,1,0:T(8,128)(2,1)}), bf16[64,2,512,128]{3,2,1,0:T(8,128)(2,1)}, u32[]{:S(2)}, u32[]{:S(2)}) async-start(bf16[64,2,512,128]{3,2,1,0:T(8,128)(2,1)} %shard_map.46), calls=%async_computation | async-start | bytes 33554432 | tf_op jit(solution)/shard_map/all_to_all | solution.py:220

commit v17 on v13

--- a/solution.py
+++ b/solution.py
@@ -108,54 +108,21 @@
 
 
 def attend_kernel(slot_ref, live_ref, q_ref, k_ref, v_ref, received_ref, o_ref, out_buf, sems):
-    head = pl.program_id(0)
-    heads = pl.num_programs(0)
+    step = pl.program_id(0)
+    steps = pl.num_programs(0)
+    heads = out_buf.shape[0]
     rows = q_ref.shape[0]
     pipe_size = lax.axis_size("pipe")
     here = lax.axis_index("pipe")
     after = lax.rem(here + 1, pipe_size)
     before = lax.rem(here + pipe_size - 1, pipe_size)
 
-    @pl.when(head == 0)
+    @pl.when(step == 0)
     def _():
         barrier = pltpu.get_barrier_semaphore()
         for peer in (before, after):
             pl.semaphore_signal(barrier, 1, device_id={"pipe": peer}, device_id_type=MESH)
         pl.semaphore_wait(barrier, 2)
-
-    score_scale = HD ** (-0.5)
-    dims = (((1,), (1,)), ((), ()))
-    query = q_ref[...]
-
-    def scores_against(key_rows):
-        raw = lax.dot_general(query, key_rows, dims, preferred_element_type=jnp.float32)
-        return raw * score_scale
-
-    row_index = lax.broadcasted_iota(jnp.int32, (rows, rows), 0)
-    col_index = lax.broadcasted_iota(jnp.int32, (rows, rows), 1)
-    own = jnp.where(row_index >= col_index, scores_against(k_ref[...]), -jnp.inf)
-    first_bias = jnp.where(live_ref[PICKS * head] > 0, 0.0, -jnp.inf)
-    second_bias = jnp.where(live_ref[PICKS * head + 1] > 0, 0.0, -jnp.inf)
-    first_block = received_ref[slot_ref[PICKS * head]]
-    second_block = received_ref[slot_ref[PICKS * head + 1]]
-    first = scores_against(first_block[0]) + first_bias
-    second = scores_against(second_block[0]) + second_bias
-    row_top = jnp.maximum(
-        jnp.maximum(jnp.max(own, axis=1), jnp.max(first, axis=1)), jnp.max(second, axis=1)
-    )[:, None]
-    own = jnp.exp(own - row_top)
-    first = jnp.exp(first - row_top)
-    second = jnp.exp(second - row_top)
-    row_scale = 1.0 / (
-        jnp.sum(own, axis=1) + jnp.sum(first, axis=1) + jnp.sum(second, axis=1)
-    )[:, None]
-    mixed = jnp.dot((own * row_scale).astype(jnp.bfloat16), v_ref[...],
-                    preferred_element_type=jnp.float32)
-    mixed += jnp.dot((first * row_scale).astype(jnp.bfloat16), first_block[1],
-                     preferred_element_type=jnp.float32)
-    mixed += jnp.dot((second * row_scale).astype(jnp.bfloat16), second_block[1],
-                     preferred_element_type=jnp.float32)
-    out_buf[head] = mixed.astype(out_buf.dtype)
 
     def relay(slot):
         return pltpu.make_async_remote_copy(
@@ -167,9 +134,52 @@
             device_id_type=MESH,
         )
 
-    relay(head).start()
-
-    @pl.when(head == heads - 1)
+    score_scale = HD ** (-0.5)
+    dims = (((1,), (1,)), ((), ()))
+    per_step = q_ref.shape[1] // HD
+    for inner in range(per_step):
+        slot = step * per_step + inner
+        lanes = slice(inner * HD, (inner + 1) * HD)
+        first_bias = jnp.where(live_ref[PICKS * slot] > 0, 0.0, -jnp.inf)
+        second_bias = jnp.where(live_ref[PICKS * slot + 1] > 0, 0.0, -jnp.inf)
+        first_block = received_ref[slot_ref[PICKS * slot]]
+        second_block = received_ref[slot_ref[PICKS * slot + 1]]
+        half = rows // 2
+        for part in range(2):
+            low = part * half
+            width = low + half
+            query = q_ref[low:low + half, lanes]
+
+            def scores_against(key_rows, query=query):
+                raw = lax.dot_general(query, key_rows, dims, preferred_element_type=jnp.float32)
+                return raw * score_scale
+
+            row_index = lax.broadcasted_iota(jnp.int32, (half, width), 0) + low
+            col_index = lax.broadcasted_iota(jnp.int32, (half, width), 1)
+            own = jnp.where(row_index >= col_index, scores_against(k_ref[:width, lanes]),
+                            -jnp.inf)
+            first = scores_against(first_block[0]) + first_bias
+            second = scores_against(second_block[0]) + second_bias
+            row_top = jnp.maximum(
+                jnp.maximum(jnp.max(own, axis=1), jnp.max(first, axis=1)),
+                jnp.max(second, axis=1),
+            )[:, None]
+            own = jnp.exp(own - row_top)
+            first = jnp.exp(first - row_top)
+            second = jnp.exp(second - row_top)
+            row_scale = 1.0 / (
+                jnp.sum(own, axis=1) + jnp.sum(first, axis=1) + jnp.sum(second, axis=1)
+            )[:, None]
+            mixed = jnp.dot((own * row_scale).astype(jnp.bfloat16), v_ref[:width, lanes],
+                            preferred_element_type=jnp.float32)
+            mixed += jnp.dot((first * row_scale).astype(jnp.bfloat16), first_block[1],
+                             preferred_element_type=jnp.float32)
+            mixed += jnp.dot((second * row_scale).astype(jnp.bfloat16), second_block[1],
+                             preferred_element_type=jnp.float32)
+            out_buf[slot, low:low + half, :] = mixed.astype(out_buf.dtype)
+        relay(slot).start()
+
+    @pl.when(step == steps - 1)
     def _():
         def finish(slot, carry):
             relay(slot).wait_send()
@@ -181,10 +191,11 @@
 
 def attend_and_pass(slots, live, queries, keys, values, received):
     rows = queries.shape[0]
-    head_block = pl.BlockSpec((rows, HD), lambda h, slot_ref, live_ref: (0, h))
+    per_step = 2
+    head_block = pl.BlockSpec((rows, per_step * HD), lambda h, slot_ref, live_ref: (0, h))
     grid_spec = pltpu.PrefetchScalarGridSpec(
         num_scalar_prefetch=2,
-        grid=(HEADS,),
+        grid=(HEADS // per_step,),
         in_specs=[
             head_block,
             head_block,

time: 457 us -> 456 us (level)
  no operation moved by 1% of the time
where the time goes in v17:
time: 456 us
  waiting for transfers between devices  371 us (81%)
  Pallas kernels  69 us (15%)
  starting transfers between devices  12.1 us (3%)
    all_to_all x1, waiting for transfers between devices, per_device(): lax.all_to_all(send, 'ctx', split_axis=0, concat_axis=0, tiled=True)  371 us
    pallas_call x1, Pallas kernels, attend_and_pass(): pl.pallas_call(attend_kernel, grid_spec=grid_spec, out_shape=jax.ShapeDty...  57.7 us
    all_to_all x1, starting transfers between devices, per_device(): lax.all_to_all(send, 'ctx', split_axis=0, concat_axis=0, tiled=True)  12.1 us
    pallas_call x1, Pallas kernels, pack_requested(): pl.pallas_call(functools.partial(pack_kernel, group), grid_spec=grid_spec...  11.4 us
  transfers between devices with their start and end apart: 1, of which 1 were waited for; matrix products, arithmetic and copies ran while one was open for 0% of the time, Pallas kernels for 0%

profile of v17, /device:TPU:48, one launch (start us, length us, event | category | flops | bytes accessed | tf_op | source)
XLA Modules:
  0.0 455.9 jit_solution(10921745839593665214)
XLA Ops:
  0.0 1.3 fusion.1.asked_ref
  1.3 11.4 %shard_map.46 = bf16[64,2,512,128]{3,2,1,0:T(8,128)(2,1)} custom-call(s32[64]{0:T(128)} %fusion.1.asked_ref, bf16[512,2048]{1,0:T(8,128)(2,1)} %bitcast.10, bf16[512,2048]{1,0:T(8,128)(2,1)} %bitcast.12), custom_call_target="tpu_custom_call" | custom-call | tf_op jit(solution)/shard_map/pallas_call | solution.py:41
  12.6 0.0 copy-start.1
  12.6 0.0 copy-start
  12.6 12.1 %all-to-all-start = ((bf16[64,2,512,128]{3,2,1,0:T(8,128)(2,1)}), bf16[64,2,512,128]{3,2,1,0:T(8,128)(2,1)}, u32[]{:S(2)}, u32[]{:S(2)}) async-start(bf16[64,2,512,128]{3,2,1,0:T(8,128)(2,1)} %shard_map.46), calls=%async_computation | async-start | bytes 33554432 | tf_op jit(solution)/shard_map/all_to_all | solution.py:227
  24.7 0.0 copy-done.1
  24.7 0.7 fusion
  25.4 0.1 reshape.12.live_ref
  25.5 0.1 max.6.slot_ref
  25.6 371.3 %all-to-all-done.received_ref = bf16[64,2,512,128]{3,2,1,0:T(8,128)(2,1)} async-done(((bf16[64,2,512,128]{3,2,1,0:T(8,128)(2,1)}), bf16[64,2,512,128]{3,2,1,0:T(8,128)(2,1)}, u32[]{:S(2)}, u32[]{:S(2)}) %all-to-all-start) | async-done | bytes 16777248 | tf_op jit(solution)/shard_map/all_to_all | solution.py:227
  396.9 0.0 copy-done
  396.9 57.7 %shard_map.47 = bf16[512,2048]{1,0:T(8,128)(2,1)S(1)} custom-call(s32[32]{0:T(128)S(1)} %max.6.slot_ref, s32[32]{0:T(128)S(1)} %reshape.12.live_ref, bf16[512,2048]{1,0:T(8,128)(2,1)S(1)} %bitcast.9, bf16[512,2048]{1,0:T(8,128)(2,1)} %bitcast.11, bf16[512,2048]{1,0:T(8,128)(2,1)} %bitcast.13, bf16[64,2,512,128]{3,2,1,0:T(8,128)(2,1)} %all-to-all-done.received_ref), custom_call_target="tpu_custom_call" | custom-call | tf_op jit(solution)/shard_map/pallas_call | solution.py:211
  454.6 1.3 copy.6
Async XLA Ops:
  12.6 12.1 %copy-start.1 = (s32[1,64,16,2]{1,3,2,0:T(2,128)S(1)}, s32[1,64,16,2]{1,3,2,0:T(2,128)}, u32[]{:S(2)}) copy-start(s32[1,64,16,2]{1,3,2,0:T(2,128)} %param.7) | copy-start | bytes 24580
  12.6 384.3 %copy-start = (bf16[1,512,2048]{2,1,0:T(8,128)(2,1)S(1)}, bf16[1,512,2048]{2,1,0:T(8,128)(2,1)}, u32[]{:S(2)}) copy-start(bf16[1,512,2048]{2,1,0:T(8,128)(2,1)} %param.4) | copy-start | bytes 6291460
  12.6 384.3 %all-to-all-start = ((bf16[64,2,512,128]{3,2,1,0:T(8,128)(2,1)}), bf16[64,2,512,128]{3,2,1,0:T(8,128)(2,1)}, u32[]{:S(2)}, u32[]{:S(2)}) async-start(bf16[64,2,512,128]{3,2,1,0:T(8,128)(2,1)} %shard_map.46), calls=%async_computation | async-start | bytes 33554432 | tf_op jit(solution)/shard_map/all_to_all | solution.py:227

commit v18 on v14

--- a/solution.py
+++ b/solution.py
@@ -122,6 +122,17 @@
         for peer in (before, after):
             pl.semaphore_signal(barrier, 1, device_id={"pipe": peer}, device_id_type=MESH)
         pl.semaphore_wait(barrier, 2)
+
+    def relay(slot, part):
+        low = part * (rows // 2)
+        return pltpu.make_async_remote_copy(
+            src_ref=out_buf.at[slot, pl.ds(low, rows // 2)],
+            dst_ref=o_ref.at[pl.ds(low, rows // 2), pl.ds(pl.multiple_of(slot * HD, HD), HD)],
+            send_sem=sems.at[0, part, slot],
+            recv_sem=sems.at[1, part, slot],
+            device_id={"pipe": after},
+            device_id_type=MESH,
+        )
 
     score_scale = HD ** (-0.5)
     dims = (((1,), (1,)), ((), ()))
@@ -160,24 +171,14 @@
         mixed += jnp.dot((second * row_scale).astype(jnp.bfloat16), second_block[1],
                          preferred_element_type=jnp.float32)
         out_buf[head, low:low + half, :] = mixed.astype(out_buf.dtype)
-
-    def relay(slot):
-        return pltpu.make_async_remote_copy(
-            src_ref=out_buf.at[slot],
-            dst_ref=o_ref.at[:, pl.ds(pl.multiple_of(slot * HD, HD), HD)],
-            send_sem=sems.at[0, slot],
-            recv_sem=sems.at[1, slot],
-            device_id={"pipe": after},
-            device_id_type=MESH,
-        )
-
-    relay(head).start()
+        relay(head, part).start()
 
     @pl.when(head == heads - 1)
     def _():
         def finish(slot, carry):
-            relay(slot).wait_send()
-            relay(slot).wait_recv()
+            for part in range(2):
+                relay(slot, part).wait_send()
+                relay(slot, part).wait_recv()
             return carry
 
         lax.fori_loop(0, heads, finish, 0)
@@ -198,7 +199,7 @@
         out_specs=pl.BlockSpec(memory_space=pl.ANY),
         scratch_shapes=[
             pltpu.VMEM((HEADS, rows, HD), queries.dtype),
-            pltpu.SemaphoreType.DMA((2, HEADS)),
+            pltpu.SemaphoreType.DMA((2, 2, HEADS)),
         ],
     )
     return pl.pallas_call(

time: 456 us -> 456 us (level)
  no operation moved by 1% of the time
where the time goes in v18:
time: 456 us
  waiting for transfers between devices  371 us (81%)
  Pallas kernels  68.6 us (15%)
  starting transfers between devices  12.2 us (3%)
    all_to_all x1, waiting for transfers between devices, per_device(): lax.all_to_all(send, 'ctx', split_axis=0, concat_axis=0, tiled=True)  371 us
    pallas_call x1, Pallas kernels, attend_and_pass(): pl.pallas_call(attend_kernel, grid_spec=grid_spec, out_shape=jax.ShapeDty...  57.4 us
    all_to_all x1, starting transfers between devices, per_device(): lax.all_to_all(send, 'ctx', split_axis=0, concat_axis=0, tiled=True)  12.2 us
    pallas_call x1, Pallas kernels, pack_requested(): pl.pallas_call(functools.partial(pack_kernel, group), grid_spec=grid_spec...  11.3 us
  transfers between devices with their start and end apart: 1, of which 1 were waited for; matrix products, arithmetic and copies ran while one was open for 0% of the time, Pallas kernels for 0%

profile of v18, /device:TPU:48, one launch (start us, length us, event | category | flops | bytes accessed | tf_op | source)
XLA Modules:
  0.0 455.6 jit_solution(17916015862795358335)
XLA Ops:
  0.0 1.3 fusion.1.asked_ref
  1.3 11.3 %shard_map.46 = bf16[64,2,512,128]{3,2,1,0:T(8,128)(2,1)} custom-call(s32[64]{0:T(128)} %fusion.1.asked_ref, bf16[512,2048]{1,0:T(8,128)(2,1)} %bitcast.10, bf16[512,2048]{1,0:T(8,128)(2,1)} %bitcast.12), custom_call_target="tpu_custom_call" | custom-call | tf_op jit(solution)/shard_map/pallas_call | solution.py:41
  12.5 0.0 copy-start.1
  12.5 0.0 copy-start
  12.5 12.2 %all-to-all-start = ((bf16[64,2,512,128]{3,2,1,0:T(8,128)(2,1)}), bf16[64,2,512,128]{3,2,1,0:T(8,128)(2,1)}, u32[]{:S(2)}, u32[]{:S(2)}) async-start(bf16[64,2,512,128]{3,2,1,0:T(8,128)(2,1)} %shard_map.46), calls=%async_computation | async-start | bytes 33554432 | tf_op jit(solution)/shard_map/all_to_all | solution.py:221
  24.7 0.0 copy-done.1
  24.7 0.7 fusion
  25.4 0.1 reshape.12.live_ref
  25.5 0.1 max.6.slot_ref
  25.6 371.3 %all-to-all-done.received_ref = bf16[64,2,512,128]{3,2,1,0:T(8,128)(2,1)} async-done(((bf16[64,2,512,128]{3,2,1,0:T(8,128)(2,1)}), bf16[64,2,512,128]{3,2,1,0:T(8,128)(2,1)}, u32[]{:S(2)}, u32[]{:S(2)}) %all-to-all-start) | async-done | bytes 16777248 | tf_op jit(solution)/shard_map/all_to_all | solution.py:221
  396.9 0.0 copy-done
  396.9 57.4 %shard_map.47 = bf16[512,2048]{1,0:T(8,128)(2,1)S(1)} custom-call(s32[32]{0:T(128)S(1)} %max.6.slot_ref, s32[32]{0:T(128)S(1)} %reshape.12.live_ref, bf16[512,2048]{1,0:T(8,128)(2,1)S(1)} %bitcast.9, bf16[512,2048]{1,0:T(8,128)(2,1)} %bitcast.11, bf16[512,2048]{1,0:T(8,128)(2,1)} %bitcast.13, bf16[64,2,512,128]{3,2,1,0:T(8,128)(2,1)} %all-to-all-done.received_ref), custom_call_target="tpu_custom_call" | custom-call | tf_op jit(solution)/shard_map/pallas_call | solution.py:205
  454.3 1.3 copy.6
Async XLA Ops:
  12.5 12.2 %copy-start.1 = (s32[1,64,16,2]{1,3,2,0:T(2,128)S(1)}, s32[1,64,16,2]{1,3,2,0:T(2,128)}, u32[]{:S(2)}) copy-start(s32[1,64,16,2]{1,3,2,0:T(2,128)} %param.7) | copy-start | bytes 24580
  12.5 384.4 %copy-start = (bf16[1,512,2048]{2,1,0:T(8,128)(2,1)S(1)}, bf16[1,512,2048]{2,1,0:T(8,128)(2,1)}, u32[]{:S(2)}) copy-start(bf16[1,512,2048]{2,1,0:T(8,128)(2,1)} %param.4) | copy-start | bytes 6291460
  12.5 384.4 %all-to-all-start = ((bf16[64,2,512,128]{3,2,1,0:T(8,128)(2,1)}), bf16[64,2,512,128]{3,2,1,0:T(8,128)(2,1)}, u32[]{:S(2)}, u32[]{:S(2)}) async-start(bf16[64,2,512,128]{3,2,1,0:T(8,128)(2,1)} %shard_map.46), calls=%async_computation | async-start | bytes 33554432 | tf_op jit(solution)/shard_map/all_to_all | solution.py:221
